TPU v7x, 32 devices: a whole 2x2x4 slice. The times are simulated.
32 devices in a mesh: row: 2 (over x), col: 16 (over z, y, core).
Axes of the slice: x: 2, y: 2, z: 4, core: 2. Of those that a mesh axis runs over, the one named last changes fastest.
Arguments:
- queries: bfloat16 [4096, 1024], P(('row', 'col')), may hold values from -24 to 24
- query_exps: int32 [4096], P(('row', 'col')), may hold values from -1 to 3
- key_head: bfloat16 [4096, 128], P(('col', 'row')), may hold values from -5 to 5
- value_head: bfloat16 [4096, 128], P(('col', 'row')), may hold values from -6 to 6
- forward_out: bfloat16 [4096, 1024], P(('row', 'col')), may hold values from -6 to 6
- output_grad: bfloat16 [4096, 1024], P(('row', 'col')), may hold values from -6 to 6
- stripe_order: int32 [32], replicated, may hold values from 0 to 31, each once
- window_size: int32 [1], replicated, may hold values from 1024 to 2048
Outputs:
- query_grad: bfloat16 [4096, 1024], P(('row', 'col'))
- key_grad: bfloat16 [4096, 128], P(('col', 'row'))
- value_grad: bfloat16 [4096, 128], P(('col', 'row'))
Inputs may be any that keep to these rules, and one draw needn't show every extreme that they name: `stripe_order`: each stripe number appears once.
All inputs are finite; a program needn't handle non-finite values.
Results may differ from a plain program's by a relative error of at most 0.0095.
Values may be sent and summed in bfloat16 or wider, within the bound.
No kernel may reach another device: no remote copies, remote signals or barrier semaphores. Data moves between devices by JAX's collectives and lax.ppermute only.
A program may use at most 128 MiB of HBM per device.

v0:
```python
import functools
import math

import jax
import jax.numpy as jnp
from jax import lax
from jax.experimental import pallas as pl
from jax.experimental.pallas import tpu as pltpu
from jax.sharding import PartitionSpec as P

STRIPE = 128
PAIR = 2 * STRIPE
AXES = ("row", "col")
neg_big = -1e30
far_away = 1 << 29
keep_bytes = 24 << 20


class Layout:
    def __init__(self, rows, cols):
        self.rows, self.cols = rows, cols
        self.near, self.far = rows * 2, cols // 4
        self.square = self.near == self.far
        self.count = rows * cols

    def split(self, row, col):
        return row * 2 + (col // 2) % 2, col // 4, col % 2

    def join(self, near, far, core):
        return (near // 2) * self.cols + far * 4 + (near % 2) * 2 + core

    def hop(self, first=0, second=0, core_flip=0):
        pairs = []
        for device in range(self.count):
            near, far, core = self.split(device // self.cols, device % self.cols)
            if self.square and core == 1:
                near, far = near ^ second, far ^ first
            else:
                near, far = near ^ first, far ^ second
            pairs.append((device, self.join(near, far, core ^ core_flip)))
        return pairs

    def slot(self, own, stored):
        near, far, core = self.split(stored % self.rows, stored // self.rows)
        near, far = near ^ own[0], far ^ own[1]
        place = far * self.near + near
        if self.square:
            place = jnp.where(core == 1, near * self.far + far, place)
        return place + jnp.where(core == own[2], 0, self.count // 2)


def dot(left, right, left_dim, right_dim):
    return lax.dot_general(
        left, right, (((left_dim,), (right_dim,)), ((), ())), preferred_element_type=jnp.float32
    )


def prepare(layout, heads, here, order, window, q_ref, e_ref, g_ref, o_ref, q_out, g_out, d_out, meta):
    row, col = here[0], here[1]
    own = layout.split(row, col)
    own_block = order[row * layout.cols + col]
    live = jnp.minimum(own_block, (window[0] + STRIPE - 2) // STRIPE) + 1
    meta[0] = live
    meta[1] = window[0]

    def clear(back, carry):
        meta[2 + back] = layout.count * PAIR
        return carry

    def place(stored, carry):
        back = own_block - order[stored]

        @pl.when((back >= 0) & (back < live))
        def _():
            meta[2 + back] = layout.slot(own, stored) * PAIR

        return carry

    lax.fori_loop(0, layout.count + 2, clear, 0)
    lax.fori_loop(0, layout.count, place, 0)
    power = jnp.left_shift(1, e_ref[...] + 1).astype(jnp.float32) * 0.5
    power = jnp.broadcast_to(power, (STRIPE, STRIPE)).T
    for head in range(heads):
        cols = pl.ds(head * STRIPE, STRIPE)
        q_out[cols] = (q_ref[:, cols].astype(jnp.float32) * power).astype(jnp.bfloat16)
        grads = g_ref[:, cols]
        g_out[cols] = grads
        product = grads.astype(jnp.float32) * o_ref[:, cols].astype(jnp.float32)
        sums = jnp.sum(product.T, axis=0, keepdims=True)
        d_out[:, cols] = sums.astype(jnp.bfloat16).astype(jnp.float32)


def attend(
    stripes, pieces, heads, keep, inv_scale,
    meta, q_ref, g_ref, delta_ref, *refs,
):
    held, rest = refs[: 2 * pieces], refs[2 * pieces :]
    dq_ref, own_out, other_out, rest = rest[0], rest[1], rest[2 : 2 + pieces], rest[2 + pieces :]
    kv, probs, tops, weight_buf, grad_buf, run_max, run_sum = rest
    half_rows = stripes // 2 * PAIR
    piece_rows = half_rows // pieces
    to_log2 = inv_scale * math.log2(math.e)
    live, window_len = meta[0], meta[1]
    turns = (live + 1) // 2

    for i, ref in enumerate(held):
        kv[pl.ds(i * piece_rows, piece_rows)] = ref[...]
    kv[pl.ds(2 * half_rows, PAIR)] = jnp.zeros((PAIR, STRIPE), kv.dtype)
    for ref in (own_out, *other_out):
        ref[...] = jnp.zeros_like(ref)
    run_max[...] = jnp.full_like(run_max, neg_big)
    run_sum[...] = jnp.zeros_like(run_sum)
    dq_ref[...] = jnp.zeros_like(dq_ref)

    relative = lax.broadcasted_iota(jnp.int32, (STRIPE, STRIPE), 1) - lax.broadcasted_iota(
        jnp.int32, (STRIPE, STRIPE), 0
    )

    def offsets_of(turn):
        return [pl.multiple_of(meta[2 + 2 * turn + i], PAIR) for i in range(2)]

    def rows_at(offsets, shift):
        return jnp.concatenate([kv[pl.ds(offset + shift, STRIPE)] for offset in offsets], 0)

    def visible_at(turn):
        masks = []
        for i in range(2):
            block = 2 * turn + i
            distance = relative + jnp.where(block < live, block * STRIPE, far_away)
            masks.append((distance >= 0) & (distance < window_len))
        return jnp.concatenate(masks, 0)

    def head_cols(head):
        return pl.ds(head * STRIPE, STRIPE)

    def masked_scores(key_rows, visible, head):
        scores = dot(key_rows, q_ref[head_cols(head)], 1, 1) * to_log2
        return jnp.where(visible, scores, neg_big)

    def add_stats(turn, carry):
        key_rows = rows_at(offsets_of(turn), 0)
        visible = visible_at(turn)
        for head in range(heads):
            cols = head_cols(head)
            scores = masked_scores(key_rows, visible, head)
            old_max = run_max[:, cols]
            new_max = jnp.maximum(old_max, jnp.max(scores, axis=0, keepdims=True))
            part = jnp.exp2(scores - new_max)
            summed = jnp.sum(part.reshape(-1, 8, STRIPE), axis=0)
            run_sum[:, cols] = run_sum[:, cols] * jnp.exp2(old_max - new_max) + summed
            run_max[:, cols] = new_max
            if keep:
                probs[turn, :, cols] = part
                tops[turn, :, cols] = new_max
        return carry

    lax.fori_loop(0, turns, add_stats, 0)
    total = jnp.sum(run_sum[...], axis=0, keepdims=True)
    run_sum[pl.ds(0, 1)] = 1.0 / total

    def add_grads(turn, carry):
        offsets = offsets_of(turn)
        key_rows, value_rows = rows_at(offsets, 0), rows_at(offsets, STRIPE)
        if not keep:
            visible = visible_at(turn)
        for head in range(heads):
            cols = head_cols(head)
            if keep:
                factor = jnp.exp2(tops[turn, :, cols] - run_max[:, cols]) * run_sum[pl.ds(0, 1), cols]
                weights = probs[turn, :, cols] * factor
            else:
                scores = masked_scores(key_rows, visible, head)
                weights = jnp.exp2(scores - run_max[:, cols]) * run_sum[pl.ds(0, 1), cols]
            weight_grad = dot(value_rows, g_ref[cols], 1, 1)
            score_grad = weights * (weight_grad - delta_ref[:, cols])
            weight_buf[:, cols] = weights.astype(jnp.bfloat16)
            grad_buf[:, cols] = score_grad.astype(jnp.bfloat16)
        score_grads = grad_buf[...]
        dq_ref[...] += dot(key_rows, score_grads, 0, 0)
        key_part = (dot(score_grads, q_ref[...], 1, 0) * inv_scale).astype(jnp.bfloat16)
        value_part = dot(weight_buf[...], g_ref[...], 1, 0).astype(jnp.bfloat16)
        for i, offset in enumerate(offsets):
            part = slice(i * STRIPE, (i + 1) * STRIPE)
            spans = [(0, half_rows, own_out)] + [
                (half_rows + j * piece_rows, piece_rows, ref) for j, ref in enumerate(other_out)
            ]
            for start, length, ref in spans:

                @pl.when((offset >= start) & (offset < start + length))
                def _(start=start, ref=ref):
                    inner = pl.multiple_of(offset - start, PAIR)
                    ref[pl.ds(inner, STRIPE)] = key_part[part]
                    ref[pl.ds(inner + STRIPE, STRIPE)] = value_part[part]

        return carry

    lax.fori_loop(0, turns, add_grads, 0)


def turn_queries(heads, inv_scale, turned, out):
    for head in range(heads):
        cols = pl.ds(head * STRIPE, STRIPE)
        out[:, cols] = (turned[:, cols].T * inv_scale).astype(jnp.bfloat16)


vmem_spec = pl.BlockSpec(memory_space=pltpu.VMEM)
smem_spec = pl.BlockSpec(memory_space=pltpu.SMEM)


def run_prepare(layout, heads, here, order, window, queries, exps, grads, outs):
    flat = jax.ShapeDtypeStruct((heads * STRIPE, STRIPE), jnp.bfloat16)
    return pl.pallas_call(
        functools.partial(prepare, layout, heads),
        out_shape=[
            flat,
            flat,
            jax.ShapeDtypeStruct((1, heads * STRIPE), jnp.float32),
            jax.ShapeDtypeStruct((layout.count + 4,), jnp.int32),
        ],
        in_specs=[smem_spec] * 3 + [vmem_spec] * 4,
        out_specs=[vmem_spec] * 3 + [smem_spec],
        name="prep",
    )(here, order, window, queries, exps, grads, outs)


def run_attend(meta, q_flat, g_flat, delta, held, stripes, heads, inv_scale):
    pieces = len(held) // 2
    wide = q_flat.shape[0]
    turns = stripes // 2 + 1
    keep = turns * PAIR * wide * 4 <= keep_bytes
    kept = turns if keep else 1
    half_rows = stripes // 2 * PAIR
    other = jax.ShapeDtypeStruct((half_rows // pieces, STRIPE), jnp.bfloat16)
    return pl.pallas_call(
        functools.partial(attend, stripes, pieces, heads, keep, inv_scale),
        out_shape=[
            jax.ShapeDtypeStruct((STRIPE, wide), jnp.float32),
            jax.ShapeDtypeStruct((half_rows, STRIPE), jnp.bfloat16),
        ]
        + [other] * pieces,
        in_specs=[smem_spec] + [vmem_spec] * (3 + len(held)),
        out_specs=[vmem_spec] * (2 + pieces),
        scratch_shapes=[
            pltpu.VMEM((2 * half_rows + PAIR, STRIPE), jnp.bfloat16),
            pltpu.VMEM((kept, PAIR, wide), jnp.float32),
            pltpu.VMEM((kept, 1, wide), jnp.float32),
            pltpu.VMEM((PAIR, wide), jnp.bfloat16),
            pltpu.VMEM((PAIR, wide), jnp.bfloat16),
            pltpu.VMEM((1, wide), jnp.float32),
            pltpu.VMEM((8, wide), jnp.float32),
        ],
        name="attend",
    )(meta, q_flat, g_flat, delta, *held)


def run_turn(turned, heads, inv_scale):
    return pl.pallas_call(
        functools.partial(turn_queries, heads, inv_scale),
        out_shape=jax.ShapeDtypeStruct(turned.shape, jnp.bfloat16),
        in_specs=[vmem_spec],
        out_specs=vmem_spec,
        name="turn",
    )(turned)


def per_device(
    layout,
    queries, query_exps, key_head, value_head, forward_out, output_grad, stripe_order, window_size
):
    head_dim = key_head.shape[1]
    tokens, feat_width = queries.shape
    heads = feat_width // head_dim
    inv_scale = 1.0 / math.sqrt(head_dim)
    stripes = layout.count
    row, col = lax.axis_index("row"), lax.axis_index("col")

    def send(value, **where):
        return lax.ppermute(value, AXES, layout.hop(**where))

    def widen(value):
        return value.astype(jnp.float32)

    pair = jnp.concatenate([key_head, value_head], 0)
    stage = [pair] + [send(pair, first=i) for i in range(1, layout.near)]
    plane = jnp.concatenate(stage, 0)
    own_pieces = [plane] + [send(plane, second=j) for j in range(1, layout.far)]
    other_pieces = [send(piece, core_flip=1) for piece in own_pieces]

    here = jnp.stack([row, col]).astype(jnp.int32)
    q_flat, g_flat, delta, meta = run_prepare(
        layout, heads, here, stripe_order, window_size,
        queries, query_exps.reshape(1, -1), output_grad, forward_out,
    )
    results = run_attend(
        meta, q_flat, g_flat, delta, own_pieces + other_pieces, stripes, heads, inv_scale
    )
    turned, own_part, other_parts = results[0], results[1], results[2:]
    query_grad = run_turn(turned, heads, inv_scale)

    piece_rows = plane.shape[0]
    summed = [
        widen(own_part[j * piece_rows : (j + 1) * piece_rows])
        + widen(send(other_parts[j], core_flip=1))
        for j in range(layout.far)
    ]
    plane_sum = summed[0]
    for j in range(1, layout.far):
        plane_sum = plane_sum + widen(send(summed[j].astype(jnp.bfloat16), second=j))
    pair_sum = plane_sum[:PAIR]
    for i in range(1, layout.near):
        part = plane_sum[i * PAIR : (i + 1) * PAIR].astype(jnp.bfloat16)
        pair_sum = pair_sum + widen(send(part, first=i))
    pair_sum = pair_sum.astype(jnp.bfloat16)
    return (query_grad, pair_sum[:tokens], pair_sum[tokens:])


def solution(mesh):
    layout = Layout(mesh.shape["row"], mesh.shape["col"])

    def whole(*arrays):
        return per_device(layout, *arrays)

    return jax.shard_map(
        whole,
        mesh=mesh,
        in_specs=(
            P(("row", "col"), None),
            P(("row", "col")),
            P(("col", "row"), None),
            P(("col", "row"), None),
            P(("row", "col"), None),
            P(("row", "col"), None),
            P(),
            P(),
        ),
        out_specs=(P(("row", "col"), None), P(("col", "row"), None), P(("col", "row"), None)),
        check_vma=False,
    )
```

profile of v0, /device:TPU:0, one launch (start us, length us, event | category | flops | bytes accessed | tf_op | source)
XLA Modules:
  0.0 78.1 jit_solution(5001204135663186310)
XLA Ops:
  0.6 0.8 constant_dynamic-update-slice_fusion.1
  1.4 3.1 %collective-permute-start = (bf16[256,128]{1,0:T(8,128)(2,1)S(1)}, bf16[256,128]{1,0:T(8,128)(2,1)S(1)}, u32[]{:S(2)}, u32[]{:S(2)}) collective-permute-start(bf16[256,128]{1,0:T(8,128)(2,1)S(1)} %get-tuple-element.33), channel_id=1, source_target_pairs={{0,2},{1,5},{2,0},{3,7},{4,6},{5,1},{6,4},{7,3},{8,10},{9,13},{10,... | collective-permute-start | bytes 196616 | tf_op jit(solution)/shard_map/ppermute | solution.py:278
  4.5 1.4 %collective-permute-start.2 = (bf16[256,128]{1,0:T(8,128)(2,1)S(1)}, bf16[256,128]{1,0:T(8,128)(2,1)S(1)}, u32[]{:S(2)}, u32[]{:S(2)}) collective-permute-start(bf16[256,128]{1,0:T(8,128)(2,1)S(1)} %get-tuple-element.33), channel_id=1, source_target_pairs={{0,18},{1,13},{2,16},{3,15},{4,22},{5,9},{6,20},{7,11},{8,26},{9,5... | collective-permute-start | bytes 196616 | tf_op jit(solution)/shard_map/ppermute | solution.py:278
  6.0 0.7 collective-permute-done
  6.8 3.4 %collective-permute-done.1 = bf16[256,128]{1,0:T(8,128)(2,1)S(1)} collective-permute-done((bf16[256,128]{1,0:T(8,128)(2,1)S(1)}, bf16[256,128]{1,0:T(8,128)(2,1)S(1)}, u32[]{:S(2)}, u32[]{:S(2)}) %collective-permute-start.1) | collective-permute-done | bytes 65568 | tf_op jit(solution)/shard_map/ppermute | solution.py:278
  10.3 3.7 %collective-permute-start.5 = (bf16[1024,128]{1,0:T(8,128)(2,1)S(1)}, bf16[1024,128]{1,0:T(8,128)(2,1)S(1)}, u32[]{:S(2)}, u32[]{:S(2)}) collective-permute-start(bf16[1024,128]{1,0:T(8,128)(2,1)S(1)} %constant_dynamic-update-slice_fusion.2.refs_0_), channel_id=1, source_target_pairs={{0,12},{1,19},{2,14},{3,17},{4,8},{5,23},{6,10},{7,21},{8,4},{9,27... | collective-permute-start | bytes 786440 | tf_op jit(solution)/shard_map/ppermute | solution.py:278
  13.9 0.8 %collective-permute-start.3 = (bf16[1024,128]{1,0:T(8,128)(2,1)S(1)}, bf16[1024,128]{1,0:T(8,128)(2,1)S(1)}, u32[]{:S(2)}, u32[]{:S(2)}) collective-permute-start(bf16[1024,128]{1,0:T(8,128)(2,1)S(1)} %constant_dynamic-update-slice_fusion.2.refs_0_), channel_id=1, source_target_pairs={{0,4},{1,3},{2,6},{3,1},{4,0},{5,7},{6,2},{7,5},{8,12},{9,11},{10,... | collective-permute-start | bytes 786440 | tf_op jit(solution)/shard_map/ppermute | solution.py:278
  14.7 4.0 %collective-permute-done.5.refs_3_ = bf16[1024,128]{1,0:T(8,128)(2,1)S(1)} collective-permute-done((bf16[1024,128]{1,0:T(8,128)(2,1)S(1)}, bf16[1024,128]{1,0:T(8,128)(2,1)S(1)}, u32[]{:S(2)}, u32[]{:S(2)}) %collective-permute-start.5) | collective-permute-done | bytes 262176 | tf_op jit(solution)/shard_map/ppermute | solution.py:278
  18.7 7.4 %collective-permute-done.4.refs_2_ = bf16[1024,128]{1,0:T(8,128)(2,1)S(1)} collective-permute-done((bf16[1024,128]{1,0:T(8,128)(2,1)S(1)}, bf16[1024,128]{1,0:T(8,128)(2,1)S(1)}, u32[]{:S(2)}, u32[]{:S(2)}) %collective-permute-start.4) | collective-permute-done | bytes 262176 | tf_op jit(solution)/shard_map/ppermute | solution.py:278
  28.0 3.1 %prep.1 = (bf16[1024,128]{1,0:T(8,128)(2,1)}, bf16[1024,128]{1,0:T(8,128)(2,1)}, f32[1,1024]{1,0:T(1,128)}, s32[36]{0:T(128)}) custom-call(s32[2]{0:T(128)} %pad_add_fusion.here, s32[32]{0:T(128)} %order.1, s32[1]{0:T(128)S(6)} %copy.16.window, bf16[128,1024]{1,0:T(8,128)(2,1)} %q_ref.1, s32[1,128]{1,0:T(1,128)} %bitcast.3, bf16[128,1024]{1,0:T(8,128)(2,1)} %g_ref.1, ...), custom_call_target="tpu_custom_call" | custom-call | tf_op jit(solution)/shard_map/prep/pallas_call | solution.py:212
  32.1 14.7 %attend.1 = (f32[128,1024]{1,0:T(8,128)}, bf16[4096,128]{1,0:T(8,128)(2,1)}, bf16[1024,128]{1,0:T(8,128)(2,1)}, bf16[1024,128]{1,0:T(8,128)(2,1)}, bf16[1024,128]{1,0:T(8,128)(2,1)}, /*index=5*/bf16[1024,128]{1,0:T(8,128)(2,1)}) custom-call(s32[36]{0:T(128)} %get-tuple-element.13.meta, bf16[1024,128]{1,0:T(8,128)(2,1)} %get-tuple-element.14.q_ref, ...), custom_call_target="tpu_custom_call" | custom-call | tf_op jit(solution)/shard_map/attend/pallas_call | solution.py:234
  47.9 0.7 collective-permute-done.11
  49.3 1.3 %add_convert_fusion.2 = (bf16[1024,128]{1,0:T(8,128)(2,1)S(1)}, bf16[1024,128]{1,0:T(8,128)(2,1)S(1)}, bf16[1024,128]{1,0:T(8,128)(2,1)S(1)}) fusion(bf16[1024,128]{1,0:T(8,128)(2,1)S(1)} %collective-permute-done.11, bf16[4096,128]{1,0:T(8,128)(2,1)} %get-tuple-element.18, bf16[1024,128]{1,0:T(8,128)(2,1)S(1)} %collective-permute-done.15, ...), kind=kLoop, calls=%fused_computation.3 | loop fusion | flops 1572864 | bytes 2359296 | tf_op jit(solution)/shard_map/convert_element_type | solution.py:308
  50.7 2.3 %collective-permute-start.16 = (bf16[1024,128]{1,0:T(8,128)(2,1)S(1)}, bf16[1024,128]{1,0:T(8,128)(2,1)S(1)}, u32[]{:S(2)}, u32[]{:S(2)}) collective-permute-start(bf16[1024,128]{1,0:T(8,128)(2,1)S(1)} %get-tuple-element.26), channel_id=1, source_target_pairs={{0,12},{1,19},{2,14},{3,17},{4,8},{5,23},{6,10},{7,21},{8,4},{9,27... | collective-permute-start | bytes 786440 | tf_op jit(solution)/shard_map/ppermute | solution.py:278
  53.0 1.2 %collective-permute-start.14 = (bf16[1024,128]{1,0:T(8,128)(2,1)S(1)}, bf16[1024,128]{1,0:T(8,128)(2,1)S(1)}, u32[]{:S(2)}, u32[]{:S(2)}) collective-permute-start(bf16[1024,128]{1,0:T(8,128)(2,1)S(1)} %get-tuple-element.27), channel_id=1, source_target_pairs={{0,8},{1,17},{2,10},{3,19},{4,12},{5,21},{6,14},{7,23},{8,0},{9,25... | collective-permute-start | bytes 786440 | tf_op jit(solution)/shard_map/ppermute | solution.py:278
  54.2 2.9 %collective-permute-done.12 = bf16[1024,128]{1,0:T(8,128)(2,1)S(1)} collective-permute-done((bf16[1024,128]{1,0:T(8,128)(2,1)S(1)}, bf16[1024,128]{1,0:T(8,128)(2,1)S(1)}, u32[]{:S(2)}, u32[]{:S(2)}) %collective-permute-start.12) | collective-permute-done | bytes 262176 | tf_op jit(solution)/shard_map/ppermute | solution.py:278
  57.1 3.1 %collective-permute-done.16 = bf16[1024,128]{1,0:T(8,128)(2,1)S(1)} collective-permute-done((bf16[1024,128]{1,0:T(8,128)(2,1)S(1)}, bf16[1024,128]{1,0:T(8,128)(2,1)S(1)}, u32[]{:S(2)}, u32[]{:S(2)}) %collective-permute-start.16) | collective-permute-done | bytes 262176 | tf_op jit(solution)/shard_map/ppermute | solution.py:278
  60.2 9.7 %collective-permute-done.14 = bf16[1024,128]{1,0:T(8,128)(2,1)S(1)} collective-permute-done((bf16[1024,128]{1,0:T(8,128)(2,1)S(1)}, bf16[1024,128]{1,0:T(8,128)(2,1)S(1)}, u32[]{:S(2)}, u32[]{:S(2)}) %collective-permute-start.14) | collective-permute-done | bytes 262176 | tf_op jit(solution)/shard_map/ppermute | solution.py:278
  69.8 1.1 %fusion.3 = (bf16[1024,128]{1,0:T(8,128)(2,1)S(1)}, f32[1024,128]{1,0:T(8,128)S(1)}) fusion(bf16[1024,128]{1,0:T(8,128)(2,1)S(1)} %collective-permute-done.16, bf16[1024,128]{1,0:T(8,128)(2,1)S(1)} %collective-permute-done.14, bf16[1024,128]{1,0:T(8,128)(2,1)S(1)} %collective-permute-done.12, bf16[1024,128]{1,0:T(8,128)(2,1)S(1)} %collective-permute-done.10, ...), kind=kLoop, calls=%fused_computation.16 | loop fusion | flops 1310720 | bytes 2097152 | tf_op jit(solution)/shard_map/convert.2
  71.0 1.3 %collective-permute-start.17 = (bf16[256,128]{1,0:T(8,128)(2,1)S(1)}, bf16[256,128]{1,0:T(8,128)(2,1)S(1)}, u32[]{:S(2)}, u32[]{:S(2)}) collective-permute-start(bf16[256,128]{1,0:T(8,128)(2,1)S(1)} %get-tuple-element.28), channel_id=1, source_target_pairs={{0,2},{1,5},{2,0},{3,7},{4,6},{5,1},{6,4},{7,3},{8,10},{9,13},{10,... | collective-permute-start | bytes 196616 | tf_op jit(solution)/shard_map/ppermute | solution.py:278
  72.2 0.9 %collective-permute-start.19 = (bf16[256,128]{1,0:T(8,128)(2,1)S(1)}, bf16[256,128]{1,0:T(8,128)(2,1)S(1)}, u32[]{:S(2)}, u32[]{:S(2)}) collective-permute-start(bf16[256,128]{1,0:T(8,128)(2,1)S(1)} %get-tuple-element.29), channel_id=1, source_target_pairs={{0,18},{1,13},{2,16},{3,15},{4,22},{5,9},{6,20},{7,11},{8,26},{9,5... | collective-permute-start | bytes 196616 | tf_op jit(solution)/shard_map/ppermute | solution.py:278
  73.1 1.4 %collective-permute-start.18 = (bf16[256,128]{1,0:T(8,128)(2,1)S(1)}, bf16[256,128]{1,0:T(8,128)(2,1)S(1)}, u32[]{:S(2)}, u32[]{:S(2)}) collective-permute-start(bf16[256,128]{1,0:T(8,128)(2,1)S(1)} %get-tuple-element.30), channel_id=1, source_target_pairs={{0,16},{1,9},{2,18},{3,11},{4,20},{5,13},{6,22},{7,15},{8,24},{9,1... | collective-permute-start | bytes 196616 | tf_op jit(solution)/shard_map/ppermute | solution.py:278
  74.5 1.9 %turn.1 = bf16[128,1024]{1,0:T(8,128)(2,1)} custom-call(f32[128,1024]{1,0:T(8,128)} %get-tuple-element.17.turned), custom_call_target="tpu_custom_call" | custom-call | tf_op jit(solution)/shard_map/turn/pallas_call | solution.py:257
  76.5 0.9 %collective-permute-done.19 = bf16[256,128]{1,0:T(8,128)(2,1)S(1)} collective-permute-done((bf16[256,128]{1,0:T(8,128)(2,1)S(1)}, bf16[256,128]{1,0:T(8,128)(2,1)S(1)}, u32[]{:S(2)}, u32[]{:S(2)}) %collective-permute-start.19) | collective-permute-done | bytes 65568 | tf_op jit(solution)/shard_map/ppermute | solution.py:278
  (48 shorter events, 4.9 us)
Async XLA Ops:
  1.4 5.3 %collective-permute-start = (bf16[256,128]{1,0:T(8,128)(2,1)S(1)}, bf16[256,128]{1,0:T(8,128)(2,1)S(1)}, u32[]{:S(2)}, u32[]{:S(2)}) collective-permute-start(bf16[256,128]{1,0:T(8,128)(2,1)S(1)} %get-tuple-element.33), channel_id=1, source_target_pairs={{0,2},{1,5},{2,0},{3,7},{4,6},{5,1},{6,4},{7,3},{8,10},{9,13},{10,... | collective-permute-start | bytes 196616 | tf_op jit(solution)/shard_map/ppermute | solution.py:278
  4.5 5.7 %collective-permute-start.2 = (bf16[256,128]{1,0:T(8,128)(2,1)S(1)}, bf16[256,128]{1,0:T(8,128)(2,1)S(1)}, u32[]{:S(2)}, u32[]{:S(2)}) collective-permute-start(bf16[256,128]{1,0:T(8,128)(2,1)S(1)} %get-tuple-element.33), channel_id=1, source_target_pairs={{0,18},{1,13},{2,16},{3,15},{4,22},{5,9},{6,20},{7,11},{8,26},{9,5... | collective-permute-start | bytes 196616 | tf_op jit(solution)/shard_map/ppermute | solution.py:278
  5.9 4.3 %collective-permute-start.1 = (bf16[256,128]{1,0:T(8,128)(2,1)S(1)}, bf16[256,128]{1,0:T(8,128)(2,1)S(1)}, u32[]{:S(2)}, u32[]{:S(2)}) collective-permute-start(bf16[256,128]{1,0:T(8,128)(2,1)S(1)} %get-tuple-element.33), channel_id=1, source_target_pairs={{0,16},{1,9},{2,18},{3,11},{4,20},{5,13},{6,22},{7,15},{8,24},{9,1... | collective-permute-start | bytes 196616 | tf_op jit(solution)/shard_map/ppermute | solution.py:278
  10.3 20.8 %copy-start = (bf16[1024,128]{1,0:T(8,128)(2,1)}, bf16[1024,128]{1,0:T(8,128)(2,1)S(1)}, u32[]{:S(2)}) copy-start(bf16[1024,128]{1,0:T(8,128)(2,1)S(1)} %constant_dynamic-update-slice_fusion.2.refs_0_) | copy-start | bytes 786436
  10.3 8.4 %collective-permute-start.5 = (bf16[1024,128]{1,0:T(8,128)(2,1)S(1)}, bf16[1024,128]{1,0:T(8,128)(2,1)S(1)}, u32[]{:S(2)}, u32[]{:S(2)}) collective-permute-start(bf16[1024,128]{1,0:T(8,128)(2,1)S(1)} %constant_dynamic-update-slice_fusion.2.refs_0_), channel_id=1, source_target_pairs={{0,12},{1,19},{2,14},{3,17},{4,8},{5,23},{6,10},{7,21},{8,4},{9,27... | collective-permute-start | bytes 786440 | tf_op jit(solution)/shard_map/ppermute | solution.py:278
  13.9 12.2 %collective-permute-start.4 = (bf16[1024,128]{1,0:T(8,128)(2,1)S(1)}, bf16[1024,128]{1,0:T(8,128)(2,1)S(1)}, u32[]{:S(2)}, u32[]{:S(2)}) collective-permute-start(bf16[1024,128]{1,0:T(8,128)(2,1)S(1)} %constant_dynamic-update-slice_fusion.2.refs_0_), channel_id=1, source_target_pairs={{0,8},{1,17},{2,10},{3,19},{4,12},{5,21},{6,14},{7,23},{8,0},{9,25... | collective-permute-start | bytes 786440 | tf_op jit(solution)/shard_map/ppermute | solution.py:278
  13.9 12.2 %collective-permute-start.3 = (bf16[1024,128]{1,0:T(8,128)(2,1)S(1)}, bf16[1024,128]{1,0:T(8,128)(2,1)S(1)}, u32[]{:S(2)}, u32[]{:S(2)}) collective-permute-start(bf16[1024,128]{1,0:T(8,128)(2,1)S(1)} %constant_dynamic-update-slice_fusion.2.refs_0_), channel_id=1, source_target_pairs={{0,4},{1,3},{2,6},{3,1},{4,0},{5,7},{6,2},{7,5},{8,12},{9,11},{10,... | collective-permute-start | bytes 786440 | tf_op jit(solution)/shard_map/ppermute | solution.py:278
  14.7 16.4 %collective-permute-start.6 = (bf16[1024,128]{1,0:T(8,128)(2,1)S(1)}, bf16[1024,128]{1,0:T(8,128)(2,1)S(1)}, u32[]{:S(2)}, u32[]{:S(2)}) collective-permute-start(bf16[1024,128]{1,0:T(8,128)(2,1)S(1)} %constant_dynamic-update-slice_fusion.2.refs_0_), channel_id=1, source_target_pairs={{0,1},{1,0},{2,3},{3,2},{4,5},{5,4},{6,7},{7,6},{8,9},{9,8},{10,11... | collective-permute-start | bytes 786440 | tf_op jit(solution)/shard_map/ppermute | solution.py:278
  18.7 12.4 %copy-start.1 = (bf16[1024,128]{1,0:T(8,128)(2,1)}, bf16[1024,128]{1,0:T(8,128)(2,1)S(1)}, u32[]{:S(2)}) copy-start(bf16[1024,128]{1,0:T(8,128)(2,1)S(1)} %collective-permute-done.5.refs_3_) | copy-start | bytes 786436
  18.7 12.4 %collective-permute-start.9 = (bf16[1024,128]{1,0:T(8,128)(2,1)S(1)}, bf16[1024,128]{1,0:T(8,128)(2,1)S(1)}, u32[]{:S(2)}, u32[]{:S(2)}) collective-permute-start(bf16[1024,128]{1,0:T(8,128)(2,1)S(1)} %collective-permute-done.5.refs_3_), channel_id=1, source_target_pairs={{0,1},{1,0},{2,3},{3,2},{4,5},{5,4},{6,7},{7,6},{8,9},{9,8},{10,11... | collective-permute-start | bytes 786440 | tf_op jit(solution)/shard_map/ppermute | solution.py:278
  26.1 5.0 %copy-start.2 = (bf16[1024,128]{1,0:T(8,128)(2,1)}, bf16[1024,128]{1,0:T(8,128)(2,1)S(1)}, u32[]{:S(2)}) copy-start(bf16[1024,128]{1,0:T(8,128)(2,1)S(1)} %collective-permute-done.4.refs_2_) | copy-start | bytes 786436
  26.1 5.0 %collective-permute-start.8 = (bf16[1024,128]{1,0:T(8,128)(2,1)S(1)}, bf16[1024,128]{1,0:T(8,128)(2,1)S(1)}, u32[]{:S(2)}, u32[]{:S(2)}) collective-permute-start(bf16[1024,128]{1,0:T(8,128)(2,1)S(1)} %collective-permute-done.4.refs_2_), channel_id=1, source_target_pairs={{0,1},{1,0},{2,3},{3,2},{4,5},{5,4},{6,7},{7,6},{8,9},{9,8},{10,11... | collective-permute-start | bytes 786440 | tf_op jit(solution)/shard_map/ppermute | solution.py:278
  26.1 5.0 %copy-start.3 = (bf16[1024,128]{1,0:T(8,128)(2,1)}, bf16[1024,128]{1,0:T(8,128)(2,1)S(1)}, u32[]{:S(2)}) copy-start(bf16[1024,128]{1,0:T(8,128)(2,1)S(1)} %collective-permute-done.3.refs_1_) | copy-start | bytes 786436
  26.2 5.0 %collective-permute-start.7 = (bf16[1024,128]{1,0:T(8,128)(2,1)S(1)}, bf16[1024,128]{1,0:T(8,128)(2,1)S(1)}, u32[]{:S(2)}, u32[]{:S(2)}) collective-permute-start(bf16[1024,128]{1,0:T(8,128)(2,1)S(1)} %collective-permute-done.3.refs_1_), channel_id=1, source_target_pairs={{0,1},{1,0},{2,3},{3,2},{4,5},{5,4},{6,7},{7,6},{8,9},{9,8},{10,11... | collective-permute-start | bytes 786440 | tf_op jit(solution)/shard_map/ppermute | solution.py:278
  46.8 1.7 %collective-permute-start.11 = (bf16[1024,128]{1,0:T(8,128)(2,1)}, bf16[1024,128]{1,0:T(8,128)(2,1)S(1)}, u32[]{:S(2)}, u32[]{:S(2)}) collective-permute-start(bf16[1024,128]{1,0:T(8,128)(2,1)} %get-tuple-element.20), channel_id=1, source_target_pairs={{0,1},{1,0},{2,3},{3,2},{4,5},{5,4},{6,7},{7,6},{8,9},{9,8},{10,11... | collective-permute-start | bytes 786440 | tf_op jit(solution)/shard_map/ppermute | solution.py:278
  46.9 2.0 %collective-permute-start.13 = (bf16[1024,128]{1,0:T(8,128)(2,1)}, bf16[1024,128]{1,0:T(8,128)(2,1)S(1)}, u32[]{:S(2)}, u32[]{:S(2)}) collective-permute-start(bf16[1024,128]{1,0:T(8,128)(2,1)} %get-tuple-element.21), channel_id=1, source_target_pairs={{0,1},{1,0},{2,3},{3,2},{4,5},{5,4},{6,7},{7,6},{8,9},{9,8},{10,11... | collective-permute-start | bytes 786440 | tf_op jit(solution)/shard_map/ppermute | solution.py:278
  47.3 2.0 %collective-permute-start.15 = (bf16[1024,128]{1,0:T(8,128)(2,1)}, bf16[1024,128]{1,0:T(8,128)(2,1)S(1)}, u32[]{:S(2)}, u32[]{:S(2)}) collective-permute-start(bf16[1024,128]{1,0:T(8,128)(2,1)} %get-tuple-element.22), channel_id=1, source_target_pairs={{0,1},{1,0},{2,3},{3,2},{4,5},{5,4},{6,7},{7,6},{8,9},{9,8},{10,11... | collective-permute-start | bytes 786440 | tf_op jit(solution)/shard_map/ppermute | solution.py:278
  47.4 6.8 %collective-permute-start.10 = (bf16[1024,128]{1,0:T(8,128)(2,1)}, bf16[1024,128]{1,0:T(8,128)(2,1)S(1)}, u32[]{:S(2)}, u32[]{:S(2)}) collective-permute-start(bf16[1024,128]{1,0:T(8,128)(2,1)} %get-tuple-element.19), channel_id=1, source_target_pairs={{0,1},{1,0},{2,3},{3,2},{4,5},{5,4},{6,7},{7,6},{8,9},{9,8},{10,11... | collective-permute-start | bytes 786440 | tf_op jit(solution)/shard_map/ppermute | solution.py:278
  50.6 6.4 %collective-permute-start.12 = (bf16[1024,128]{1,0:T(8,128)(2,1)S(1)}, bf16[1024,128]{1,0:T(8,128)(2,1)S(1)}, u32[]{:S(2)}, u32[]{:S(2)}) collective-permute-start(bf16[1024,128]{1,0:T(8,128)(2,1)S(1)} %get-tuple-element.25), channel_id=1, source_target_pairs={{0,4},{1,3},{2,6},{3,1},{4,0},{5,7},{6,2},{7,5},{8,12},{9,11},{10,... | collective-permute-start | bytes 786440 | tf_op jit(solution)/shard_map/ppermute | solution.py:278
  50.7 9.4 %collective-permute-start.16 = (bf16[1024,128]{1,0:T(8,128)(2,1)S(1)}, bf16[1024,128]{1,0:T(8,128)(2,1)S(1)}, u32[]{:S(2)}, u32[]{:S(2)}) collective-permute-start(bf16[1024,128]{1,0:T(8,128)(2,1)S(1)} %get-tuple-element.26), channel_id=1, source_target_pairs={{0,12},{1,19},{2,14},{3,17},{4,8},{5,23},{6,10},{7,21},{8,4},{9,27... | collective-permute-start | bytes 786440 | tf_op jit(solution)/shard_map/ppermute | solution.py:278
  53.0 16.8 %collective-permute-start.14 = (bf16[1024,128]{1,0:T(8,128)(2,1)S(1)}, bf16[1024,128]{1,0:T(8,128)(2,1)S(1)}, u32[]{:S(2)}, u32[]{:S(2)}) collective-permute-start(bf16[1024,128]{1,0:T(8,128)(2,1)S(1)} %get-tuple-element.27), channel_id=1, source_target_pairs={{0,8},{1,17},{2,10},{3,19},{4,12},{5,21},{6,14},{7,23},{8,0},{9,25... | collective-permute-start | bytes 786440 | tf_op jit(solution)/shard_map/ppermute | solution.py:278
  71.0 5.5 %collective-permute-start.17 = (bf16[256,128]{1,0:T(8,128)(2,1)S(1)}, bf16[256,128]{1,0:T(8,128)(2,1)S(1)}, u32[]{:S(2)}, u32[]{:S(2)}) collective-permute-start(bf16[256,128]{1,0:T(8,128)(2,1)S(1)} %get-tuple-element.28), channel_id=1, source_target_pairs={{0,2},{1,5},{2,0},{3,7},{4,6},{5,1},{6,4},{7,3},{8,10},{9,13},{10,... | collective-permute-start | bytes 196616 | tf_op jit(solution)/shard_map/ppermute | solution.py:278
  72.2 5.2 %collective-permute-start.19 = (bf16[256,128]{1,0:T(8,128)(2,1)S(1)}, bf16[256,128]{1,0:T(8,128)(2,1)S(1)}, u32[]{:S(2)}, u32[]{:S(2)}) collective-permute-start(bf16[256,128]{1,0:T(8,128)(2,1)S(1)} %get-tuple-element.29), channel_id=1, source_target_pairs={{0,18},{1,13},{2,16},{3,15},{4,22},{5,9},{6,20},{7,11},{8,26},{9,5... | collective-permute-start | bytes 196616 | tf_op jit(solution)/shard_map/ppermute | solution.py:278
  73.1 4.4 %collective-permute-start.18 = (bf16[256,128]{1,0:T(8,128)(2,1)S(1)}, bf16[256,128]{1,0:T(8,128)(2,1)S(1)}, u32[]{:S(2)}, u32[]{:S(2)}) collective-permute-start(bf16[256,128]{1,0:T(8,128)(2,1)S(1)} %get-tuple-element.30), channel_id=1, source_target_pairs={{0,16},{1,9},{2,18},{3,11},{4,20},{5,13},{6,22},{7,15},{8,24},{9,1... | collective-permute-start | bytes 196616 | tf_op jit(solution)/shard_map/ppermute | solution.py:278
  (5 other events, 4.1 us)
where the time goes:
time: 78.5 us; the launch traced here: 78.1 us
  waiting for transfers between devices  33.7 us (43%)
  Pallas kernels  19.8 us (25%)
  starting transfers between devices  17.7 us (23%)
  other arithmetic  3.12 us (4%)
  local copies, waits for them, and re-layouts  2.41 us (3%)
  between operations  1.49 us (2%)
    ppermute x20, waiting for transfers between devices, send(): return lax.ppermute(value, AXES, layout.hop(**where))  33.7 us
    ppermute x20, starting transfers between devices, send(): return lax.ppermute(value, AXES, layout.hop(**where))  17.7 us
    pallas_call x1, Pallas kernels, run_attend(): pl.pallas_call(functools.partial(attend, stripes, pieces, heads, keep, in...  14.7 us
    pallas_call x1, Pallas kernels, run_prepare(): pl.pallas_call(functools.partial(prepare, layout, heads), out_shape=[flat...  3.1 us
    pallas_call x1, Pallas kernels, run_turn(): pl.pallas_call(functools.partial(turn_queries, heads, inv_scale), out_sha...  1.95 us
    unnamed x21, local copies, waits for them, and re-layouts  1.74 us
  transfers between devices with their start and end apart: 20, of which 12 were waited for; matrix products, arithmetic and copies ran while one was open for 3% of the time, Pallas kernels for 6%

commit v1 on v0

--- a/solution.py
+++ b/solution.py
@@ -24,10 +24,14 @@
         self.count = rows * cols
 
     def split(self, row, col):
-        return row * 2 + (col // 2) % 2, col // 4, col % 2
+        ring = col // 4
+        half = ring // 2
+        return row * 2 + (ring + half) % 2, half * 2 + (col // 2) % 2, col % 2
 
     def join(self, near, far, core):
-        return (near // 2) * self.cols + far * 4 + (near % 2) * 2 + core
+        half = far // 2
+        ring = half * 2 + (near + half) % 2
+        return (near // 2) * self.cols + ring * 4 + (far % 2) * 2 + core
 
     def hop(self, first=0, second=0, core_flip=0):
         pairs = []
@@ -203,6 +207,10 @@
         out[:, cols] = (turned[:, cols].T * inv_scale).astype(jnp.bfloat16)
 
 
+def vmem_limit(nbytes):
+    return pltpu.CompilerParams(vmem_limit_bytes=nbytes)
+
+
 vmem_spec = pl.BlockSpec(memory_space=pltpu.VMEM)
 smem_spec = pl.BlockSpec(memory_space=pltpu.SMEM)
 
@@ -219,6 +227,7 @@
         ],
         in_specs=[smem_spec] * 3 + [vmem_spec] * 4,
         out_specs=[vmem_spec] * 3 + [smem_spec],
+        compiler_params=vmem_limit(24 * STRIPE * heads * STRIPE * 2),
         name="prep",
     )(here, order, window, queries, exps, grads, outs)
 
@@ -231,6 +240,7 @@
     kept = turns if keep else 1
     half_rows = stripes // 2 * PAIR
     other = jax.ShapeDtypeStruct((half_rows // pieces, STRIPE), jnp.bfloat16)
+    limit = kept * PAIR * wide * 4 + 3 * 2 * half_rows * STRIPE * 2 + 10 * PAIR * wide * 2
     return pl.pallas_call(
         functools.partial(attend, stripes, pieces, heads, keep, inv_scale),
         out_shape=[
@@ -249,6 +259,7 @@
             pltpu.VMEM((1, wide), jnp.float32),
             pltpu.VMEM((8, wide), jnp.float32),
         ],
+        compiler_params=vmem_limit(limit),
         name="attend",
     )(meta, q_flat, g_flat, delta, *held)
 
@@ -259,6 +270,7 @@
         out_shape=jax.ShapeDtypeStruct(turned.shape, jnp.bfloat16),
         in_specs=[vmem_spec],
         out_specs=vmem_spec,
+        compiler_params=vmem_limit(24 * STRIPE * heads * STRIPE * 2),
         name="turn",
     )(turned)
 

time: 78.5 us -> 70.5 us (0.90)
  waiting for transfers between devices: 33.7 us -> 28.6 us
  Pallas kernels: 19.8 us -> 15.5 us
  starting transfers between devices: 17.7 us -> 21.1 us
  other arithmetic: 3.12 us -> 0.49 us
    ppermute x20, waiting for transfers between devices: 33.7 us -> 28.6 us  [send(): return lax.ppermute(value, AXES, layout.hop(**where))]
    ppermute x20, starting transfers between devices: 17.7 us -> 21.1 us  [send(): return lax.ppermute(value, AXES, layout.hop(**where))]
    pallas_call x1, Pallas kernels: 14.7 us -> 12.1 us  [run_attend(): pl.pallas_call(functools.partial(attend, stripes, pieces, heads, keep, in...]
    convert_element_type x1, other arithmetic: 1.31 us -> 0.21 us  [per_device(): summed[j].astype(jnp.bfloat16)]
    pallas_call x1, Pallas kernels: 1.95 us -> 0.91 us  [run_turn(): pl.pallas_call(functools.partial(turn_queries, heads, inv_scale), out_sha...]
    another operation x1, other arithmetic: 1.12 us -> 0.17 us
    unnamed x21 -> x15, local copies, waits for them, and re-layouts: 1.74 us -> 2.46 us
  transfers between devices with their start and end apart: 20 -> 20, of which waited for: 12 -> 12; matrix products, arithmetic and copies ran while one was open for 3% -> 0% of each run, Pallas kernels for 6% -> 5%
where the time goes in v1:
time: 70.5 us; the launch traced here: 70.3 us
  waiting for transfers between devices  28.6 us (41%)
  starting transfers between devices  21.1 us (30%)
  Pallas kernels  15.5 us (22%)
  local copies, waits for them, and re-layouts  3.14 us (4%)
  between operations  1.43 us (2%)
    ppermute x20, waiting for transfers between devices, send(): return lax.ppermute(value, AXES, layout.hop(**where))  28.6 us
    ppermute x20, starting transfers between devices, send(): return lax.ppermute(value, AXES, layout.hop(**where))  21.1 us
    pallas_call x1, Pallas kernels, run_attend(): pl.pallas_call(functools.partial(attend, stripes, pieces, heads, keep, in...  12.1 us
    pallas_call x1, Pallas kernels, run_prepare(): pl.pallas_call(functools.partial(prepare, layout, heads), out_shape=[flat...  2.49 us
    unnamed x15, local copies, waits for them, and re-layouts  2.46 us
  transfers between devices with their start and end apart: 20, of which 12 were waited for; matrix products, arithmetic and copies ran while one was open for 0% of the time, Pallas kernels for 5%

profile of v1, /device:TPU:0, one launch (start us, length us, event | category | flops | bytes accessed | tf_op | source)
XLA Modules:
  0.0 70.3 jit_solution(14862976824683230466)
XLA Ops:
  0.7 0.8 %constant_dynamic-update-slice_fusion.1 = (bf16[256,128]{1,0:T(8,128)(2,1)S(1)}, bf16[1024,128]{1,0:T(8,128)(2,1)S(1)}) fusion(bf16[128,128]{1,0:T(8,128)(2,1)} %param.10), kind=kLoop, calls=%fused_computation.9 | loop fusion | bytes 98304
  1.5 3.1 %collective-permute-start = (bf16[256,128]{1,0:T(8,128)(2,1)S(1)}, bf16[256,128]{1,0:T(8,128)(2,1)S(1)}, u32[]{:S(2)}, u32[]{:S(2)}) collective-permute-start(bf16[256,128]{1,0:T(8,128)(2,1)S(1)} %get-tuple-element.33), channel_id=1, source_target_pairs={{0,4},{1,3},{2,6},{3,1},{4,0},{5,7},{6,2},{7,5},{8,12},{9,11},{10,... | collective-permute-start | bytes 196616 | tf_op jit(solution)/shard_map/ppermute | solution.py:290
  4.6 1.4 %collective-permute-start.2 = (bf16[256,128]{1,0:T(8,128)(2,1)S(1)}, bf16[256,128]{1,0:T(8,128)(2,1)S(1)}, u32[]{:S(2)}, u32[]{:S(2)}) collective-permute-start(bf16[256,128]{1,0:T(8,128)(2,1)S(1)} %get-tuple-element.33), channel_id=1, source_target_pairs={{0,20},{1,15},{2,22},{3,13},{4,16},{5,11},{6,18},{7,9},{8,28},{9,7... | collective-permute-start | bytes 196616 | tf_op jit(solution)/shard_map/ppermute | solution.py:290
  6.2 0.7 %collective-permute-done = bf16[256,128]{1,0:T(8,128)(2,1)S(1)} collective-permute-done((bf16[256,128]{1,0:T(8,128)(2,1)S(1)}, bf16[256,128]{1,0:T(8,128)(2,1)S(1)}, u32[]{:S(2)}, u32[]{:S(2)}) %collective-permute-start) | collective-permute-done | bytes 65568 | tf_op jit(solution)/shard_map/ppermute | solution.py:290
  6.9 3.6 %collective-permute-done.1 = bf16[256,128]{1,0:T(8,128)(2,1)S(1)} collective-permute-done((bf16[256,128]{1,0:T(8,128)(2,1)S(1)}, bf16[256,128]{1,0:T(8,128)(2,1)S(1)}, u32[]{:S(2)}, u32[]{:S(2)}) %collective-permute-start.1) | collective-permute-done | bytes 65568 | tf_op jit(solution)/shard_map/ppermute | solution.py:290
  10.5 4.4 %collective-permute-start.5 = (bf16[1024,128]{1,0:T(8,128)(2,1)S(1)}, bf16[1024,128]{1,0:T(8,128)(2,1)S(1)}, u32[]{:S(2)}, u32[]{:S(2)}) collective-permute-start(bf16[1024,128]{1,0:T(8,128)(2,1)S(1)} %constant_dynamic-update-slice_fusion.2.refs_0_), channel_id=1, source_target_pairs={{0,14},{1,21},{2,12},{3,23},{4,10},{5,17},{6,8},{7,19},{8,6},{9,29... | collective-permute-start | bytes 786440 | tf_op jit(solution)/shard_map/ppermute | solution.py:290
  15.9 6.6 %collective-permute-done.5.refs_3_ = bf16[1024,128]{1,0:T(8,128)(2,1)S(1)} collective-permute-done((bf16[1024,128]{1,0:T(8,128)(2,1)S(1)}, bf16[1024,128]{1,0:T(8,128)(2,1)S(1)}, u32[]{:S(2)}, u32[]{:S(2)}) %collective-permute-start.5) | collective-permute-done | bytes 262176 | tf_op jit(solution)/shard_map/ppermute | solution.py:290
  22.5 3.4 %collective-permute-done.4.refs_2_ = bf16[1024,128]{1,0:T(8,128)(2,1)S(1)} collective-permute-done((bf16[1024,128]{1,0:T(8,128)(2,1)S(1)}, bf16[1024,128]{1,0:T(8,128)(2,1)S(1)}, u32[]{:S(2)}, u32[]{:S(2)}) %collective-permute-start.4) | collective-permute-done | bytes 262176 | tf_op jit(solution)/shard_map/ppermute | solution.py:290
  25.9 1.1 %collective-permute-start.7 = (bf16[1024,128]{1,0:T(8,128)(2,1)S(1)}, bf16[1024,128]{1,0:T(8,128)(2,1)S(1)}, u32[]{:S(2)}, u32[]{:S(2)}) collective-permute-start(bf16[1024,128]{1,0:T(8,128)(2,1)S(1)} %collective-permute-done.3.refs_1_), channel_id=1, source_target_pairs={{0,1},{1,0},{2,3},{3,2},{4,5},{5,4},{6,7},{7,6},{8,9},{9,8},{10,11... | collective-permute-start | bytes 786440 | tf_op jit(solution)/shard_map/ppermute | solution.py:290
  28.4 0.9 %copy-done.2 = bf16[128,1024]{1,0:T(8,128)(2,1)S(1)} copy-done((bf16[128,1024]{1,0:T(8,128)(2,1)S(1)}, bf16[128,1024]{1,0:T(8,128)(2,1)}, u32[]{:S(2)}) %copy-start.2) | copy-done | bytes 262168
  29.4 2.5 %prep.1 = (bf16[1024,128]{1,0:T(8,128)(2,1)S(1)}, bf16[1024,128]{1,0:T(8,128)(2,1)S(1)}, f32[1,1024]{1,0:T(1,128)S(1)}, s32[36]{0:T(128)S(1)}) custom-call(s32[2]{0:T(128)S(1)} %pad_add_fusion.here, s32[32]{0:T(128)S(1)} %copy-done.3, s32[1]{0:T(128)S(6)} %copy.16.window, bf16[128,1024]{1,0:T(8,128)(2,1)S(1)} %copy-done, s32[1,128]{1,0:T(1,128)S(1)} %bitcast.3, ...), custom_call_target="tpu_custom_call" | custom-call | tf_op jit(solution)/shard_map/prep/pallas_call | solution.py:220
  31.9 12.1 %attend.1 = (f32[128,1024]{1,0:T(8,128)S(1)}, bf16[4096,128]{1,0:T(8,128)(2,1)S(1)}, bf16[1024,128]{1,0:T(8,128)(2,1)S(1)}, bf16[1024,128]{1,0:T(8,128)(2,1)S(1)...) custom-call(s32[36]{0:T(128)S(1)} %get-tuple-element.13.meta, ...), custom_call_target="tpu_custom_call" | custom-call | tf_op jit(solution)/shard_map/attend/pallas_call | solution.py:244
  46.6 1.2 %collective-permute-start.12 = (bf16[1024,128]{1,0:T(8,128)(2,1)S(1)}, bf16[1024,128]{1,0:T(8,128)(2,1)S(1)}, u32[]{:S(2)}, u32[]{:S(2)}) collective-permute-start(bf16[1024,128]{1,0:T(8,128)(2,1)S(1)} %get-tuple-element.25), channel_id=1, source_target_pairs={{0,2},{1,5},{2,0},{3,7},{4,6},{5,1},{6,4},{7,3},{8,10},{9,13},{10,... | collective-permute-start | bytes 786440 | tf_op jit(solution)/shard_map/ppermute | solution.py:290
  47.8 2.0 %collective-permute-start.16 = (bf16[1024,128]{1,0:T(8,128)(2,1)S(1)}, bf16[1024,128]{1,0:T(8,128)(2,1)S(1)}, u32[]{:S(2)}, u32[]{:S(2)}) collective-permute-start(bf16[1024,128]{1,0:T(8,128)(2,1)S(1)} %get-tuple-element.26), channel_id=1, source_target_pairs={{0,14},{1,21},{2,12},{3,23},{4,10},{5,17},{6,8},{7,19},{8,6},{9,29... | collective-permute-start | bytes 786440 | tf_op jit(solution)/shard_map/ppermute | solution.py:290
  49.8 2.2 %collective-permute-start.14 = (bf16[1024,128]{1,0:T(8,128)(2,1)S(1)}, bf16[1024,128]{1,0:T(8,128)(2,1)S(1)}, u32[]{:S(2)}, u32[]{:S(2)}) collective-permute-start(bf16[1024,128]{1,0:T(8,128)(2,1)S(1)} %get-tuple-element.27), channel_id=1, source_target_pairs={{0,12},{1,17},{2,14},{3,19},{4,8},{5,21},{6,10},{7,23},{8,4},{9,25... | collective-permute-start | bytes 786440 | tf_op jit(solution)/shard_map/ppermute | solution.py:290
  52.0 1.1 %collective-permute-done.12 = bf16[1024,128]{1,0:T(8,128)(2,1)S(1)} collective-permute-done((bf16[1024,128]{1,0:T(8,128)(2,1)S(1)}, bf16[1024,128]{1,0:T(8,128)(2,1)S(1)}, u32[]{:S(2)}, u32[]{:S(2)}) %collective-permute-start.12) | collective-permute-done | bytes 262176 | tf_op jit(solution)/shard_map/ppermute | solution.py:290
  53.1 6.6 %collective-permute-done.16 = bf16[1024,128]{1,0:T(8,128)(2,1)S(1)} collective-permute-done((bf16[1024,128]{1,0:T(8,128)(2,1)S(1)}, bf16[1024,128]{1,0:T(8,128)(2,1)S(1)}, u32[]{:S(2)}, u32[]{:S(2)}) %collective-permute-start.16) | collective-permute-done | bytes 262176 | tf_op jit(solution)/shard_map/ppermute | solution.py:290
  59.6 2.9 %collective-permute-done.14 = bf16[1024,128]{1,0:T(8,128)(2,1)S(1)} collective-permute-done((bf16[1024,128]{1,0:T(8,128)(2,1)S(1)}, bf16[1024,128]{1,0:T(8,128)(2,1)S(1)}, u32[]{:S(2)}, u32[]{:S(2)}) %collective-permute-start.14) | collective-permute-done | bytes 262176 | tf_op jit(solution)/shard_map/ppermute | solution.py:290
  62.7 1.0 %collective-permute-start.17 = (bf16[256,128]{1,0:T(8,128)(2,1)S(1)}, bf16[256,128]{1,0:T(8,128)(2,1)S(1)}, u32[]{:S(2)}, u32[]{:S(2)}) collective-permute-start(bf16[256,128]{1,0:T(8,128)(2,1)S(1)} %get-tuple-element.28), channel_id=1, source_target_pairs={{0,4},{1,3},{2,6},{3,1},{4,0},{5,7},{6,2},{7,5},{8,12},{9,11},{10,... | collective-permute-start | bytes 196616 | tf_op jit(solution)/shard_map/ppermute | solution.py:290
  63.7 1.5 %collective-permute-start.19 = (bf16[256,128]{1,0:T(8,128)(2,1)S(1)}, bf16[256,128]{1,0:T(8,128)(2,1)S(1)}, u32[]{:S(2)}, u32[]{:S(2)}) collective-permute-start(bf16[256,128]{1,0:T(8,128)(2,1)S(1)} %get-tuple-element.29), channel_id=1, source_target_pairs={{0,20},{1,15},{2,22},{3,13},{4,16},{5,11},{6,18},{7,9},{8,28},{9,7... | collective-permute-start | bytes 196616 | tf_op jit(solution)/shard_map/ppermute | solution.py:290
  65.3 1.0 %collective-permute-start.18 = (bf16[256,128]{1,0:T(8,128)(2,1)S(1)}, bf16[256,128]{1,0:T(8,128)(2,1)S(1)}, u32[]{:S(2)}, u32[]{:S(2)}) collective-permute-start(bf16[256,128]{1,0:T(8,128)(2,1)S(1)} %get-tuple-element.30), channel_id=1, source_target_pairs={{0,16},{1,13},{2,18},{3,15},{4,20},{5,9},{6,22},{7,11},{8,24},{9,5... | collective-permute-start | bytes 196616 | tf_op jit(solution)/shard_map/ppermute | solution.py:290
  66.3 0.9 %turn.1 = bf16[128,1024]{1,0:T(8,128)(2,1)} custom-call(f32[128,1024]{1,0:T(8,128)S(1)} %get-tuple-element.17.turned), custom_call_target="tpu_custom_call" | custom-call | tf_op jit(solution)/shard_map/turn/pallas_call | solution.py:268
  67.2 1.7 %collective-permute-done.19 = bf16[256,128]{1,0:T(8,128)(2,1)S(1)} collective-permute-done((bf16[256,128]{1,0:T(8,128)(2,1)S(1)}, bf16[256,128]{1,0:T(8,128)(2,1)S(1)}, u32[]{:S(2)}, u32[]{:S(2)}) %collective-permute-start.19) | collective-permute-done | bytes 65568 | tf_op jit(solution)/shard_map/ppermute | solution.py:290
  68.9 0.7 collective-permute-done.18
  (42 shorter events, 5.4 us)
Async XLA Ops:
  0.6 0.8 %copy-start.5 = (bf16[128,128]{1,0:T(8,128)(2,1)S(1)}, bf16[128,128]{1,0:T(8,128)(2,1)}, u32[]{:S(2)}) copy-start(bf16[128,128]{1,0:T(8,128)(2,1)} %param.11) | copy-start | bytes 98308
  0.6 27.1 %copy-start.1 = (bf16[128,1024]{1,0:T(8,128)(2,1)S(1)}, bf16[128,1024]{1,0:T(8,128)(2,1)}, u32[]{:S(2)}) copy-start(bf16[128,1024]{1,0:T(8,128)(2,1)} %g_ref.1) | copy-start | bytes 786436
  1.5 26.3 %copy-start = (bf16[128,1024]{1,0:T(8,128)(2,1)S(1)}, bf16[128,1024]{1,0:T(8,128)(2,1)}, u32[]{:S(2)}) copy-start(bf16[128,1024]{1,0:T(8,128)(2,1)} %q_ref.1) | copy-start | bytes 786436
  1.5 5.4 %collective-permute-start = (bf16[256,128]{1,0:T(8,128)(2,1)S(1)}, bf16[256,128]{1,0:T(8,128)(2,1)S(1)}, u32[]{:S(2)}, u32[]{:S(2)}) collective-permute-start(bf16[256,128]{1,0:T(8,128)(2,1)S(1)} %get-tuple-element.33), channel_id=1, source_target_pairs={{0,4},{1,3},{2,6},{3,1},{4,0},{5,7},{6,2},{7,5},{8,12},{9,11},{10,... | collective-permute-start | bytes 196616 | tf_op jit(solution)/shard_map/ppermute | solution.py:290
  4.6 5.9 %collective-permute-start.2 = (bf16[256,128]{1,0:T(8,128)(2,1)S(1)}, bf16[256,128]{1,0:T(8,128)(2,1)S(1)}, u32[]{:S(2)}, u32[]{:S(2)}) collective-permute-start(bf16[256,128]{1,0:T(8,128)(2,1)S(1)} %get-tuple-element.33), channel_id=1, source_target_pairs={{0,20},{1,15},{2,22},{3,13},{4,16},{5,11},{6,18},{7,9},{8,28},{9,7... | collective-permute-start | bytes 196616 | tf_op jit(solution)/shard_map/ppermute | solution.py:290
  6.0 4.5 %collective-permute-start.1 = (bf16[256,128]{1,0:T(8,128)(2,1)S(1)}, bf16[256,128]{1,0:T(8,128)(2,1)S(1)}, u32[]{:S(2)}, u32[]{:S(2)}) collective-permute-start(bf16[256,128]{1,0:T(8,128)(2,1)S(1)} %get-tuple-element.33), channel_id=1, source_target_pairs={{0,16},{1,13},{2,18},{3,15},{4,20},{5,9},{6,22},{7,11},{8,24},{9,5... | collective-permute-start | bytes 196616 | tf_op jit(solution)/shard_map/ppermute | solution.py:290
  10.5 11.9 %collective-permute-start.5 = (bf16[1024,128]{1,0:T(8,128)(2,1)S(1)}, bf16[1024,128]{1,0:T(8,128)(2,1)S(1)}, u32[]{:S(2)}, u32[]{:S(2)}) collective-permute-start(bf16[1024,128]{1,0:T(8,128)(2,1)S(1)} %constant_dynamic-update-slice_fusion.2.refs_0_), channel_id=1, source_target_pairs={{0,14},{1,21},{2,12},{3,23},{4,10},{5,17},{6,8},{7,19},{8,6},{9,29... | collective-permute-start | bytes 786440 | tf_op jit(solution)/shard_map/ppermute | solution.py:290
  14.9 11.0 %collective-permute-start.4 = (bf16[1024,128]{1,0:T(8,128)(2,1)S(1)}, bf16[1024,128]{1,0:T(8,128)(2,1)S(1)}, u32[]{:S(2)}, u32[]{:S(2)}) collective-permute-start(bf16[1024,128]{1,0:T(8,128)(2,1)S(1)} %constant_dynamic-update-slice_fusion.2.refs_0_), channel_id=1, source_target_pairs={{0,12},{1,17},{2,14},{3,19},{4,8},{5,21},{6,10},{7,23},{8,4},{9,25... | collective-permute-start | bytes 786440 | tf_op jit(solution)/shard_map/ppermute | solution.py:290
  15.5 10.5 %collective-permute-start.3 = (bf16[1024,128]{1,0:T(8,128)(2,1)S(1)}, bf16[1024,128]{1,0:T(8,128)(2,1)S(1)}, u32[]{:S(2)}, u32[]{:S(2)}) collective-permute-start(bf16[1024,128]{1,0:T(8,128)(2,1)S(1)} %constant_dynamic-update-slice_fusion.2.refs_0_), channel_id=1, source_target_pairs={{0,2},{1,5},{2,0},{3,7},{4,6},{5,1},{6,4},{7,3},{8,10},{9,13},{10,... | collective-permute-start | bytes 786440 | tf_op jit(solution)/shard_map/ppermute | solution.py:290
  15.9 16.0 %collective-permute-start.6 = (bf16[1024,128]{1,0:T(8,128)(2,1)S(1)}, bf16[1024,128]{1,0:T(8,128)(2,1)S(1)}, u32[]{:S(2)}, u32[]{:S(2)}) collective-permute-start(bf16[1024,128]{1,0:T(8,128)(2,1)S(1)} %constant_dynamic-update-slice_fusion.2.refs_0_), channel_id=1, source_target_pairs={{0,1},{1,0},{2,3},{3,2},{4,5},{5,4},{6,7},{7,6},{8,9},{9,8},{10,11... | collective-permute-start | bytes 786440 | tf_op jit(solution)/shard_map/ppermute | solution.py:290
  22.5 9.4 %collective-permute-start.9 = (bf16[1024,128]{1,0:T(8,128)(2,1)S(1)}, bf16[1024,128]{1,0:T(8,128)(2,1)S(1)}, u32[]{:S(2)}, u32[]{:S(2)}) collective-permute-start(bf16[1024,128]{1,0:T(8,128)(2,1)S(1)} %collective-permute-done.5.refs_3_), channel_id=1, source_target_pairs={{0,1},{1,0},{2,3},{3,2},{4,5},{5,4},{6,7},{7,6},{8,9},{9,8},{10,11... | collective-permute-start | bytes 786440 | tf_op jit(solution)/shard_map/ppermute | solution.py:290
  25.9 6.0 %collective-permute-start.8 = (bf16[1024,128]{1,0:T(8,128)(2,1)S(1)}, bf16[1024,128]{1,0:T(8,128)(2,1)S(1)}, u32[]{:S(2)}, u32[]{:S(2)}) collective-permute-start(bf16[1024,128]{1,0:T(8,128)(2,1)S(1)} %collective-permute-done.4.refs_2_), channel_id=1, source_target_pairs={{0,1},{1,0},{2,3},{3,2},{4,5},{5,4},{6,7},{7,6},{8,9},{9,8},{10,11... | collective-permute-start | bytes 786440 | tf_op jit(solution)/shard_map/ppermute | solution.py:290
  25.9 6.0 %collective-permute-start.7 = (bf16[1024,128]{1,0:T(8,128)(2,1)S(1)}, bf16[1024,128]{1,0:T(8,128)(2,1)S(1)}, u32[]{:S(2)}, u32[]{:S(2)}) collective-permute-start(bf16[1024,128]{1,0:T(8,128)(2,1)S(1)} %collective-permute-done.3.refs_1_), channel_id=1, source_target_pairs={{0,1},{1,0},{2,3},{3,2},{4,5},{5,4},{6,7},{7,6},{8,9},{9,8},{10,11... | collective-permute-start | bytes 786440 | tf_op jit(solution)/shard_map/ppermute | solution.py:290
  28.4 0.9 %copy-start.2 = (bf16[128,1024]{1,0:T(8,128)(2,1)S(1)}, bf16[128,1024]{1,0:T(8,128)(2,1)}, u32[]{:S(2)}) copy-start(bf16[128,1024]{1,0:T(8,128)(2,1)} %o_ref.1) | copy-start | bytes 786436
  44.1 1.6 %collective-permute-start.11 = (bf16[1024,128]{1,0:T(8,128)(2,1)S(1)}, bf16[1024,128]{1,0:T(8,128)(2,1)S(1)}, u32[]{:S(2)}, u32[]{:S(2)}) collective-permute-start(bf16[1024,128]{1,0:T(8,128)(2,1)S(1)} %get-tuple-element.20), channel_id=1, source_target_pairs={{0,1},{1,0},{2,3},{3,2},{4,5},{5,4},{6,7},{7,6},{8,9},{9,8},{10,11... | collective-permute-start | bytes 786440 | tf_op jit(solution)/shard_map/ppermute | solution.py:290
  44.2 1.9 %collective-permute-start.13 = (bf16[1024,128]{1,0:T(8,128)(2,1)S(1)}, bf16[1024,128]{1,0:T(8,128)(2,1)S(1)}, u32[]{:S(2)}, u32[]{:S(2)}) collective-permute-start(bf16[1024,128]{1,0:T(8,128)(2,1)S(1)} %get-tuple-element.21), channel_id=1, source_target_pairs={{0,1},{1,0},{2,3},{3,2},{4,5},{5,4},{6,7},{7,6},{8,9},{9,8},{10,11... | collective-permute-start | bytes 786440 | tf_op jit(solution)/shard_map/ppermute | solution.py:290
  44.6 1.8 %collective-permute-start.15 = (bf16[1024,128]{1,0:T(8,128)(2,1)S(1)}, bf16[1024,128]{1,0:T(8,128)(2,1)S(1)}, u32[]{:S(2)}, u32[]{:S(2)}) collective-permute-start(bf16[1024,128]{1,0:T(8,128)(2,1)S(1)} %get-tuple-element.22), channel_id=1, source_target_pairs={{0,1},{1,0},{2,3},{3,2},{4,5},{5,4},{6,7},{7,6},{8,9},{9,8},{10,11... | collective-permute-start | bytes 786440 | tf_op jit(solution)/shard_map/ppermute | solution.py:290
  44.7 7.3 %collective-permute-start.10 = (bf16[1024,128]{1,0:T(8,128)(2,1)S(1)}, bf16[1024,128]{1,0:T(8,128)(2,1)S(1)}, u32[]{:S(2)}, u32[]{:S(2)}) collective-permute-start(bf16[1024,128]{1,0:T(8,128)(2,1)S(1)} %get-tuple-element.19), channel_id=1, source_target_pairs={{0,1},{1,0},{2,3},{3,2},{4,5},{5,4},{6,7},{7,6},{8,9},{9,8},{10,11... | collective-permute-start | bytes 786440 | tf_op jit(solution)/shard_map/ppermute | solution.py:290
  46.6 6.4 %collective-permute-start.12 = (bf16[1024,128]{1,0:T(8,128)(2,1)S(1)}, bf16[1024,128]{1,0:T(8,128)(2,1)S(1)}, u32[]{:S(2)}, u32[]{:S(2)}) collective-permute-start(bf16[1024,128]{1,0:T(8,128)(2,1)S(1)} %get-tuple-element.25), channel_id=1, source_target_pairs={{0,2},{1,5},{2,0},{3,7},{4,6},{5,1},{6,4},{7,3},{8,10},{9,13},{10,... | collective-permute-start | bytes 786440 | tf_op jit(solution)/shard_map/ppermute | solution.py:290
  47.8 11.8 %collective-permute-start.16 = (bf16[1024,128]{1,0:T(8,128)(2,1)S(1)}, bf16[1024,128]{1,0:T(8,128)(2,1)S(1)}, u32[]{:S(2)}, u32[]{:S(2)}) collective-permute-start(bf16[1024,128]{1,0:T(8,128)(2,1)S(1)} %get-tuple-element.26), channel_id=1, source_target_pairs={{0,14},{1,21},{2,12},{3,23},{4,10},{5,17},{6,8},{7,19},{8,6},{9,29... | collective-permute-start | bytes 786440 | tf_op jit(solution)/shard_map/ppermute | solution.py:290
  49.8 12.8 %collective-permute-start.14 = (bf16[1024,128]{1,0:T(8,128)(2,1)S(1)}, bf16[1024,128]{1,0:T(8,128)(2,1)S(1)}, u32[]{:S(2)}, u32[]{:S(2)}) collective-permute-start(bf16[1024,128]{1,0:T(8,128)(2,1)S(1)} %get-tuple-element.27), channel_id=1, source_target_pairs={{0,12},{1,17},{2,14},{3,19},{4,8},{5,21},{6,10},{7,23},{8,4},{9,25... | collective-permute-start | bytes 786440 | tf_op jit(solution)/shard_map/ppermute | solution.py:290
  62.7 4.5 %collective-permute-start.17 = (bf16[256,128]{1,0:T(8,128)(2,1)S(1)}, bf16[256,128]{1,0:T(8,128)(2,1)S(1)}, u32[]{:S(2)}, u32[]{:S(2)}) collective-permute-start(bf16[256,128]{1,0:T(8,128)(2,1)S(1)} %get-tuple-element.28), channel_id=1, source_target_pairs={{0,4},{1,3},{2,6},{3,1},{4,0},{5,7},{6,2},{7,5},{8,12},{9,11},{10,... | collective-permute-start | bytes 196616 | tf_op jit(solution)/shard_map/ppermute | solution.py:290
  63.7 5.2 %collective-permute-start.19 = (bf16[256,128]{1,0:T(8,128)(2,1)S(1)}, bf16[256,128]{1,0:T(8,128)(2,1)S(1)}, u32[]{:S(2)}, u32[]{:S(2)}) collective-permute-start(bf16[256,128]{1,0:T(8,128)(2,1)S(1)} %get-tuple-element.29), channel_id=1, source_target_pairs={{0,20},{1,15},{2,22},{3,13},{4,16},{5,11},{6,18},{7,9},{8,28},{9,7... | collective-permute-start | bytes 196616 | tf_op jit(solution)/shard_map/ppermute | solution.py:290
  65.3 4.4 %collective-permute-start.18 = (bf16[256,128]{1,0:T(8,128)(2,1)S(1)}, bf16[256,128]{1,0:T(8,128)(2,1)S(1)}, u32[]{:S(2)}, u32[]{:S(2)}) collective-permute-start(bf16[256,128]{1,0:T(8,128)(2,1)S(1)} %get-tuple-element.30), channel_id=1, source_target_pairs={{0,16},{1,13},{2,18},{3,15},{4,20},{5,9},{6,22},{7,11},{8,24},{9,5... | collective-permute-start | bytes 196616 | tf_op jit(solution)/shard_map/ppermute | solution.py:290
  (2 other events, 1.3 us)

commit v2 on v1

--- a/solution.py
+++ b/solution.py
@@ -100,12 +100,14 @@
 ):
     held, rest = refs[: 2 * pieces], refs[2 * pieces :]
     dq_ref, own_out, other_out, rest = rest[0], rest[1], rest[2 : 2 + pieces], rest[2 + pieces :]
-    kv, probs, tops, weight_buf, grad_buf, run_max, run_sum = rest
+    kv, probs, weight_a, weight_b, grad_a, grad_b, run_max, run_sum, top, inverse = rest
     half_rows = stripes // 2 * PAIR
     piece_rows = half_rows // pieces
     to_log2 = inv_scale * math.log2(math.e)
     live, window_len = meta[0], meta[1]
     turns = (live + 1) // 2
+    last_whole = jnp.minimum(live - 1, (window_len - STRIPE) // STRIPE)
+    middle = jnp.maximum((last_whole + 1) // 2, 1)
 
     for i, ref in enumerate(held):
         kv[pl.ds(i * piece_rows, piece_rows)] = ref[...]
@@ -116,89 +118,128 @@
     run_sum[...] = jnp.zeros_like(run_sum)
     dq_ref[...] = jnp.zeros_like(dq_ref)
 
-    relative = lax.broadcasted_iota(jnp.int32, (STRIPE, STRIPE), 1) - lax.broadcasted_iota(
-        jnp.int32, (STRIPE, STRIPE), 0
-    )
+    group = 2 if heads % 2 == 0 else 1
+    wide = group * STRIPE
+    groups = [pl.ds(i * wide, wide) for i in range(heads // group)]
 
     def offsets_of(turn):
         return [pl.multiple_of(meta[2 + 2 * turn + i], PAIR) for i in range(2)]
 
-    def rows_at(offsets, shift):
-        return jnp.concatenate([kv[pl.ds(offset + shift, STRIPE)] for offset in offsets], 0)
+    def rows_at(turn, shift):
+        return jnp.concatenate([kv[pl.ds(offset + shift, STRIPE)] for offset in offsets_of(turn)], 0)
 
     def visible_at(turn):
+        relative = lax.broadcasted_iota(jnp.int32, (STRIPE, STRIPE), 1) - lax.broadcasted_iota(
+            jnp.int32, (STRIPE, STRIPE), 0
+        )
         masks = []
         for i in range(2):
             block = 2 * turn + i
             distance = relative + jnp.where(block < live, block * STRIPE, far_away)
             masks.append((distance >= 0) & (distance < window_len))
-        return jnp.concatenate(masks, 0)
-
-    def head_cols(head):
-        return pl.ds(head * STRIPE, STRIPE)
-
-    def masked_scores(key_rows, visible, head):
-        scores = dot(key_rows, q_ref[head_cols(head)], 1, 1) * to_log2
-        return jnp.where(visible, scores, neg_big)
-
-    def add_stats(turn, carry):
-        key_rows = rows_at(offsets_of(turn), 0)
-        visible = visible_at(turn)
-        for head in range(heads):
-            cols = head_cols(head)
-            scores = masked_scores(key_rows, visible, head)
-            old_max = run_max[:, cols]
-            new_max = jnp.maximum(old_max, jnp.max(scores, axis=0, keepdims=True))
-            part = jnp.exp2(scores - new_max)
-            summed = jnp.sum(part.reshape(-1, 8, STRIPE), axis=0)
-            run_sum[:, cols] = run_sum[:, cols] * jnp.exp2(old_max - new_max) + summed
-            run_max[:, cols] = new_max
+        mask = jnp.concatenate(masks, 0)
+        return jnp.concatenate([mask] * group, 1)
+
+    def scores_of(key_rows, visible, cols):
+        scores = dot(key_rows, q_ref[cols], 1, 1)
+        return scores if visible is None else jnp.where(visible, scores, neg_big)
+
+    def by_eight(value):
+        return value.reshape(-1, 8, value.shape[1])
+
+    def find_max(turn, visible):
+        key_rows = rows_at(turn, 0)
+        for cols in groups:
+            scores = scores_of(key_rows, visible, cols)
+            run_max[:, cols] = jnp.maximum(run_max[:, cols], jnp.max(by_eight(scores), axis=0))
+            if keep:
+                probs[turn, :, cols] = scores
+
+    def masked_max(turn, carry):
+        find_max(turn, visible_at(turn))
+        return carry
+
+    def plain_max(turn, carry):
+        find_max(turn, None)
+        return carry
+
+    lax.fori_loop(0, 1, masked_max, 0)
+    lax.fori_loop(1, middle, plain_max, 0)
+    lax.fori_loop(middle, turns, masked_max, 0)
+    top[...] = jnp.max(run_max[...], axis=0, keepdims=True) * to_log2
+
+    def exponentials(turn, cols):
+        if keep:
+            scores = probs[turn, :, cols]
+        else:
+            scores = scores_of(rows_at(turn, 0), visible_at(turn), cols)
+        return jnp.exp2(scores * to_log2 - top[:, cols])
+
+    def add_sums(turn, carry):
+        for cols in groups:
+            part = exponentials(turn, cols)
+            run_sum[:, cols] += jnp.sum(by_eight(part), axis=0)
             if keep:
                 probs[turn, :, cols] = part
-                tops[turn, :, cols] = new_max
-        return carry
-
-    lax.fori_loop(0, turns, add_stats, 0)
-    total = jnp.sum(run_sum[...], axis=0, keepdims=True)
-    run_sum[pl.ds(0, 1)] = 1.0 / total
-
-    def add_grads(turn, carry):
-        offsets = offsets_of(turn)
-        key_rows, value_rows = rows_at(offsets, 0), rows_at(offsets, STRIPE)
-        if not keep:
-            visible = visible_at(turn)
-        for head in range(heads):
-            cols = head_cols(head)
-            if keep:
-                factor = jnp.exp2(tops[turn, :, cols] - run_max[:, cols]) * run_sum[pl.ds(0, 1), cols]
-                weights = probs[turn, :, cols] * factor
-            else:
-                scores = masked_scores(key_rows, visible, head)
-                weights = jnp.exp2(scores - run_max[:, cols]) * run_sum[pl.ds(0, 1), cols]
+        return carry
+
+    lax.fori_loop(0, turns, add_sums, 0)
+    inverse[...] = 1.0 / jnp.sum(run_sum[...], axis=0, keepdims=True)
+
+    def find_grads(turn, weight_buf, grad_buf):
+        value_rows = rows_at(turn, STRIPE)
+        for cols in groups:
+            part = probs[turn, :, cols] if keep else exponentials(turn, cols)
+            weights = part * inverse[:, cols]
             weight_grad = dot(value_rows, g_ref[cols], 1, 1)
             score_grad = weights * (weight_grad - delta_ref[:, cols])
             weight_buf[:, cols] = weights.astype(jnp.bfloat16)
             grad_buf[:, cols] = score_grad.astype(jnp.bfloat16)
+
+    def products(turn, weight_buf, grad_buf):
         score_grads = grad_buf[...]
-        dq_ref[...] += dot(key_rows, score_grads, 0, 0)
+        dq_ref[...] += dot(rows_at(turn, 0), score_grads, 0, 0)
         key_part = (dot(score_grads, q_ref[...], 1, 0) * inv_scale).astype(jnp.bfloat16)
         value_part = dot(weight_buf[...], g_ref[...], 1, 0).astype(jnp.bfloat16)
-        for i, offset in enumerate(offsets):
-            part = slice(i * STRIPE, (i + 1) * STRIPE)
-            spans = [(0, half_rows, own_out)] + [
-                (half_rows + j * piece_rows, piece_rows, ref) for j, ref in enumerate(other_out)
-            ]
+        return key_part, value_part
+
+    def store(turn, parts):
+        spans = [(0, half_rows, own_out)] + [
+            (half_rows + j * piece_rows, piece_rows, ref) for j, ref in enumerate(other_out)
+        ]
+        for i, offset in enumerate(offsets_of(turn)):
+            rows = slice(i * STRIPE, (i + 1) * STRIPE)
             for start, length, ref in spans:
 
                 @pl.when((offset >= start) & (offset < start + length))
                 def _(start=start, ref=ref):
                     inner = pl.multiple_of(offset - start, PAIR)
-                    ref[pl.ds(inner, STRIPE)] = key_part[part]
-                    ref[pl.ds(inner + STRIPE, STRIPE)] = value_part[part]
-
-        return carry
-
-    lax.fori_loop(0, turns, add_grads, 0)
+                    for j, part in enumerate(parts):
+                        ref[pl.ds(inner + j * STRIPE, STRIPE)] = part[rows]
+
+    a, b = (weight_a, grad_a), (weight_b, grad_b)
+
+    def step(turn, now, before):
+        parts = products(turn - 1, *before)
+        find_grads(turn, *now)
+        store(turn - 1, parts)
+
+    def two_steps(pair, carry):
+        step(2 * pair + 1, b, a)
+        step(2 * pair + 2, a, b)
+        return carry
+
+    find_grads(0, *a)
+    lax.fori_loop(0, (turns - 1) // 2, two_steps, 0)
+
+    @pl.when(turns % 2 == 0)
+    def _():
+        step(turns - 1, b, a)
+        store(turns - 1, products(turns - 1, *b))
+
+    @pl.when(turns % 2 == 1)
+    def _():
+        store(turns - 1, products(turns - 1, *a))
 
 
 def turn_queries(heads, inv_scale, turned, out):
@@ -253,11 +294,9 @@
         scratch_shapes=[
             pltpu.VMEM((2 * half_rows + PAIR, STRIPE), jnp.bfloat16),
             pltpu.VMEM((kept, PAIR, wide), jnp.float32),
-            pltpu.VMEM((kept, 1, wide), jnp.float32),
-            pltpu.VMEM((PAIR, wide), jnp.bfloat16),
-            pltpu.VMEM((PAIR, wide), jnp.bfloat16),
-            pltpu.VMEM((1, wide), jnp.float32),
-            pltpu.VMEM((8, wide), jnp.float32),
+            *[pltpu.VMEM((PAIR, wide), jnp.bfloat16)] * 4,
+            *[pltpu.VMEM((8, wide), jnp.float32)] * 2,
+            *[pltpu.VMEM((1, wide), jnp.float32)] * 2,
         ],
         compiler_params=vmem_limit(limit),
         name="attend",

time: 70.5 us -> 69.2 us (0.982)
  Pallas kernels: 15.5 us -> 14.2 us
    pallas_call x1, Pallas kernels: 12.1 us -> 10.8 us  [run_attend(): pl.pallas_call(functools.partial(attend, stripes, pieces, heads, keep, in...]
where the time goes in v2:
time: 69.2 us; the launch traced here: 69 us
  waiting for transfers between devices  28.6 us (41%)
  starting transfers between devices  21.1 us (30%)
  Pallas kernels  14.2 us (21%)
  local copies, waits for them, and re-layouts  3.14 us (5%)
  between operations  1.44 us (2%)
    ppermute x20, waiting for transfers between devices, send(): return lax.ppermute(value, AXES, layout.hop(**where))  28.6 us
    ppermute x20, starting transfers between devices, send(): return lax.ppermute(value, AXES, layout.hop(**where))  21.1 us
    pallas_call x1, Pallas kernels, run_attend(): pl.pallas_call(functools.partial(attend, stripes, pieces, heads, keep, in...  10.8 us
    pallas_call x1, Pallas kernels, run_prepare(): pl.pallas_call(functools.partial(prepare, layout, heads), out_shape=[flat...  2.49 us
    unnamed x15, local copies, waits for them, and re-layouts  2.46 us
  transfers between devices with their start and end apart: 20, of which 12 were waited for; matrix products, arithmetic and copies ran while one was open for 0% of the time, Pallas kernels for 5%

profile of v2, /device:TPU:0, one launch (start us, length us, event | category | flops | bytes accessed | tf_op | source)
XLA Modules:
  0.0 69.0 jit_solution(8060791040807268863)
XLA Ops:
  0.7 0.8 %constant_dynamic-update-slice_fusion.1 = (bf16[256,128]{1,0:T(8,128)(2,1)S(1)}, bf16[1024,128]{1,0:T(8,128)(2,1)S(1)}) fusion(bf16[128,128]{1,0:T(8,128)(2,1)} %param.10), kind=kLoop, calls=%fused_computation.9 | loop fusion | bytes 98304
  1.5 3.1 %collective-permute-start = (bf16[256,128]{1,0:T(8,128)(2,1)S(1)}, bf16[256,128]{1,0:T(8,128)(2,1)S(1)}, u32[]{:S(2)}, u32[]{:S(2)}) collective-permute-start(bf16[256,128]{1,0:T(8,128)(2,1)S(1)} %get-tuple-element.33), channel_id=1, source_target_pairs={{0,4},{1,3},{2,6},{3,1},{4,0},{5,7},{6,2},{7,5},{8,12},{9,11},{10,... | collective-permute-start | bytes 196616 | tf_op jit(solution)/shard_map/ppermute | solution.py:329
  4.6 1.4 %collective-permute-start.2 = (bf16[256,128]{1,0:T(8,128)(2,1)S(1)}, bf16[256,128]{1,0:T(8,128)(2,1)S(1)}, u32[]{:S(2)}, u32[]{:S(2)}) collective-permute-start(bf16[256,128]{1,0:T(8,128)(2,1)S(1)} %get-tuple-element.33), channel_id=1, source_target_pairs={{0,20},{1,15},{2,22},{3,13},{4,16},{5,11},{6,18},{7,9},{8,28},{9,7... | collective-permute-start | bytes 196616 | tf_op jit(solution)/shard_map/ppermute | solution.py:329
  6.2 0.7 %collective-permute-done = bf16[256,128]{1,0:T(8,128)(2,1)S(1)} collective-permute-done((bf16[256,128]{1,0:T(8,128)(2,1)S(1)}, bf16[256,128]{1,0:T(8,128)(2,1)S(1)}, u32[]{:S(2)}, u32[]{:S(2)}) %collective-permute-start) | collective-permute-done | bytes 65568 | tf_op jit(solution)/shard_map/ppermute | solution.py:329
  6.9 3.6 %collective-permute-done.1 = bf16[256,128]{1,0:T(8,128)(2,1)S(1)} collective-permute-done((bf16[256,128]{1,0:T(8,128)(2,1)S(1)}, bf16[256,128]{1,0:T(8,128)(2,1)S(1)}, u32[]{:S(2)}, u32[]{:S(2)}) %collective-permute-start.1) | collective-permute-done | bytes 65568 | tf_op jit(solution)/shard_map/ppermute | solution.py:329
  10.5 4.4 %collective-permute-start.5 = (bf16[1024,128]{1,0:T(8,128)(2,1)S(1)}, bf16[1024,128]{1,0:T(8,128)(2,1)S(1)}, u32[]{:S(2)}, u32[]{:S(2)}) collective-permute-start(bf16[1024,128]{1,0:T(8,128)(2,1)S(1)} %constant_dynamic-update-slice_fusion.2.refs_0_), channel_id=1, source_target_pairs={{0,14},{1,21},{2,12},{3,23},{4,10},{5,17},{6,8},{7,19},{8,6},{9,29... | collective-permute-start | bytes 786440 | tf_op jit(solution)/shard_map/ppermute | solution.py:329
  15.9 6.6 %collective-permute-done.5.refs_3_ = bf16[1024,128]{1,0:T(8,128)(2,1)S(1)} collective-permute-done((bf16[1024,128]{1,0:T(8,128)(2,1)S(1)}, bf16[1024,128]{1,0:T(8,128)(2,1)S(1)}, u32[]{:S(2)}, u32[]{:S(2)}) %collective-permute-start.5) | collective-permute-done | bytes 262176 | tf_op jit(solution)/shard_map/ppermute | solution.py:329
  22.5 3.4 %collective-permute-done.4.refs_2_ = bf16[1024,128]{1,0:T(8,128)(2,1)S(1)} collective-permute-done((bf16[1024,128]{1,0:T(8,128)(2,1)S(1)}, bf16[1024,128]{1,0:T(8,128)(2,1)S(1)}, u32[]{:S(2)}, u32[]{:S(2)}) %collective-permute-start.4) | collective-permute-done | bytes 262176 | tf_op jit(solution)/shard_map/ppermute | solution.py:329
  25.9 1.1 %collective-permute-start.7 = (bf16[1024,128]{1,0:T(8,128)(2,1)S(1)}, bf16[1024,128]{1,0:T(8,128)(2,1)S(1)}, u32[]{:S(2)}, u32[]{:S(2)}) collective-permute-start(bf16[1024,128]{1,0:T(8,128)(2,1)S(1)} %collective-permute-done.3.refs_1_), channel_id=1, source_target_pairs={{0,1},{1,0},{2,3},{3,2},{4,5},{5,4},{6,7},{7,6},{8,9},{9,8},{10,11... | collective-permute-start | bytes 786440 | tf_op jit(solution)/shard_map/ppermute | solution.py:329
  28.4 0.9 %copy-done.2 = bf16[128,1024]{1,0:T(8,128)(2,1)S(1)} copy-done((bf16[128,1024]{1,0:T(8,128)(2,1)S(1)}, bf16[128,1024]{1,0:T(8,128)(2,1)}, u32[]{:S(2)}) %copy-start.2) | copy-done | bytes 262168
  29.4 2.5 %prep.1 = (bf16[1024,128]{1,0:T(8,128)(2,1)S(1)}, bf16[1024,128]{1,0:T(8,128)(2,1)S(1)}, f32[1,1024]{1,0:T(1,128)S(1)}, s32[36]{0:T(128)S(1)}) custom-call(s32[2]{0:T(128)S(1)} %pad_add_fusion.here, s32[32]{0:T(128)S(1)} %copy-done.3, s32[1]{0:T(128)S(6)} %copy.16.window, bf16[128,1024]{1,0:T(8,128)(2,1)S(1)} %copy-done, s32[1,128]{1,0:T(1,128)S(1)} %bitcast.3, ...), custom_call_target="tpu_custom_call" | custom-call | tf_op jit(solution)/shard_map/prep/pallas_call | solution.py:261
  31.9 10.8 %attend.1 = (f32[128,1024]{1,0:T(8,128)S(1)}, bf16[4096,128]{1,0:T(8,128)(2,1)S(1)}, bf16[1024,128]{1,0:T(8,128)(2,1)S(1)}, bf16[1024,128]{1,0:T(8,128)(2,1)S(1)...) custom-call(s32[36]{0:T(128)S(1)} %get-tuple-element.13.meta, ...), custom_call_target="tpu_custom_call" | custom-call | tf_op jit(solution)/shard_map/attend/pallas_call | solution.py:285
  45.3 1.2 %collective-permute-start.12 = (bf16[1024,128]{1,0:T(8,128)(2,1)S(1)}, bf16[1024,128]{1,0:T(8,128)(2,1)S(1)}, u32[]{:S(2)}, u32[]{:S(2)}) collective-permute-start(bf16[1024,128]{1,0:T(8,128)(2,1)S(1)} %get-tuple-element.25), channel_id=1, source_target_pairs={{0,2},{1,5},{2,0},{3,7},{4,6},{5,1},{6,4},{7,3},{8,10},{9,13},{10,... | collective-permute-start | bytes 786440 | tf_op jit(solution)/shard_map/ppermute | solution.py:329
  46.5 2.0 %collective-permute-start.16 = (bf16[1024,128]{1,0:T(8,128)(2,1)S(1)}, bf16[1024,128]{1,0:T(8,128)(2,1)S(1)}, u32[]{:S(2)}, u32[]{:S(2)}) collective-permute-start(bf16[1024,128]{1,0:T(8,128)(2,1)S(1)} %get-tuple-element.26), channel_id=1, source_target_pairs={{0,14},{1,21},{2,12},{3,23},{4,10},{5,17},{6,8},{7,19},{8,6},{9,29... | collective-permute-start | bytes 786440 | tf_op jit(solution)/shard_map/ppermute | solution.py:329
  48.5 2.2 %collective-permute-start.14 = (bf16[1024,128]{1,0:T(8,128)(2,1)S(1)}, bf16[1024,128]{1,0:T(8,128)(2,1)S(1)}, u32[]{:S(2)}, u32[]{:S(2)}) collective-permute-start(bf16[1024,128]{1,0:T(8,128)(2,1)S(1)} %get-tuple-element.27), channel_id=1, source_target_pairs={{0,12},{1,17},{2,14},{3,19},{4,8},{5,21},{6,10},{7,23},{8,4},{9,25... | collective-permute-start | bytes 786440 | tf_op jit(solution)/shard_map/ppermute | solution.py:329
  50.7 1.1 %collective-permute-done.12 = bf16[1024,128]{1,0:T(8,128)(2,1)S(1)} collective-permute-done((bf16[1024,128]{1,0:T(8,128)(2,1)S(1)}, bf16[1024,128]{1,0:T(8,128)(2,1)S(1)}, u32[]{:S(2)}, u32[]{:S(2)}) %collective-permute-start.12) | collective-permute-done | bytes 262176 | tf_op jit(solution)/shard_map/ppermute | solution.py:329
  51.8 6.6 %collective-permute-done.16 = bf16[1024,128]{1,0:T(8,128)(2,1)S(1)} collective-permute-done((bf16[1024,128]{1,0:T(8,128)(2,1)S(1)}, bf16[1024,128]{1,0:T(8,128)(2,1)S(1)}, u32[]{:S(2)}, u32[]{:S(2)}) %collective-permute-start.16) | collective-permute-done | bytes 262176 | tf_op jit(solution)/shard_map/ppermute | solution.py:329
  58.3 2.9 %collective-permute-done.14 = bf16[1024,128]{1,0:T(8,128)(2,1)S(1)} collective-permute-done((bf16[1024,128]{1,0:T(8,128)(2,1)S(1)}, bf16[1024,128]{1,0:T(8,128)(2,1)S(1)}, u32[]{:S(2)}, u32[]{:S(2)}) %collective-permute-start.14) | collective-permute-done | bytes 262176 | tf_op jit(solution)/shard_map/ppermute | solution.py:329
  61.4 1.0 %collective-permute-start.17 = (bf16[256,128]{1,0:T(8,128)(2,1)S(1)}, bf16[256,128]{1,0:T(8,128)(2,1)S(1)}, u32[]{:S(2)}, u32[]{:S(2)}) collective-permute-start(bf16[256,128]{1,0:T(8,128)(2,1)S(1)} %get-tuple-element.28), channel_id=1, source_target_pairs={{0,4},{1,3},{2,6},{3,1},{4,0},{5,7},{6,2},{7,5},{8,12},{9,11},{10,... | collective-permute-start | bytes 196616 | tf_op jit(solution)/shard_map/ppermute | solution.py:329
  62.4 1.5 %collective-permute-start.19 = (bf16[256,128]{1,0:T(8,128)(2,1)S(1)}, bf16[256,128]{1,0:T(8,128)(2,1)S(1)}, u32[]{:S(2)}, u32[]{:S(2)}) collective-permute-start(bf16[256,128]{1,0:T(8,128)(2,1)S(1)} %get-tuple-element.29), channel_id=1, source_target_pairs={{0,20},{1,15},{2,22},{3,13},{4,16},{5,11},{6,18},{7,9},{8,28},{9,7... | collective-permute-start | bytes 196616 | tf_op jit(solution)/shard_map/ppermute | solution.py:329
  63.9 1.0 %collective-permute-start.18 = (bf16[256,128]{1,0:T(8,128)(2,1)S(1)}, bf16[256,128]{1,0:T(8,128)(2,1)S(1)}, u32[]{:S(2)}, u32[]{:S(2)}) collective-permute-start(bf16[256,128]{1,0:T(8,128)(2,1)S(1)} %get-tuple-element.30), channel_id=1, source_target_pairs={{0,16},{1,13},{2,18},{3,15},{4,20},{5,9},{6,22},{7,11},{8,24},{9,5... | collective-permute-start | bytes 196616 | tf_op jit(solution)/shard_map/ppermute | solution.py:329
  65.0 0.9 %turn.1 = bf16[128,1024]{1,0:T(8,128)(2,1)} custom-call(f32[128,1024]{1,0:T(8,128)S(1)} %get-tuple-element.17.turned), custom_call_target="tpu_custom_call" | custom-call | tf_op jit(solution)/shard_map/turn/pallas_call | solution.py:307
  65.9 1.7 %collective-permute-done.19 = bf16[256,128]{1,0:T(8,128)(2,1)S(1)} collective-permute-done((bf16[256,128]{1,0:T(8,128)(2,1)S(1)}, bf16[256,128]{1,0:T(8,128)(2,1)S(1)}, u32[]{:S(2)}, u32[]{:S(2)}) %collective-permute-start.19) | collective-permute-done | bytes 65568 | tf_op jit(solution)/shard_map/ppermute | solution.py:329
  67.6 0.7 %collective-permute-done.18 = bf16[256,128]{1,0:T(8,128)(2,1)S(1)} collective-permute-done((bf16[256,128]{1,0:T(8,128)(2,1)S(1)}, bf16[256,128]{1,0:T(8,128)(2,1)S(1)}, u32[]{:S(2)}, u32[]{:S(2)}) %collective-permute-start.18) | collective-permute-done | bytes 65568 | tf_op jit(solution)/shard_map/ppermute | solution.py:329
  (42 shorter events, 5.4 us)
Async XLA Ops:
  0.6 0.8 %copy-start.5 = (bf16[128,128]{1,0:T(8,128)(2,1)S(1)}, bf16[128,128]{1,0:T(8,128)(2,1)}, u32[]{:S(2)}) copy-start(bf16[128,128]{1,0:T(8,128)(2,1)} %param.11) | copy-start | bytes 98308
  0.6 27.1 %copy-start.1 = (bf16[128,1024]{1,0:T(8,128)(2,1)S(1)}, bf16[128,1024]{1,0:T(8,128)(2,1)}, u32[]{:S(2)}) copy-start(bf16[128,1024]{1,0:T(8,128)(2,1)} %g_ref.1) | copy-start | bytes 786436
  1.5 26.3 %copy-start = (bf16[128,1024]{1,0:T(8,128)(2,1)S(1)}, bf16[128,1024]{1,0:T(8,128)(2,1)}, u32[]{:S(2)}) copy-start(bf16[128,1024]{1,0:T(8,128)(2,1)} %q_ref.1) | copy-start | bytes 786436
  1.5 5.4 %collective-permute-start = (bf16[256,128]{1,0:T(8,128)(2,1)S(1)}, bf16[256,128]{1,0:T(8,128)(2,1)S(1)}, u32[]{:S(2)}, u32[]{:S(2)}) collective-permute-start(bf16[256,128]{1,0:T(8,128)(2,1)S(1)} %get-tuple-element.33), channel_id=1, source_target_pairs={{0,4},{1,3},{2,6},{3,1},{4,0},{5,7},{6,2},{7,5},{8,12},{9,11},{10,... | collective-permute-start | bytes 196616 | tf_op jit(solution)/shard_map/ppermute | solution.py:329
  4.6 5.9 %collective-permute-start.2 = (bf16[256,128]{1,0:T(8,128)(2,1)S(1)}, bf16[256,128]{1,0:T(8,128)(2,1)S(1)}, u32[]{:S(2)}, u32[]{:S(2)}) collective-permute-start(bf16[256,128]{1,0:T(8,128)(2,1)S(1)} %get-tuple-element.33), channel_id=1, source_target_pairs={{0,20},{1,15},{2,22},{3,13},{4,16},{5,11},{6,18},{7,9},{8,28},{9,7... | collective-permute-start | bytes 196616 | tf_op jit(solution)/shard_map/ppermute | solution.py:329
  6.0 4.5 %collective-permute-start.1 = (bf16[256,128]{1,0:T(8,128)(2,1)S(1)}, bf16[256,128]{1,0:T(8,128)(2,1)S(1)}, u32[]{:S(2)}, u32[]{:S(2)}) collective-permute-start(bf16[256,128]{1,0:T(8,128)(2,1)S(1)} %get-tuple-element.33), channel_id=1, source_target_pairs={{0,16},{1,13},{2,18},{3,15},{4,20},{5,9},{6,22},{7,11},{8,24},{9,5... | collective-permute-start | bytes 196616 | tf_op jit(solution)/shard_map/ppermute | solution.py:329
  10.5 11.9 %collective-permute-start.5 = (bf16[1024,128]{1,0:T(8,128)(2,1)S(1)}, bf16[1024,128]{1,0:T(8,128)(2,1)S(1)}, u32[]{:S(2)}, u32[]{:S(2)}) collective-permute-start(bf16[1024,128]{1,0:T(8,128)(2,1)S(1)} %constant_dynamic-update-slice_fusion.2.refs_0_), channel_id=1, source_target_pairs={{0,14},{1,21},{2,12},{3,23},{4,10},{5,17},{6,8},{7,19},{8,6},{9,29... | collective-permute-start | bytes 786440 | tf_op jit(solution)/shard_map/ppermute | solution.py:329
  14.9 11.0 %collective-permute-start.4 = (bf16[1024,128]{1,0:T(8,128)(2,1)S(1)}, bf16[1024,128]{1,0:T(8,128)(2,1)S(1)}, u32[]{:S(2)}, u32[]{:S(2)}) collective-permute-start(bf16[1024,128]{1,0:T(8,128)(2,1)S(1)} %constant_dynamic-update-slice_fusion.2.refs_0_), channel_id=1, source_target_pairs={{0,12},{1,17},{2,14},{3,19},{4,8},{5,21},{6,10},{7,23},{8,4},{9,25... | collective-permute-start | bytes 786440 | tf_op jit(solution)/shard_map/ppermute | solution.py:329
  15.5 10.5 %collective-permute-start.3 = (bf16[1024,128]{1,0:T(8,128)(2,1)S(1)}, bf16[1024,128]{1,0:T(8,128)(2,1)S(1)}, u32[]{:S(2)}, u32[]{:S(2)}) collective-permute-start(bf16[1024,128]{1,0:T(8,128)(2,1)S(1)} %constant_dynamic-update-slice_fusion.2.refs_0_), channel_id=1, source_target_pairs={{0,2},{1,5},{2,0},{3,7},{4,6},{5,1},{6,4},{7,3},{8,10},{9,13},{10,... | collective-permute-start | bytes 786440 | tf_op jit(solution)/shard_map/ppermute | solution.py:329
  15.9 16.0 %collective-permute-start.6 = (bf16[1024,128]{1,0:T(8,128)(2,1)S(1)}, bf16[1024,128]{1,0:T(8,128)(2,1)S(1)}, u32[]{:S(2)}, u32[]{:S(2)}) collective-permute-start(bf16[1024,128]{1,0:T(8,128)(2,1)S(1)} %constant_dynamic-update-slice_fusion.2.refs_0_), channel_id=1, source_target_pairs={{0,1},{1,0},{2,3},{3,2},{4,5},{5,4},{6,7},{7,6},{8,9},{9,8},{10,11... | collective-permute-start | bytes 786440 | tf_op jit(solution)/shard_map/ppermute | solution.py:329
  22.5 9.4 %collective-permute-start.9 = (bf16[1024,128]{1,0:T(8,128)(2,1)S(1)}, bf16[1024,128]{1,0:T(8,128)(2,1)S(1)}, u32[]{:S(2)}, u32[]{:S(2)}) collective-permute-start(bf16[1024,128]{1,0:T(8,128)(2,1)S(1)} %collective-permute-done.5.refs_3_), channel_id=1, source_target_pairs={{0,1},{1,0},{2,3},{3,2},{4,5},{5,4},{6,7},{7,6},{8,9},{9,8},{10,11... | collective-permute-start | bytes 786440 | tf_op jit(solution)/shard_map/ppermute | solution.py:329
  25.9 6.0 %collective-permute-start.8 = (bf16[1024,128]{1,0:T(8,128)(2,1)S(1)}, bf16[1024,128]{1,0:T(8,128)(2,1)S(1)}, u32[]{:S(2)}, u32[]{:S(2)}) collective-permute-start(bf16[1024,128]{1,0:T(8,128)(2,1)S(1)} %collective-permute-done.4.refs_2_), channel_id=1, source_target_pairs={{0,1},{1,0},{2,3},{3,2},{4,5},{5,4},{6,7},{7,6},{8,9},{9,8},{10,11... | collective-permute-start | bytes 786440 | tf_op jit(solution)/shard_map/ppermute | solution.py:329
  25.9 6.0 %collective-permute-start.7 = (bf16[1024,128]{1,0:T(8,128)(2,1)S(1)}, bf16[1024,128]{1,0:T(8,128)(2,1)S(1)}, u32[]{:S(2)}, u32[]{:S(2)}) collective-permute-start(bf16[1024,128]{1,0:T(8,128)(2,1)S(1)} %collective-permute-done.3.refs_1_), channel_id=1, source_target_pairs={{0,1},{1,0},{2,3},{3,2},{4,5},{5,4},{6,7},{7,6},{8,9},{9,8},{10,11... | collective-permute-start | bytes 786440 | tf_op jit(solution)/shard_map/ppermute | solution.py:329
  28.4 0.9 %copy-start.2 = (bf16[128,1024]{1,0:T(8,128)(2,1)S(1)}, bf16[128,1024]{1,0:T(8,128)(2,1)}, u32[]{:S(2)}) copy-start(bf16[128,1024]{1,0:T(8,128)(2,1)} %o_ref.1) | copy-start | bytes 786436
  42.8 1.6 %collective-permute-start.11 = (bf16[1024,128]{1,0:T(8,128)(2,1)S(1)}, bf16[1024,128]{1,0:T(8,128)(2,1)S(1)}, u32[]{:S(2)}, u32[]{:S(2)}) collective-permute-start(bf16[1024,128]{1,0:T(8,128)(2,1)S(1)} %get-tuple-element.20), channel_id=1, source_target_pairs={{0,1},{1,0},{2,3},{3,2},{4,5},{5,4},{6,7},{7,6},{8,9},{9,8},{10,11... | collective-permute-start | bytes 786440 | tf_op jit(solution)/shard_map/ppermute | solution.py:329
  42.9 1.9 %collective-permute-start.13 = (bf16[1024,128]{1,0:T(8,128)(2,1)S(1)}, bf16[1024,128]{1,0:T(8,128)(2,1)S(1)}, u32[]{:S(2)}, u32[]{:S(2)}) collective-permute-start(bf16[1024,128]{1,0:T(8,128)(2,1)S(1)} %get-tuple-element.21), channel_id=1, source_target_pairs={{0,1},{1,0},{2,3},{3,2},{4,5},{5,4},{6,7},{7,6},{8,9},{9,8},{10,11... | collective-permute-start | bytes 786440 | tf_op jit(solution)/shard_map/ppermute | solution.py:329
  43.4 1.8 %collective-permute-start.15 = (bf16[1024,128]{1,0:T(8,128)(2,1)S(1)}, bf16[1024,128]{1,0:T(8,128)(2,1)S(1)}, u32[]{:S(2)}, u32[]{:S(2)}) collective-permute-start(bf16[1024,128]{1,0:T(8,128)(2,1)S(1)} %get-tuple-element.22), channel_id=1, source_target_pairs={{0,1},{1,0},{2,3},{3,2},{4,5},{5,4},{6,7},{7,6},{8,9},{9,8},{10,11... | collective-permute-start | bytes 786440 | tf_op jit(solution)/shard_map/ppermute | solution.py:329
  43.4 7.3 %collective-permute-start.10 = (bf16[1024,128]{1,0:T(8,128)(2,1)S(1)}, bf16[1024,128]{1,0:T(8,128)(2,1)S(1)}, u32[]{:S(2)}, u32[]{:S(2)}) collective-permute-start(bf16[1024,128]{1,0:T(8,128)(2,1)S(1)} %get-tuple-element.19), channel_id=1, source_target_pairs={{0,1},{1,0},{2,3},{3,2},{4,5},{5,4},{6,7},{7,6},{8,9},{9,8},{10,11... | collective-permute-start | bytes 786440 | tf_op jit(solution)/shard_map/ppermute | solution.py:329
  45.3 6.4 %collective-permute-start.12 = (bf16[1024,128]{1,0:T(8,128)(2,1)S(1)}, bf16[1024,128]{1,0:T(8,128)(2,1)S(1)}, u32[]{:S(2)}, u32[]{:S(2)}) collective-permute-start(bf16[1024,128]{1,0:T(8,128)(2,1)S(1)} %get-tuple-element.25), channel_id=1, source_target_pairs={{0,2},{1,5},{2,0},{3,7},{4,6},{5,1},{6,4},{7,3},{8,10},{9,13},{10,... | collective-permute-start | bytes 786440 | tf_op jit(solution)/shard_map/ppermute | solution.py:329
  46.5 11.8 %collective-permute-start.16 = (bf16[1024,128]{1,0:T(8,128)(2,1)S(1)}, bf16[1024,128]{1,0:T(8,128)(2,1)S(1)}, u32[]{:S(2)}, u32[]{:S(2)}) collective-permute-start(bf16[1024,128]{1,0:T(8,128)(2,1)S(1)} %get-tuple-element.26), channel_id=1, source_target_pairs={{0,14},{1,21},{2,12},{3,23},{4,10},{5,17},{6,8},{7,19},{8,6},{9,29... | collective-permute-start | bytes 786440 | tf_op jit(solution)/shard_map/ppermute | solution.py:329
  48.5 12.8 %collective-permute-start.14 = (bf16[1024,128]{1,0:T(8,128)(2,1)S(1)}, bf16[1024,128]{1,0:T(8,128)(2,1)S(1)}, u32[]{:S(2)}, u32[]{:S(2)}) collective-permute-start(bf16[1024,128]{1,0:T(8,128)(2,1)S(1)} %get-tuple-element.27), channel_id=1, source_target_pairs={{0,12},{1,17},{2,14},{3,19},{4,8},{5,21},{6,10},{7,23},{8,4},{9,25... | collective-permute-start | bytes 786440 | tf_op jit(solution)/shard_map/ppermute | solution.py:329
  61.4 4.5 %collective-permute-start.17 = (bf16[256,128]{1,0:T(8,128)(2,1)S(1)}, bf16[256,128]{1,0:T(8,128)(2,1)S(1)}, u32[]{:S(2)}, u32[]{:S(2)}) collective-permute-start(bf16[256,128]{1,0:T(8,128)(2,1)S(1)} %get-tuple-element.28), channel_id=1, source_target_pairs={{0,4},{1,3},{2,6},{3,1},{4,0},{5,7},{6,2},{7,5},{8,12},{9,11},{10,... | collective-permute-start | bytes 196616 | tf_op jit(solution)/shard_map/ppermute | solution.py:329
  62.4 5.2 %collective-permute-start.19 = (bf16[256,128]{1,0:T(8,128)(2,1)S(1)}, bf16[256,128]{1,0:T(8,128)(2,1)S(1)}, u32[]{:S(2)}, u32[]{:S(2)}) collective-permute-start(bf16[256,128]{1,0:T(8,128)(2,1)S(1)} %get-tuple-element.29), channel_id=1, source_target_pairs={{0,20},{1,15},{2,22},{3,13},{4,16},{5,11},{6,18},{7,9},{8,28},{9,7... | collective-permute-start | bytes 196616 | tf_op jit(solution)/shard_map/ppermute | solution.py:329
  63.9 4.4 %collective-permute-start.18 = (bf16[256,128]{1,0:T(8,128)(2,1)S(1)}, bf16[256,128]{1,0:T(8,128)(2,1)S(1)}, u32[]{:S(2)}, u32[]{:S(2)}) collective-permute-start(bf16[256,128]{1,0:T(8,128)(2,1)S(1)} %get-tuple-element.30), channel_id=1, source_target_pairs={{0,16},{1,13},{2,18},{3,15},{4,20},{5,9},{6,22},{7,11},{8,24},{9,5... | collective-permute-start | bytes 196616 | tf_op jit(solution)/shard_map/ppermute | solution.py:329
  (2 other events, 1.3 us)

commit v3 on v2

v3 whole, which is shorter than its diff:
```python
import functools
import math

import jax
import jax.numpy as jnp
from jax import lax
from jax.experimental import pallas as pl
from jax.experimental.pallas import tpu as pltpu
from jax.sharding import PartitionSpec as P

STRIPE = 128
PAIR = 2 * STRIPE
AXES = ("row", "col")
neg_big = -1e30
far_blocks = 1 << 22
head_len = 3
keep_bytes = 24 << 20


class Layout:
    def __init__(self, rows, cols):
        self.rows, self.cols = rows, cols
        self.near, self.far = rows * 2, cols // 4
        self.square = self.near == self.far
        self.count = rows * cols

    def split(self, row, col):
        ring = col // 4
        half = ring // 2
        return row * 2 + (ring + half) % 2, half * 2 + (col // 2) % 2, col % 2

    def join(self, near, far, core):
        half = far // 2
        ring = half * 2 + (near + half) % 2
        return (near // 2) * self.cols + ring * 4 + (far % 2) * 2 + core

    def hop(self, first=0, second=0, core_flip=0):
        pairs = []
        for device in range(self.count):
            near, far, core = self.split(device // self.cols, device % self.cols)
            if self.square and core == 1:
                near, far = near ^ second, far ^ first
            else:
                near, far = near ^ first, far ^ second
            pairs.append((device, self.join(near, far, core ^ core_flip)))
        return pairs

    def slot(self, own, stored):
        near, far, core = self.split(stored % self.rows, stored // self.rows)
        near, far = near ^ own[0], far ^ own[1]
        place = far * self.near + near
        if self.square:
            place = jnp.where(core == 1, near * self.far + far, place)
        return place + jnp.where(core == own[2], 0, self.count // 2)

    def early(self, slot):
        return slot % (self.count // 2) >= self.count // 4


def dot(left, right, left_dim, right_dim):
    return lax.dot_general(
        left, right, (((left_dim,), (right_dim,)), ((), ())), preferred_element_type=jnp.float32
    )


def prepare(
    layout, heads, here, order, window, q_ref, e_ref, g_ref, o_ref, q_out, g_out, d_out, meta
):
    row, col = here[0], here[1]
    own = layout.split(row, col)
    own_block = order[row * layout.cols + col]
    live = jnp.minimum(own_block, (window[0] + STRIPE - 2) // STRIPE) + 1
    part_len = layout.count + 2

    def write(part, place, slot, back):
        start = head_len + part * part_len + 2 * place
        meta[start] = slot
        meta[start + 1] = back

    def visit(stored, filled):
        back = own_block - order[stored]
        slot = layout.slot(own, stored)
        early = layout.early(slot)
        wanted = (back >= 0) & (back < live)

        @pl.when(wanted)
        def _():
            write(jnp.where(early, 0, 1), jnp.where(early, filled[0], filled[1]), slot, back)

        return (
            filled[0] + (wanted & early).astype(jnp.int32),
            filled[1] + (wanted & jnp.logical_not(early)).astype(jnp.int32),
        )

    filled = lax.fori_loop(0, layout.count, visit, (jnp.int32(0), jnp.int32(0)))
    turns = [(count + 1) // 2 for count in filled]
    for part, count in enumerate(filled):
        write(part, count, layout.count, far_blocks)
    meta[0] = turns[0]
    meta[1] = turns[0] + turns[1]
    meta[2] = window[0]
    power = jnp.left_shift(1, e_ref[...] + 1).astype(jnp.float32) * 0.5
    power = jnp.broadcast_to(power, (STRIPE, STRIPE)).T
    for head in range(heads):
        cols = pl.ds(head * STRIPE, STRIPE)
        q_out[cols] = (q_ref[:, cols].astype(jnp.float32) * power).astype(jnp.bfloat16)
        grads = g_ref[:, cols]
        g_out[cols] = grads
        product = grads.astype(jnp.float32) * o_ref[:, cols].astype(jnp.float32)
        sums = jnp.sum(product.T, axis=0, keepdims=True)
        d_out[:, cols] = sums.astype(jnp.bfloat16).astype(jnp.float32)


def blocks_of(meta, turn):
    part_len = (meta.shape[0] - head_len) // 2
    early = meta[0]
    start = head_len + jnp.where(turn < early, 4 * turn, part_len + 4 * (turn - early))
    return [meta[start], meta[start + 2]], [meta[start + 1], meta[start + 3]]


def rows_at(meta, kv, turn, shift):
    slots, _ = blocks_of(meta, turn)
    return jnp.concatenate(
        [kv[pl.ds(pl.multiple_of(slot * PAIR, PAIR) + shift, STRIPE)] for slot in slots], 0
    )


def visible_at(meta, turn):
    relative = lax.broadcasted_iota(jnp.int32, (STRIPE, STRIPE), 1) - lax.broadcasted_iota(
        jnp.int32, (STRIPE, STRIPE), 0
    )
    _, backs = blocks_of(meta, turn)
    distances = [relative + back * STRIPE for back in backs]
    return jnp.concatenate([(d >= 0) & (d < meta[2]) for d in distances], 0)


def groups_of(heads):
    group = 2 if heads % 2 == 0 else 1
    wide = group * STRIPE
    return group, [pl.ds(i * wide, wide) for i in range(heads // group)]


def masked_scores(meta, q_ref, kv, turn, cols, group):
    scores = dot(rows_at(meta, kv, turn, 0), q_ref[cols], 1, 1)
    visible = jnp.concatenate([visible_at(meta, turn)] * group, 1)
    return jnp.where(visible, scores, neg_big)


def by_eight(value):
    return value.reshape(-1, 8, value.shape[1])


def find_weights(heads, keep, to_log2, meta, q_ref, kv, probs, run_max, run_sum, top, inverse):
    group, groups = groups_of(heads)
    turns, window_len = meta[1], meta[2]
    run_max[...] = jnp.full_like(run_max, neg_big)
    run_sum[...] = jnp.zeros_like(run_sum)

    def find_max(turn, masked):
        key_rows = rows_at(meta, kv, turn, 0)
        if masked:
            visible = jnp.concatenate([visible_at(meta, turn)] * group, 1)
        for cols in groups:
            scores = dot(key_rows, q_ref[cols], 1, 1)
            if masked:
                scores = jnp.where(visible, scores, neg_big)
            run_max[:, cols] = jnp.maximum(run_max[:, cols], jnp.max(by_eight(scores), axis=0))
            if keep:
                probs[turn, :, cols] = scores

    def add_max(turn, carry):
        _, backs = blocks_of(meta, turn)
        nearest, farthest = jnp.minimum(*backs), jnp.maximum(*backs)
        whole = (nearest >= 1) & (farthest * STRIPE + (STRIPE - 1) < window_len)

        @pl.when(whole)
        def _():
            find_max(turn, False)

        @pl.when(jnp.logical_not(whole))
        def _():
            find_max(turn, True)

        return carry

    lax.fori_loop(0, turns, add_max, 0)
    top[...] = jnp.max(run_max[...], axis=0, keepdims=True) * to_log2

    def add_sums(turn, carry):
        for cols in groups:
            if keep:
                scores = probs[turn, :, cols]
            else:
                scores = masked_scores(meta, q_ref, kv, turn, cols, group)
            part = jnp.exp2(scores * to_log2 - top[:, cols])
            run_sum[:, cols] += jnp.sum(by_eight(part), axis=0)
            if keep:
                probs[turn, :, cols] = part
        return carry

    lax.fori_loop(0, turns, add_sums, 0)
    inverse[...] = 1.0 / jnp.sum(run_sum[...], axis=0, keepdims=True)


def add_gradients(
    heads, keep, inv_scale, meta, begin, end,
    q_ref, g_ref, delta_ref, kv, probs, top, inverse, dq_ref, outs, buffers,
):
    group, groups = groups_of(heads)
    to_log2 = inv_scale * math.log2(math.e)

    def find_grads(turn, weight_buf, grad_buf):
        value_rows = rows_at(meta, kv, turn, STRIPE)
        for cols in groups:
            if keep:
                part = probs[turn, :, cols]
            else:
                scores = masked_scores(meta, q_ref, kv, turn, cols, group)
                part = jnp.exp2(scores * to_log2 - top[:, cols])
            weights = part * inverse[:, cols]
            weight_grad = dot(value_rows, g_ref[cols], 1, 1)
            score_grad = weights * (weight_grad - delta_ref[:, cols])
            weight_buf[:, cols] = weights.astype(jnp.bfloat16)
            grad_buf[:, cols] = score_grad.astype(jnp.bfloat16)

    def products(turn, weight_buf, grad_buf):
        score_grads = grad_buf[...]
        dq_ref[...] += dot(rows_at(meta, kv, turn, 0), score_grads, 0, 0)
        key_part = (dot(score_grads, q_ref[...], 1, 0) * inv_scale).astype(jnp.bfloat16)
        value_part = dot(weight_buf[...], g_ref[...], 1, 0).astype(jnp.bfloat16)
        return key_part, value_part

    def store(turn, parts):
        slots, _ = blocks_of(meta, turn)
        for i, slot in enumerate(slots):
            rows = slice(i * STRIPE, (i + 1) * STRIPE)
            for start, ref in outs:

                @pl.when((slot >= start) & (slot < start + ref.shape[0] // PAIR))
                def _(start=start, ref=ref):
                    inner = pl.multiple_of((slot - start) * PAIR, PAIR)
                    for j, part in enumerate(parts):
                        ref[pl.ds(inner + j * STRIPE, STRIPE)] = part[rows]

    for _, ref in outs:
        ref[...] = jnp.zeros_like(ref)
    weight_a, weight_b, grad_a, grad_b = buffers
    a, b = (weight_a, grad_a), (weight_b, grad_b)
    last = end - 1
    pairs = jnp.maximum(last - begin, 0) // 2

    def step(turn, now, before):
        parts = products(turn - 1, *before)
        find_grads(turn, *now)
        store(turn - 1, parts)

    def two_steps(pair, carry):
        turn = begin + 2 * pair
        step(turn + 1, b, a)
        step(turn + 2, a, b)
        return carry

    @pl.when(end > begin)
    def _():
        find_grads(begin, *a)
        lax.fori_loop(0, pairs, two_steps, 0)

    @pl.when((end > begin) & ((end - begin) % 2 == 0))
    def _():
        step(last, b, a)
        store(last, products(last, *b))

    @pl.when((end > begin) & ((end - begin) % 2 == 1))
    def _():
        store(last, products(last, *a))


def spans_of(stripes, pieces, refs, first_piece):
    length = stripes // 2 // pieces
    half = len(refs) // 2
    own = [((first_piece + i) * length, ref) for i, ref in enumerate(refs[:half])]
    other = [
        (stripes // 2 + (first_piece + i) * length, ref) for i, ref in enumerate(refs[half:])
    ]
    return own + other


def attend_early(stripes, pieces, heads, keep, inv_scale, meta, q_ref, g_ref, delta_ref, *refs):
    held, rest = refs[: 2 * pieces], refs[2 * pieces :]
    kv, probs, top, inverse, dq_ref, rest = *rest[:5], rest[5:]
    outs, rest = rest[:pieces], rest[pieces:]
    run_max, run_sum, *buffers = rest
    rows = held[0].shape[0]
    for i, piece in enumerate(held):
        kv[pl.ds(i * rows, rows)] = piece[...]
    kv[pl.ds(len(held) * rows, PAIR)] = jnp.zeros((PAIR, STRIPE), kv.dtype)
    dq_ref[...] = jnp.zeros_like(dq_ref)
    to_log2 = inv_scale * math.log2(math.e)
    find_weights(heads, keep, to_log2, meta, q_ref, kv, probs, run_max, run_sum, top, inverse)
    add_gradients(
        heads, keep, inv_scale, meta, 0, meta[0],
        q_ref, g_ref, delta_ref, kv, probs, top, inverse, dq_ref,
        spans_of(stripes, pieces, outs, pieces // 2), buffers,
    )


def attend_late(
    stripes, pieces, heads, keep, inv_scale,
    meta, q_ref, g_ref, delta_ref, kv, probs, top, inverse, dq_early, dq_ref, *refs,
):
    outs, buffers = refs[:pieces], refs[pieces:]
    dq_ref[...] = dq_early[...]
    add_gradients(
        heads, keep, inv_scale, meta, meta[0], meta[1],
        q_ref, g_ref, delta_ref, kv, probs, top, inverse, dq_ref,
        spans_of(stripes, pieces, outs, 0), buffers,
    )


def turn_queries(heads, inv_scale, turned, out):
    for head in range(heads):
        cols = pl.ds(head * STRIPE, STRIPE)
        out[:, cols] = (turned[:, cols].T * inv_scale).astype(jnp.bfloat16)


def vmem_limit(nbytes):
    return pltpu.CompilerParams(vmem_limit_bytes=nbytes)


vmem_spec = pl.BlockSpec(memory_space=pltpu.VMEM)
smem_spec = pl.BlockSpec(memory_space=pltpu.SMEM)


def run_prepare(layout, heads, here, order, window, queries, exps, grads, outs):
    flat = jax.ShapeDtypeStruct((heads * STRIPE, STRIPE), jnp.bfloat16)
    return pl.pallas_call(
        functools.partial(prepare, layout, heads),
        out_shape=[
            flat,
            flat,
            jax.ShapeDtypeStruct((1, heads * STRIPE), jnp.float32),
            jax.ShapeDtypeStruct((head_len + 2 * (layout.count + 2),), jnp.int32),
        ],
        in_specs=[smem_spec] * 3 + [vmem_spec] * 4,
        out_specs=[vmem_spec] * 3 + [smem_spec],
        compiler_params=vmem_limit(24 * STRIPE * heads * STRIPE * 2),
        name="prep",
    )(here, order, window, queries, exps, grads, outs)


def run_attend(early, meta, q_flat, g_flat, delta, others, pieces, stripes, heads, inv_scale):
    wide = q_flat.shape[0]
    turns = stripes // 2 + 2
    keep = turns * PAIR * wide * 4 <= keep_bytes
    half_rows = stripes // 2 * PAIR
    query_sum = jax.ShapeDtypeStruct((STRIPE, wide), jnp.float32)
    row = jax.ShapeDtypeStruct((1, wide), jnp.float32)
    outs = [query_sum] + [
        jax.ShapeDtypeStruct((half_rows // pieces, STRIPE), jnp.bfloat16)
    ] * pieces
    scratch = [pltpu.VMEM((PAIR, wide), jnp.bfloat16)] * 4
    if early:
        outs = [
            jax.ShapeDtypeStruct((2 * half_rows + PAIR, STRIPE), jnp.bfloat16),
            jax.ShapeDtypeStruct((turns if keep else 1, PAIR, wide), jnp.float32),
            row,
            row,
        ] + outs
        scratch = [pltpu.VMEM((8, wide), jnp.float32)] * 2 + scratch
    body = attend_early if early else attend_late
    return pl.pallas_call(
        functools.partial(body, stripes, pieces, heads, keep, inv_scale),
        out_shape=outs,
        in_specs=[smem_spec] + [vmem_spec] * (3 + len(others)),
        out_specs=[vmem_spec] * len(outs),
        scratch_shapes=scratch,
        compiler_params=vmem_limit(13 * half_rows * STRIPE + 12 * PAIR * wide * 2),
        name="early" if early else "late",
    )(meta, q_flat, g_flat, delta, *others)


def run_turn(turned, heads, inv_scale):
    return pl.pallas_call(
        functools.partial(turn_queries, heads, inv_scale),
        out_shape=jax.ShapeDtypeStruct(turned.shape, jnp.bfloat16),
        in_specs=[vmem_spec],
        out_specs=vmem_spec,
        compiler_params=vmem_limit(24 * STRIPE * heads * STRIPE * 2),
        name="turn",
    )(turned)


def per_device(
    layout,
    queries, query_exps, key_head, value_head, forward_out, output_grad, stripe_order, window_size
):
    head_dim = key_head.shape[1]
    tokens, feat_width = queries.shape
    heads = feat_width // head_dim
    inv_scale = 1.0 / math.sqrt(head_dim)
    stripes = layout.count
    row, col = lax.axis_index("row"), lax.axis_index("col")

    def send(value, **where):
        return lax.ppermute(value, AXES, layout.hop(**where))

    def widen(value):
        return value.astype(jnp.float32)

    pair = jnp.concatenate([key_head, value_head], 0)
    stage = [pair] + [send(pair, first=i) for i in range(1, layout.near)]
    plane = jnp.concatenate(stage, 0)
    own_pieces = [plane] + [send(plane, second=j) for j in range(1, layout.far)]
    other_pieces = [send(piece, core_flip=1) for piece in own_pieces]

    here = jnp.stack([row, col]).astype(jnp.int32)
    q_flat, g_flat, delta, meta = run_prepare(
        layout, heads, here, stripe_order, window_size,
        queries, query_exps.reshape(1, -1), output_grad, forward_out,
    )
    pieces = layout.far
    split = pieces // 2
    results = run_attend(
        True, meta, q_flat, g_flat, delta, own_pieces + other_pieces,
        pieces, stripes, heads, inv_scale,
    )
    between, early_parts = results[:5], results[5:]
    results = run_attend(
        False, meta, q_flat, g_flat, delta, between, pieces, stripes, heads, inv_scale
    )
    turned, late_parts = results[0], results[1:]
    query_grad = run_turn(turned, heads, inv_scale)

    own_parts = late_parts[:split] + early_parts[:split]
    other_parts = late_parts[split:] + early_parts[split:]
    summed = [None] * pieces
    for j in reversed(range(pieces)):
        arrived = send(other_parts[j], core_flip=1)
        summed[j] = widen(own_parts[j]) + widen(arrived)
    plane_sum = summed[0]
    for j in range(1, pieces):
        plane_sum = plane_sum + widen(send(summed[j].astype(jnp.bfloat16), second=j))
    pair_sum = plane_sum[:PAIR]
    for i in range(1, layout.near):
        part = plane_sum[i * PAIR : (i + 1) * PAIR].astype(jnp.bfloat16)
        pair_sum = pair_sum + widen(send(part, first=i))
    pair_sum = pair_sum.astype(jnp.bfloat16)
    return (query_grad, pair_sum[:tokens], pair_sum[tokens:])


def solution(mesh):
    layout = Layout(mesh.shape["row"], mesh.shape["col"])

    def whole(*arrays):
        return per_device(layout, *arrays)

    return jax.shard_map(
        whole,
        mesh=mesh,
        in_specs=(
            P(("row", "col"), None),
            P(("row", "col")),
            P(("col", "row"), None),
            P(("col", "row"), None),
            P(("row", "col"), None),
            P(("row", "col"), None),
            P(),
            P(),
        ),
        out_specs=(P(("row", "col"), None), P(("col", "row"), None), P(("col", "row"), None)),
        check_vma=False,
    )
```

time: 69.2 us -> 73.3 us (1.059)
  local copies, waits for them, and re-layouts: 3.14 us -> 6.39 us
  Pallas kernels: 14.2 us -> 15.4 us
    unnamed x15 -> x13, local copies, waits for them, and re-layouts: 2.46 us -> 4.95 us
    pallas_call x1 -> x2, Pallas kernels: 10.8 us -> 11.8 us  [run_attend(): pl.pallas_call(functools.partial(body, stripes, pieces, heads, keep, inv_...]
    concatenate x1, local copies, waits for them, and re-layouts: 0.02 us -> 0.78 us  [per_device(): pair = jnp.concatenate([key_head, value_head], 0)]
  transfers between devices with their start and end apart: 20 -> 20, of which waited for: 12 -> 10; matrix products, arithmetic and copies ran while one was open for 0% -> 0% of each run, Pallas kernels for 5% -> 5%
where the time goes in v3:
time: 73.3 us; the launch traced here: 72.9 us
  waiting for transfers between devices  28 us (38%)
  starting transfers between devices  21.2 us (29%)
  Pallas kernels  15.4 us (21%)
  local copies, waits for them, and re-layouts  6.39 us (9%)
  between operations  1.41 us (2%)
    ppermute x20, waiting for transfers between devices, send(): return lax.ppermute(value, AXES, layout.hop(**where))  28 us
    ppermute x20, starting transfers between devices, send(): return lax.ppermute(value, AXES, layout.hop(**where))  21.2 us
    pallas_call x2, Pallas kernels, run_attend(): pl.pallas_call(functools.partial(body, stripes, pieces, heads, keep, inv_...  11.8 us
    unnamed x13, local copies, waits for them, and re-layouts  4.95 us
    pallas_call x1, Pallas kernels, run_prepare(): pl.pallas_call(functools.partial(prepare, layout, heads), out_shape=[flat...  2.67 us
  transfers between devices with their start and end apart: 20, of which 10 were waited for; matrix products, arithmetic and copies ran while one was open for 0% of the time, Pallas kernels for 5%

profile of v3, /device:TPU:0, one launch (start us, length us, event | category | flops | bytes accessed | tf_op | source)
XLA Modules:
  0.0 72.9 jit_solution(13074450478349075732)
XLA Ops:
  2.2 3.1 %collective-permute-start = (bf16[256,128]{1,0:T(8,128)(2,1)S(1)}, bf16[256,128]{1,0:T(8,128)(2,1)S(1)}, u32[]{:S(2)}, u32[]{:S(2)}) collective-permute-start(bf16[256,128]{1,0:T(8,128)(2,1)S(1)} %get-tuple-element.46), channel_id=1, source_target_pairs={{0,4},{1,3},{2,6},{3,1},{4,0},{5,7},{6,2},{7,5},{8,12},{9,11},{10,... | collective-permute-start | bytes 196616 | tf_op jit(solution)/shard_map/ppermute | solution.py:405
  5.3 1.4 %collective-permute-start.2 = (bf16[256,128]{1,0:T(8,128)(2,1)S(1)}, bf16[256,128]{1,0:T(8,128)(2,1)S(1)}, u32[]{:S(2)}, u32[]{:S(2)}) collective-permute-start(bf16[256,128]{1,0:T(8,128)(2,1)S(1)} %get-tuple-element.46), channel_id=1, source_target_pairs={{0,20},{1,15},{2,22},{3,13},{4,16},{5,11},{6,18},{7,9},{8,28},{9,7... | collective-permute-start | bytes 196616 | tf_op jit(solution)/shard_map/ppermute | solution.py:405
  7.6 3.6 %collective-permute-done.1 = bf16[256,128]{1,0:T(8,128)(2,1)S(1)} collective-permute-done((bf16[256,128]{1,0:T(8,128)(2,1)S(1)}, bf16[256,128]{1,0:T(8,128)(2,1)S(1)}, u32[]{:S(2)}, u32[]{:S(2)}) %collective-permute-start.1) | collective-permute-done | bytes 65568 | tf_op jit(solution)/shard_map/ppermute | solution.py:405
  11.2 4.4 %collective-permute-start.5 = (bf16[1024,128]{1,0:T(8,128)(2,1)S(1)}, bf16[1024,128]{1,0:T(8,128)(2,1)S(1)}, u32[]{:S(2)}, u32[]{:S(2)}) collective-permute-start(bf16[1024,128]{1,0:T(8,128)(2,1)S(1)} %constant_dynamic-update-slice_fusion.2.refs_0_), channel_id=1, source_target_pairs={{0,14},{1,21},{2,12},{3,23},{4,10},{5,17},{6,8},{7,19},{8,6},{9,29... | collective-permute-start | bytes 786440 | tf_op jit(solution)/shard_map/ppermute | solution.py:405
  16.6 6.6 %collective-permute-done.5.refs_3_ = bf16[1024,128]{1,0:T(8,128)(2,1)S(1)} collective-permute-done((bf16[1024,128]{1,0:T(8,128)(2,1)S(1)}, bf16[1024,128]{1,0:T(8,128)(2,1)S(1)}, u32[]{:S(2)}, u32[]{:S(2)}) %collective-permute-start.5) | collective-permute-done | bytes 262176 | tf_op jit(solution)/shard_map/ppermute | solution.py:405
  23.2 3.4 %collective-permute-done.4.refs_2_ = bf16[1024,128]{1,0:T(8,128)(2,1)S(1)} collective-permute-done((bf16[1024,128]{1,0:T(8,128)(2,1)S(1)}, bf16[1024,128]{1,0:T(8,128)(2,1)S(1)}, u32[]{:S(2)}, u32[]{:S(2)}) %collective-permute-start.4) | collective-permute-done | bytes 262176 | tf_op jit(solution)/shard_map/ppermute | solution.py:405
  26.6 1.1 %collective-permute-start.7 = (bf16[1024,128]{1,0:T(8,128)(2,1)S(1)}, bf16[1024,128]{1,0:T(8,128)(2,1)S(1)}, u32[]{:S(2)}, u32[]{:S(2)}) collective-permute-start(bf16[1024,128]{1,0:T(8,128)(2,1)S(1)} %collective-permute-done.3.refs_1_), channel_id=1, source_target_pairs={{0,1},{1,0},{2,3},{3,2},{4,5},{5,4},{6,7},{7,6},{8,9},{9,8},{10,11... | collective-permute-start | bytes 786440 | tf_op jit(solution)/shard_map/ppermute | solution.py:405
  28.4 0.9 %copy-done = bf16[128,1024]{1,0:T(8,128)(2,1)S(1)} copy-done((bf16[128,1024]{1,0:T(8,128)(2,1)S(1)}, bf16[128,1024]{1,0:T(8,128)(2,1)}, u32[]{:S(2)}) %copy-start) | copy-done | bytes 262168
  29.4 0.9 %copy-done.1 = bf16[128,1024]{1,0:T(8,128)(2,1)S(1)} copy-done((bf16[128,1024]{1,0:T(8,128)(2,1)S(1)}, bf16[128,1024]{1,0:T(8,128)(2,1)}, u32[]{:S(2)}) %copy-start.1) | copy-done | bytes 262168
  30.3 0.9 %copy-done.2 = bf16[128,1024]{1,0:T(8,128)(2,1)S(1)} copy-done((bf16[128,1024]{1,0:T(8,128)(2,1)S(1)}, bf16[128,1024]{1,0:T(8,128)(2,1)}, u32[]{:S(2)}) %copy-start.2) | copy-done | bytes 262168
  32.6 2.7 %prep.1 = (bf16[1024,128]{1,0:T(8,128)(2,1)S(1)}, bf16[1024,128]{1,0:T(8,128)(2,1)S(1)}, f32[1,1024]{1,0:T(1,128)S(1)}, s32[71]{0:T(128)S(1)}) custom-call(s32[2]{0:T(128)S(1)} %pad_add_fusion.here, s32[32]{0:T(128)S(1)} %copy-done.3, s32[1]{0:T(128)S(6)} %copy.16.window, bf16[128,1024]{1,0:T(8,128)(2,1)S(1)} %copy-done, s32[1,128]{1,0:T(1,128)S(1)} %bitcast.3, ...), custom_call_target="tpu_custom_call" | custom-call | tf_op jit(solution)/shard_map/prep/pallas_call | solution.py:336
  35.3 7.9 %early.1 = (bf16[8448,128]{1,0:T(8,128)(2,1)S(1)}, f32[18,256,1024]{2,1,0:T(8,128)S(1)}, f32[1,1024]{1,0:T(1,128)S(1)}, f32[1,1024]{1,0:T(1,128)S(1)}, f32[128,1...) custom-call(s32[71]{0:T(128)S(1)} %get-tuple-element.21.meta, ...), custom_call_target="tpu_custom_call" | custom-call | tf_op jit(solution)/shard_map/early/pallas_call | solution.py:371
  43.3 3.8 %late.1 = (f32[128,1024]{1,0:T(8,128)S(1)}, bf16[1024,128]{1,0:T(8,128)(2,1)S(1)}, bf16[1024,128]{1,0:T(8,128)(2,1)S(1)}, bf16[1024,128]{1,0:T(8,128)(2,1)S(1)}, bf16[1024,128]{1,0:T(8,128)(2,1)S(1)}) custom-call(s32[71]{0:T(128)S(1)} %get-tuple-element.21.meta, bf16[1024,128]{1,0:T(8,128)(2,1)S(1)} %get-tuple-element.22.q_ref, ...), custom_call_target="tpu_custom_call" | custom-call | tf_op jit(solution)/shard_map/late/pallas_call | solution.py:371
  48.8 1.2 %collective-permute-start.12 = (bf16[1024,128]{1,0:T(8,128)(2,1)S(1)}, bf16[1024,128]{1,0:T(8,128)(2,1)S(1)}, u32[]{:S(2)}, u32[]{:S(2)}) collective-permute-start(bf16[1024,128]{1,0:T(8,128)(2,1)S(1)} %add_convert_fusion.2), channel_id=1, source_target_pairs={{0,2},{1,5},{2,0},{3,7},{4,6},{5,1},{6,4},{7,3},{8,10},{9,13},{10,... | collective-permute-start | bytes 786440 | tf_op jit(solution)/shard_map/ppermute | solution.py:405
  50.1 2.1 %collective-permute-start.14 = (bf16[1024,128]{1,0:T(8,128)(2,1)S(1)}, bf16[1024,128]{1,0:T(8,128)(2,1)S(1)}, u32[]{:S(2)}, u32[]{:S(2)}) collective-permute-start(bf16[1024,128]{1,0:T(8,128)(2,1)S(1)} %add_convert_fusion.1), channel_id=1, source_target_pairs={{0,12},{1,17},{2,14},{3,19},{4,8},{5,21},{6,10},{7,23},{8,4},{9,25... | collective-permute-start | bytes 786440 | tf_op jit(solution)/shard_map/ppermute | solution.py:405
  52.2 2.2 %collective-permute-start.16 = (bf16[1024,128]{1,0:T(8,128)(2,1)S(1)}, bf16[1024,128]{1,0:T(8,128)(2,1)S(1)}, u32[]{:S(2)}, u32[]{:S(2)}) collective-permute-start(bf16[1024,128]{1,0:T(8,128)(2,1)S(1)} %add_convert_fusion), channel_id=1, source_target_pairs={{0,14},{1,21},{2,12},{3,23},{4,10},{5,17},{6,8},{7,19},{8,6},{9,29... | collective-permute-start | bytes 786440 | tf_op jit(solution)/shard_map/ppermute | solution.py:405
  54.4 0.8 %collective-permute-done.12 = bf16[1024,128]{1,0:T(8,128)(2,1)S(1)} collective-permute-done((bf16[1024,128]{1,0:T(8,128)(2,1)S(1)}, bf16[1024,128]{1,0:T(8,128)(2,1)S(1)}, u32[]{:S(2)}, u32[]{:S(2)}) %collective-permute-start.12) | collective-permute-done | bytes 262176 | tf_op jit(solution)/shard_map/ppermute | solution.py:405
  55.2 5.9 %collective-permute-done.14 = bf16[1024,128]{1,0:T(8,128)(2,1)S(1)} collective-permute-done((bf16[1024,128]{1,0:T(8,128)(2,1)S(1)}, bf16[1024,128]{1,0:T(8,128)(2,1)S(1)}, u32[]{:S(2)}, u32[]{:S(2)}) %collective-permute-start.14) | collective-permute-done | bytes 262176 | tf_op jit(solution)/shard_map/ppermute | solution.py:405
  61.1 3.6 %collective-permute-done.16 = bf16[1024,128]{1,0:T(8,128)(2,1)S(1)} collective-permute-done((bf16[1024,128]{1,0:T(8,128)(2,1)S(1)}, bf16[1024,128]{1,0:T(8,128)(2,1)S(1)}, u32[]{:S(2)}, u32[]{:S(2)}) %collective-permute-start.16) | collective-permute-done | bytes 262176 | tf_op jit(solution)/shard_map/ppermute | solution.py:405
  64.9 1.6 %collective-permute-start.17 = (bf16[256,128]{1,0:T(8,128)(2,1)S(1)}, bf16[256,128]{1,0:T(8,128)(2,1)S(1)}, u32[]{:S(2)}, u32[]{:S(2)}) collective-permute-start(bf16[256,128]{1,0:T(8,128)(2,1)S(1)} %get-tuple-element.41), channel_id=1, source_target_pairs={{0,4},{1,3},{2,6},{3,1},{4,0},{5,7},{6,2},{7,5},{8,12},{9,11},{10,... | collective-permute-start | bytes 196616 | tf_op jit(solution)/shard_map/ppermute | solution.py:405
  66.5 0.8 %collective-permute-start.19 = (bf16[256,128]{1,0:T(8,128)(2,1)S(1)}, bf16[256,128]{1,0:T(8,128)(2,1)S(1)}, u32[]{:S(2)}, u32[]{:S(2)}) collective-permute-start(bf16[256,128]{1,0:T(8,128)(2,1)S(1)} %get-tuple-element.42), channel_id=1, source_target_pairs={{0,20},{1,15},{2,22},{3,13},{4,16},{5,11},{6,18},{7,9},{8,28},{9,7... | collective-permute-start | bytes 196616 | tf_op jit(solution)/shard_map/ppermute | solution.py:405
  67.3 1.2 %collective-permute-start.18 = (bf16[256,128]{1,0:T(8,128)(2,1)S(1)}, bf16[256,128]{1,0:T(8,128)(2,1)S(1)}, u32[]{:S(2)}, u32[]{:S(2)}) collective-permute-start(bf16[256,128]{1,0:T(8,128)(2,1)S(1)} %get-tuple-element.43), channel_id=1, source_target_pairs={{0,16},{1,13},{2,18},{3,15},{4,20},{5,9},{6,22},{7,11},{8,24},{9,5... | collective-permute-start | bytes 196616 | tf_op jit(solution)/shard_map/ppermute | solution.py:405
  68.5 0.9 %turn.1 = bf16[128,1024]{1,0:T(8,128)(2,1)} custom-call(f32[128,1024]{1,0:T(8,128)S(1)} %get-tuple-element.30.turned), custom_call_target="tpu_custom_call" | custom-call | tf_op jit(solution)/shard_map/turn/pallas_call | solution.py:383
  69.4 2.4 %collective-permute-done.19 = bf16[256,128]{1,0:T(8,128)(2,1)S(1)} collective-permute-done((bf16[256,128]{1,0:T(8,128)(2,1)S(1)}, bf16[256,128]{1,0:T(8,128)(2,1)S(1)}, u32[]{:S(2)}, u32[]{:S(2)}) %collective-permute-start.19) | collective-permute-done | bytes 65568 | tf_op jit(solution)/shard_map/ppermute | solution.py:405
  (43 shorter events, 8.0 us)
Async XLA Ops:
  2.2 5.4 %collective-permute-start = (bf16[256,128]{1,0:T(8,128)(2,1)S(1)}, bf16[256,128]{1,0:T(8,128)(2,1)S(1)}, u32[]{:S(2)}, u32[]{:S(2)}) collective-permute-start(bf16[256,128]{1,0:T(8,128)(2,1)S(1)} %get-tuple-element.46), channel_id=1, source_target_pairs={{0,4},{1,3},{2,6},{3,1},{4,0},{5,7},{6,2},{7,5},{8,12},{9,11},{10,... | collective-permute-start | bytes 196616 | tf_op jit(solution)/shard_map/ppermute | solution.py:405
  5.3 5.9 %collective-permute-start.2 = (bf16[256,128]{1,0:T(8,128)(2,1)S(1)}, bf16[256,128]{1,0:T(8,128)(2,1)S(1)}, u32[]{:S(2)}, u32[]{:S(2)}) collective-permute-start(bf16[256,128]{1,0:T(8,128)(2,1)S(1)} %get-tuple-element.46), channel_id=1, source_target_pairs={{0,20},{1,15},{2,22},{3,13},{4,16},{5,11},{6,18},{7,9},{8,28},{9,7... | collective-permute-start | bytes 196616 | tf_op jit(solution)/shard_map/ppermute | solution.py:405
  6.7 4.5 %collective-permute-start.1 = (bf16[256,128]{1,0:T(8,128)(2,1)S(1)}, bf16[256,128]{1,0:T(8,128)(2,1)S(1)}, u32[]{:S(2)}, u32[]{:S(2)}) collective-permute-start(bf16[256,128]{1,0:T(8,128)(2,1)S(1)} %get-tuple-element.46), channel_id=1, source_target_pairs={{0,16},{1,13},{2,18},{3,15},{4,20},{5,9},{6,22},{7,11},{8,24},{9,5... | collective-permute-start | bytes 196616 | tf_op jit(solution)/shard_map/ppermute | solution.py:405
  11.2 11.9 %collective-permute-start.5 = (bf16[1024,128]{1,0:T(8,128)(2,1)S(1)}, bf16[1024,128]{1,0:T(8,128)(2,1)S(1)}, u32[]{:S(2)}, u32[]{:S(2)}) collective-permute-start(bf16[1024,128]{1,0:T(8,128)(2,1)S(1)} %constant_dynamic-update-slice_fusion.2.refs_0_), channel_id=1, source_target_pairs={{0,14},{1,21},{2,12},{3,23},{4,10},{5,17},{6,8},{7,19},{8,6},{9,29... | collective-permute-start | bytes 786440 | tf_op jit(solution)/shard_map/ppermute | solution.py:405
  15.6 11.0 %collective-permute-start.4 = (bf16[1024,128]{1,0:T(8,128)(2,1)S(1)}, bf16[1024,128]{1,0:T(8,128)(2,1)S(1)}, u32[]{:S(2)}, u32[]{:S(2)}) collective-permute-start(bf16[1024,128]{1,0:T(8,128)(2,1)S(1)} %constant_dynamic-update-slice_fusion.2.refs_0_), channel_id=1, source_target_pairs={{0,12},{1,17},{2,14},{3,19},{4,8},{5,21},{6,10},{7,23},{8,4},{9,25... | collective-permute-start | bytes 786440 | tf_op jit(solution)/shard_map/ppermute | solution.py:405
  16.1 10.5 %collective-permute-start.3 = (bf16[1024,128]{1,0:T(8,128)(2,1)S(1)}, bf16[1024,128]{1,0:T(8,128)(2,1)S(1)}, u32[]{:S(2)}, u32[]{:S(2)}) collective-permute-start(bf16[1024,128]{1,0:T(8,128)(2,1)S(1)} %constant_dynamic-update-slice_fusion.2.refs_0_), channel_id=1, source_target_pairs={{0,2},{1,5},{2,0},{3,7},{4,6},{5,1},{6,4},{7,3},{8,10},{9,13},{10,... | collective-permute-start | bytes 786440 | tf_op jit(solution)/shard_map/ppermute | solution.py:405
  16.6 18.7 %collective-permute-start.6 = (bf16[1024,128]{1,0:T(8,128)(2,1)S(1)}, bf16[1024,128]{1,0:T(8,128)(2,1)S(1)}, u32[]{:S(2)}, u32[]{:S(2)}) collective-permute-start(bf16[1024,128]{1,0:T(8,128)(2,1)S(1)} %constant_dynamic-update-slice_fusion.2.refs_0_), channel_id=1, source_target_pairs={{0,1},{1,0},{2,3},{3,2},{4,5},{5,4},{6,7},{7,6},{8,9},{9,8},{10,11... | collective-permute-start | bytes 786440 | tf_op jit(solution)/shard_map/ppermute | solution.py:405
  23.2 12.1 %collective-permute-start.9 = (bf16[1024,128]{1,0:T(8,128)(2,1)S(1)}, bf16[1024,128]{1,0:T(8,128)(2,1)S(1)}, u32[]{:S(2)}, u32[]{:S(2)}) collective-permute-start(bf16[1024,128]{1,0:T(8,128)(2,1)S(1)} %collective-permute-done.5.refs_3_), channel_id=1, source_target_pairs={{0,1},{1,0},{2,3},{3,2},{4,5},{5,4},{6,7},{7,6},{8,9},{9,8},{10,11... | collective-permute-start | bytes 786440 | tf_op jit(solution)/shard_map/ppermute | solution.py:405
  26.6 8.7 %collective-permute-start.8 = (bf16[1024,128]{1,0:T(8,128)(2,1)S(1)}, bf16[1024,128]{1,0:T(8,128)(2,1)S(1)}, u32[]{:S(2)}, u32[]{:S(2)}) collective-permute-start(bf16[1024,128]{1,0:T(8,128)(2,1)S(1)} %collective-permute-done.4.refs_2_), channel_id=1, source_target_pairs={{0,1},{1,0},{2,3},{3,2},{4,5},{5,4},{6,7},{7,6},{8,9},{9,8},{10,11... | collective-permute-start | bytes 786440 | tf_op jit(solution)/shard_map/ppermute | solution.py:405
  26.6 8.7 %collective-permute-start.7 = (bf16[1024,128]{1,0:T(8,128)(2,1)S(1)}, bf16[1024,128]{1,0:T(8,128)(2,1)S(1)}, u32[]{:S(2)}, u32[]{:S(2)}) collective-permute-start(bf16[1024,128]{1,0:T(8,128)(2,1)S(1)} %collective-permute-done.3.refs_1_), channel_id=1, source_target_pairs={{0,1},{1,0},{2,3},{3,2},{4,5},{5,4},{6,7},{7,6},{8,9},{9,8},{10,11... | collective-permute-start | bytes 786440 | tf_op jit(solution)/shard_map/ppermute | solution.py:405
  28.4 1.0 %copy-start = (bf16[128,1024]{1,0:T(8,128)(2,1)S(1)}, bf16[128,1024]{1,0:T(8,128)(2,1)}, u32[]{:S(2)}) copy-start(bf16[128,1024]{1,0:T(8,128)(2,1)} %q_ref.1) | copy-start | bytes 786436
  29.4 0.9 %copy-start.1 = (bf16[128,1024]{1,0:T(8,128)(2,1)S(1)}, bf16[128,1024]{1,0:T(8,128)(2,1)}, u32[]{:S(2)}) copy-start(bf16[128,1024]{1,0:T(8,128)(2,1)} %g_ref.1) | copy-start | bytes 786436
  30.3 0.9 %copy-start.2 = (bf16[128,1024]{1,0:T(8,128)(2,1)S(1)}, bf16[128,1024]{1,0:T(8,128)(2,1)}, u32[]{:S(2)}) copy-start(bf16[128,1024]{1,0:T(8,128)(2,1)} %o_ref.1) | copy-start | bytes 786436
  31.9 0.7 copy-start.4
  47.1 1.6 %collective-permute-start.11 = (bf16[1024,128]{1,0:T(8,128)(2,1)S(1)}, bf16[1024,128]{1,0:T(8,128)(2,1)S(1)}, u32[]{:S(2)}, u32[]{:S(2)}) collective-permute-start(bf16[1024,128]{1,0:T(8,128)(2,1)S(1)} %get-tuple-element.34), channel_id=1, source_target_pairs={{0,1},{1,0},{2,3},{3,2},{4,5},{5,4},{6,7},{7,6},{8,9},{9,8},{10,11... | collective-permute-start | bytes 786440 | tf_op jit(solution)/shard_map/ppermute | solution.py:405
  47.2 2.8 %collective-permute-start.13 = (bf16[1024,128]{1,0:T(8,128)(2,1)S(1)}, bf16[1024,128]{1,0:T(8,128)(2,1)S(1)}, u32[]{:S(2)}, u32[]{:S(2)}) collective-permute-start(bf16[1024,128]{1,0:T(8,128)(2,1)S(1)} %get-tuple-element.36), channel_id=1, source_target_pairs={{0,1},{1,0},{2,3},{3,2},{4,5},{5,4},{6,7},{7,6},{8,9},{9,8},{10,11... | collective-permute-start | bytes 786440 | tf_op jit(solution)/shard_map/ppermute | solution.py:405
  47.7 6.7 %collective-permute-start.10 = (bf16[1024,128]{1,0:T(8,128)(2,1)S(1)}, bf16[1024,128]{1,0:T(8,128)(2,1)S(1)}, u32[]{:S(2)}, u32[]{:S(2)}) collective-permute-start(bf16[1024,128]{1,0:T(8,128)(2,1)S(1)} %get-tuple-element.32), channel_id=1, source_target_pairs={{0,1},{1,0},{2,3},{3,2},{4,5},{5,4},{6,7},{7,6},{8,9},{9,8},{10,11... | collective-permute-start | bytes 786440 | tf_op jit(solution)/shard_map/ppermute | solution.py:405
  47.8 4.4 %collective-permute-start.15 = (bf16[1024,128]{1,0:T(8,128)(2,1)S(1)}, bf16[1024,128]{1,0:T(8,128)(2,1)S(1)}, u32[]{:S(2)}, u32[]{:S(2)}) collective-permute-start(bf16[1024,128]{1,0:T(8,128)(2,1)S(1)} %get-tuple-element.38), channel_id=1, source_target_pairs={{0,1},{1,0},{2,3},{3,2},{4,5},{5,4},{6,7},{7,6},{8,9},{9,8},{10,11... | collective-permute-start | bytes 786440 | tf_op jit(solution)/shard_map/ppermute | solution.py:405
  48.8 6.4 %collective-permute-start.12 = (bf16[1024,128]{1,0:T(8,128)(2,1)S(1)}, bf16[1024,128]{1,0:T(8,128)(2,1)S(1)}, u32[]{:S(2)}, u32[]{:S(2)}) collective-permute-start(bf16[1024,128]{1,0:T(8,128)(2,1)S(1)} %add_convert_fusion.2), channel_id=1, source_target_pairs={{0,2},{1,5},{2,0},{3,7},{4,6},{5,1},{6,4},{7,3},{8,10},{9,13},{10,... | collective-permute-start | bytes 786440 | tf_op jit(solution)/shard_map/ppermute | solution.py:405
  50.1 11.0 %collective-permute-start.14 = (bf16[1024,128]{1,0:T(8,128)(2,1)S(1)}, bf16[1024,128]{1,0:T(8,128)(2,1)S(1)}, u32[]{:S(2)}, u32[]{:S(2)}) collective-permute-start(bf16[1024,128]{1,0:T(8,128)(2,1)S(1)} %add_convert_fusion.1), channel_id=1, source_target_pairs={{0,12},{1,17},{2,14},{3,19},{4,8},{5,21},{6,10},{7,23},{8,4},{9,25... | collective-permute-start | bytes 786440 | tf_op jit(solution)/shard_map/ppermute | solution.py:405
  52.2 12.5 %collective-permute-start.16 = (bf16[1024,128]{1,0:T(8,128)(2,1)S(1)}, bf16[1024,128]{1,0:T(8,128)(2,1)S(1)}, u32[]{:S(2)}, u32[]{:S(2)}) collective-permute-start(bf16[1024,128]{1,0:T(8,128)(2,1)S(1)} %add_convert_fusion), channel_id=1, source_target_pairs={{0,14},{1,21},{2,12},{3,23},{4,10},{5,17},{6,8},{7,19},{8,6},{9,29... | collective-permute-start | bytes 786440 | tf_op jit(solution)/shard_map/ppermute | solution.py:405
  64.9 4.5 %collective-permute-start.17 = (bf16[256,128]{1,0:T(8,128)(2,1)S(1)}, bf16[256,128]{1,0:T(8,128)(2,1)S(1)}, u32[]{:S(2)}, u32[]{:S(2)}) collective-permute-start(bf16[256,128]{1,0:T(8,128)(2,1)S(1)} %get-tuple-element.41), channel_id=1, source_target_pairs={{0,4},{1,3},{2,6},{3,1},{4,0},{5,7},{6,2},{7,5},{8,12},{9,11},{10,... | collective-permute-start | bytes 196616 | tf_op jit(solution)/shard_map/ppermute | solution.py:405
  66.5 5.3 %collective-permute-start.19 = (bf16[256,128]{1,0:T(8,128)(2,1)S(1)}, bf16[256,128]{1,0:T(8,128)(2,1)S(1)}, u32[]{:S(2)}, u32[]{:S(2)}) collective-permute-start(bf16[256,128]{1,0:T(8,128)(2,1)S(1)} %get-tuple-element.42), channel_id=1, source_target_pairs={{0,20},{1,15},{2,22},{3,13},{4,16},{5,11},{6,18},{7,9},{8,28},{9,7... | collective-permute-start | bytes 196616 | tf_op jit(solution)/shard_map/ppermute | solution.py:405
  67.3 5.0 %collective-permute-start.18 = (bf16[256,128]{1,0:T(8,128)(2,1)S(1)}, bf16[256,128]{1,0:T(8,128)(2,1)S(1)}, u32[]{:S(2)}, u32[]{:S(2)}) collective-permute-start(bf16[256,128]{1,0:T(8,128)(2,1)S(1)} %get-tuple-element.43), channel_id=1, source_target_pairs={{0,16},{1,13},{2,18},{3,15},{4,20},{5,9},{6,22},{7,11},{8,24},{9,5... | collective-permute-start | bytes 196616 | tf_op jit(solution)/shard_map/ppermute | solution.py:405
  (1 other events, 0.7 us)

commit v4 on v3

--- a/solution.py
+++ b/solution.py
@@ -24,34 +24,39 @@
         self.square = self.near == self.far
         self.count = rows * cols
 
-    def split(self, row, col):
+    def chip(self, row, col, kind):
         ring = col // 4
         half = ring // 2
-        return row * 2 + (ring + half) % 2, half * 2 + (col // 2) % 2, col % 2
-
-    def join(self, near, far, core):
-        half = far // 2
-        ring = half * 2 + (near + half) % 2
-        return (near // 2) * self.cols + ring * 4 + (far % 2) * 2 + core
+        fold = half if kind == 0 else 0
+        return row * 2 + (ring + fold) % 2, half * 2 + (col // 2) % 2
 
     def hop(self, first=0, second=0, core_flip=0):
         pairs = []
         for device in range(self.count):
-            near, far, core = self.split(device // self.cols, device % self.cols)
+            col = device % self.cols
+            core = col % 2
+            near, far = self.chip(device // self.cols, col, core)
             if self.square and core == 1:
                 near, far = near ^ second, far ^ first
             else:
                 near, far = near ^ first, far ^ second
-            pairs.append((device, self.join(near, far, core ^ core_flip)))
+            half = far // 2
+            fold = half if core == 0 else 0
+            col = (half * 2 + (near + fold) % 2) * 4 + (far % 2) * 2 + (core ^ core_flip)
+            pairs.append((device, (near // 2) * self.cols + col))
         return pairs
 
-    def slot(self, own, stored):
-        near, far, core = self.split(stored % self.rows, stored // self.rows)
-        near, far = near ^ own[0], far ^ own[1]
-        place = far * self.near + near
-        if self.square:
-            place = jnp.where(core == 1, near * self.far + far, place)
-        return place + jnp.where(core == own[2], 0, self.count // 2)
+    def slot(self, row, col, stored):
+        core = (stored // self.rows) % 2
+        places = []
+        for kind in range(2):
+            own = self.chip(row, col, kind)
+            other = self.chip(stored % self.rows, stored // self.rows, kind)
+            near, far = own[0] ^ other[0], own[1] ^ other[1]
+            turned = self.square and kind == 1
+            places.append(near * self.far + far if turned else far * self.near + near)
+        place = jnp.where(core == 1, places[1], places[0])
+        return place + jnp.where(core == col % 2, 0, self.count // 2)
 
     def early(self, slot):
         return slot % (self.count // 2) >= self.count // 4
@@ -67,7 +72,6 @@
     layout, heads, here, order, window, q_ref, e_ref, g_ref, o_ref, q_out, g_out, d_out, meta
 ):
     row, col = here[0], here[1]
-    own = layout.split(row, col)
     own_block = order[row * layout.cols + col]
     live = jnp.minimum(own_block, (window[0] + STRIPE - 2) // STRIPE) + 1
     part_len = layout.count + 2
@@ -79,7 +83,7 @@
 
     def visit(stored, filled):
         back = own_block - order[stored]
-        slot = layout.slot(own, stored)
+        slot = layout.slot(row, col, stored)
         early = layout.early(slot)
         wanted = (back >= 0) & (back < live)
 
@@ -407,7 +411,7 @@
     def widen(value):
         return value.astype(jnp.float32)
 
-    pair = jnp.concatenate([key_head, value_head], 0)
+    pair = lax.optimization_barrier(jnp.concatenate([key_head, value_head], 0))
     stage = [pair] + [send(pair, first=i) for i in range(1, layout.near)]
     plane = jnp.concatenate(stage, 0)
     own_pieces = [plane] + [send(plane, second=j) for j in range(1, layout.far)]

time: 73.3 us -> 73 us (level)
  local copies, waits for them, and re-layouts: 6.39 us -> 4.8 us
  other arithmetic: 0.5 us -> 1.3 us
    concatenate x0 -> x2, other arithmetic: none -> 0.8 us  [the longest x1 0.78 us: per_device(): pair = lax.optimization_barrier(jnp.concatenate([key_head, value_head], 0))]
    unnamed x13 -> x10, local copies, waits for them, and re-layouts: 4.95 us -> 4.16 us
    concatenate x2 -> x0, local copies, waits for them, and re-layouts: 0.79 us -> none  [the longest x1 0.78 us: per_device(): pair = jnp.concatenate([key_head, value_head], 0)]
  transfers between devices with their start and end apart: 20 -> 20, of which waited for: 10 -> 11; matrix products, arithmetic and copies ran while one was open for 0% -> 0% of each run, Pallas kernels for 5% -> 6%
where the time goes in v4:
time: 73 us; the launch traced here: 72.7 us
  waiting for transfers between devices  28.6 us (39%)
  starting transfers between devices  20.6 us (28%)
  Pallas kernels  16 us (22%)
  local copies, waits for them, and re-layouts  4.8 us (7%)
  between operations  1.4 us (2%)
  other arithmetic  1.3 us (2%)
    ppermute x20, waiting for transfers between devices, send(): return lax.ppermute(value, AXES, layout.hop(**where))  28.6 us
    ppermute x20, starting transfers between devices, send(): return lax.ppermute(value, AXES, layout.hop(**where))  20.6 us
    pallas_call x2, Pallas kernels, run_attend(): pl.pallas_call(functools.partial(body, stripes, pieces, heads, keep, inv_...  11.8 us
    unnamed x10, local copies, waits for them, and re-layouts  4.16 us
    pallas_call x1, Pallas kernels, run_prepare(): pl.pallas_call(functools.partial(prepare, layout, heads), out_shape=[flat...  3.31 us
  transfers between devices with their start and end apart: 20, of which 11 were waited for; matrix products, arithmetic and copies ran while one was open for 0% of the time, Pallas kernels for 6%

profile of v4, /device:TPU:0, one launch (start us, length us, event | category | flops | bytes accessed | tf_op | source)
XLA Modules:
  0.0 72.7 jit_solution(15606610494194255135)
XLA Ops:
  1.4 4.0 %collective-permute-start.2 = (bf16[256,128]{1,0:T(8,128)(2,1)S(1)}, bf16[256,128]{1,0:T(8,128)(2,1)S(1)}, u32[]{:S(2)}, u32[]{:S(2)}) collective-permute-start(bf16[256,128]{1,0:T(8,128)(2,1)S(1)} %pad_maximum_fusion.1), channel_id=1, source_target_pairs={{0,20},{1,11},{2,22},{3,9},{4,16},{5,15},{6,18},{7,13},{8,28},{9,3... | collective-permute-start | bytes 196616 | tf_op jit(solution)/shard_map/ppermute | solution.py:409
  6.0 1.9 %collective-permute-done.2 = bf16[256,128]{1,0:T(8,128)(2,1)S(1)} collective-permute-done((bf16[256,128]{1,0:T(8,128)(2,1)S(1)}, bf16[256,128]{1,0:T(8,128)(2,1)S(1)}, u32[]{:S(2)}, u32[]{:S(2)}) %collective-permute-start.2) | collective-permute-done | bytes 65568 | tf_op jit(solution)/shard_map/ppermute | solution.py:409
  7.9 1.8 %collective-permute-done.1 = bf16[256,128]{1,0:T(8,128)(2,1)S(1)} collective-permute-done((bf16[256,128]{1,0:T(8,128)(2,1)S(1)}, bf16[256,128]{1,0:T(8,128)(2,1)S(1)}, u32[]{:S(2)}, u32[]{:S(2)}) %collective-permute-start.1) | collective-permute-done | bytes 65568 | tf_op jit(solution)/shard_map/ppermute | solution.py:409
  9.7 1.2 %collective-permute-done = bf16[256,128]{1,0:T(8,128)(2,1)S(1)} collective-permute-done((bf16[256,128]{1,0:T(8,128)(2,1)S(1)}, bf16[256,128]{1,0:T(8,128)(2,1)S(1)}, u32[]{:S(2)}, u32[]{:S(2)}) %collective-permute-start) | collective-permute-done | bytes 65568 | tf_op jit(solution)/shard_map/ppermute | solution.py:409
  10.9 3.8 %collective-permute-start.5 = (bf16[1024,128]{1,0:T(8,128)(2,1)S(1)}, bf16[1024,128]{1,0:T(8,128)(2,1)S(1)}, u32[]{:S(2)}, u32[]{:S(2)}) collective-permute-start(bf16[1024,128]{1,0:T(8,128)(2,1)S(1)} %pad_maximum_fusion.refs_0_), channel_id=1, source_target_pairs={{0,14},{1,21},{2,12},{3,23},{4,10},{5,17},{6,8},{7,19},{8,6},{9,29... | collective-permute-start | bytes 786440 | tf_op jit(solution)/shard_map/ppermute | solution.py:409
  15.1 1.2 %collective-permute-start.3 = (bf16[1024,128]{1,0:T(8,128)(2,1)S(1)}, bf16[1024,128]{1,0:T(8,128)(2,1)S(1)}, u32[]{:S(2)}, u32[]{:S(2)}) collective-permute-start(bf16[1024,128]{1,0:T(8,128)(2,1)S(1)} %pad_maximum_fusion.refs_0_), channel_id=1, source_target_pairs={{0,2},{1,5},{2,0},{3,7},{4,6},{5,1},{6,4},{7,3},{8,10},{9,13},{10,... | collective-permute-start | bytes 786440 | tf_op jit(solution)/shard_map/ppermute | solution.py:409
  16.3 6.6 %collective-permute-done.5.refs_3_ = bf16[1024,128]{1,0:T(8,128)(2,1)S(1)} collective-permute-done((bf16[1024,128]{1,0:T(8,128)(2,1)S(1)}, bf16[1024,128]{1,0:T(8,128)(2,1)S(1)}, u32[]{:S(2)}, u32[]{:S(2)}) %collective-permute-start.5) | collective-permute-done | bytes 262176 | tf_op jit(solution)/shard_map/ppermute | solution.py:409
  22.9 3.2 %collective-permute-done.4.refs_2_ = bf16[1024,128]{1,0:T(8,128)(2,1)S(1)} collective-permute-done((bf16[1024,128]{1,0:T(8,128)(2,1)S(1)}, bf16[1024,128]{1,0:T(8,128)(2,1)S(1)}, u32[]{:S(2)}, u32[]{:S(2)}) %collective-permute-start.4) | collective-permute-done | bytes 262176 | tf_op jit(solution)/shard_map/ppermute | solution.py:409
  27.3 0.9 %copy-done = bf16[128,1024]{1,0:T(8,128)(2,1)S(1)} copy-done((bf16[128,1024]{1,0:T(8,128)(2,1)S(1)}, bf16[128,1024]{1,0:T(8,128)(2,1)}, u32[]{:S(2)}) %copy-start) | copy-done | bytes 262168
  28.2 0.9 %copy-done.1 = bf16[128,1024]{1,0:T(8,128)(2,1)S(1)} copy-done((bf16[128,1024]{1,0:T(8,128)(2,1)S(1)}, bf16[128,1024]{1,0:T(8,128)(2,1)}, u32[]{:S(2)}) %copy-start.1) | copy-done | bytes 262168
  29.2 0.9 %copy-done.2 = bf16[128,1024]{1,0:T(8,128)(2,1)S(1)} copy-done((bf16[128,1024]{1,0:T(8,128)(2,1)S(1)}, bf16[128,1024]{1,0:T(8,128)(2,1)}, u32[]{:S(2)}) %copy-start.2) | copy-done | bytes 262168
  31.4 3.3 %prep.1 = (bf16[1024,128]{1,0:T(8,128)(2,1)S(1)}, bf16[1024,128]{1,0:T(8,128)(2,1)S(1)}, f32[1,1024]{1,0:T(1,128)S(1)}, s32[71]{0:T(128)S(1)}) custom-call(s32[2]{0:T(128)S(1)} %pad_add_fusion.here, s32[32]{0:T(128)S(1)} %copy-done.3, s32[1]{0:T(128)S(6)} %copy.11.window, bf16[128,1024]{1,0:T(8,128)(2,1)S(1)} %copy-done, s32[1,128]{1,0:T(1,128)S(1)} %bitcast.3, ...), custom_call_target="tpu_custom_call" | custom-call | tf_op jit(solution)/shard_map/prep/pallas_call | solution.py:340
  34.8 8.0 %early.1 = (bf16[8448,128]{1,0:T(8,128)(2,1)S(1)}, f32[18,256,1024]{2,1,0:T(8,128)S(1)}, f32[1,1024]{1,0:T(1,128)S(1)}, f32[1,1024]{1,0:T(1,128)S(1)}, f32[128,1...) custom-call(s32[71]{0:T(128)S(1)} %get-tuple-element.21.meta, ...), custom_call_target="tpu_custom_call" | custom-call | tf_op jit(solution)/shard_map/early/pallas_call | solution.py:375
  42.8 3.8 %late.1 = (f32[128,1024]{1,0:T(8,128)S(1)}, bf16[1024,128]{1,0:T(8,128)(2,1)S(1)}, bf16[1024,128]{1,0:T(8,128)(2,1)S(1)}, bf16[1024,128]{1,0:T(8,128)(2,1)S(1)}, bf16[1024,128]{1,0:T(8,128)(2,1)S(1)}) custom-call(s32[71]{0:T(128)S(1)} %get-tuple-element.21.meta, bf16[1024,128]{1,0:T(8,128)(2,1)S(1)} %get-tuple-element.22.q_ref, ...), custom_call_target="tpu_custom_call" | custom-call | tf_op jit(solution)/shard_map/late/pallas_call | solution.py:375
  48.3 0.9 %collective-permute-start.12 = (bf16[1024,128]{1,0:T(8,128)(2,1)S(1)}, bf16[1024,128]{1,0:T(8,128)(2,1)S(1)}, u32[]{:S(2)}, u32[]{:S(2)}) collective-permute-start(bf16[1024,128]{1,0:T(8,128)(2,1)S(1)} %add_convert_fusion.2), channel_id=1, source_target_pairs={{0,2},{1,5},{2,0},{3,7},{4,6},{5,1},{6,4},{7,3},{8,10},{9,13},{10,... | collective-permute-start | bytes 786440 | tf_op jit(solution)/shard_map/ppermute | solution.py:409
  49.2 1.8 %collective-permute-start.14 = (bf16[1024,128]{1,0:T(8,128)(2,1)S(1)}, bf16[1024,128]{1,0:T(8,128)(2,1)S(1)}, u32[]{:S(2)}, u32[]{:S(2)}) collective-permute-start(bf16[1024,128]{1,0:T(8,128)(2,1)S(1)} %add_convert_fusion.1), channel_id=1, source_target_pairs={{0,12},{1,17},{2,14},{3,19},{4,8},{5,21},{6,10},{7,23},{8,4},{9,25... | collective-permute-start | bytes 786440 | tf_op jit(solution)/shard_map/ppermute | solution.py:409
  51.1 2.9 %collective-permute-start.16 = (bf16[1024,128]{1,0:T(8,128)(2,1)S(1)}, bf16[1024,128]{1,0:T(8,128)(2,1)S(1)}, u32[]{:S(2)}, u32[]{:S(2)}) collective-permute-start(bf16[1024,128]{1,0:T(8,128)(2,1)S(1)} %add_convert_fusion), channel_id=1, source_target_pairs={{0,14},{1,21},{2,12},{3,23},{4,10},{5,17},{6,8},{7,19},{8,6},{9,29... | collective-permute-start | bytes 786440 | tf_op jit(solution)/shard_map/ppermute | solution.py:409
  53.9 0.8 %collective-permute-done.12 = bf16[1024,128]{1,0:T(8,128)(2,1)S(1)} collective-permute-done((bf16[1024,128]{1,0:T(8,128)(2,1)S(1)}, bf16[1024,128]{1,0:T(8,128)(2,1)S(1)}, u32[]{:S(2)}, u32[]{:S(2)}) %collective-permute-start.12) | collective-permute-done | bytes 262176 | tf_op jit(solution)/shard_map/ppermute | solution.py:409
  54.7 5.5 %collective-permute-done.14 = bf16[1024,128]{1,0:T(8,128)(2,1)S(1)} collective-permute-done((bf16[1024,128]{1,0:T(8,128)(2,1)S(1)}, bf16[1024,128]{1,0:T(8,128)(2,1)S(1)}, u32[]{:S(2)}, u32[]{:S(2)}) %collective-permute-start.14) | collective-permute-done | bytes 262176 | tf_op jit(solution)/shard_map/ppermute | solution.py:409
  60.3 4.1 %collective-permute-done.16 = bf16[1024,128]{1,0:T(8,128)(2,1)S(1)} collective-permute-done((bf16[1024,128]{1,0:T(8,128)(2,1)S(1)}, bf16[1024,128]{1,0:T(8,128)(2,1)S(1)}, u32[]{:S(2)}, u32[]{:S(2)}) %collective-permute-start.16) | collective-permute-done | bytes 262176 | tf_op jit(solution)/shard_map/ppermute | solution.py:409
  64.6 1.6 %collective-permute-start.17 = (bf16[256,128]{1,0:T(8,128)(2,1)S(1)}, bf16[256,128]{1,0:T(8,128)(2,1)S(1)}, u32[]{:S(2)}, u32[]{:S(2)}) collective-permute-start(bf16[256,128]{1,0:T(8,128)(2,1)S(1)} %get-tuple-element.41), channel_id=1, source_target_pairs={{0,4},{1,3},{2,6},{3,1},{4,0},{5,7},{6,2},{7,5},{8,12},{9,11},{10,... | collective-permute-start | bytes 196616 | tf_op jit(solution)/shard_map/ppermute | solution.py:409
  66.2 1.3 %collective-permute-start.19 = (bf16[256,128]{1,0:T(8,128)(2,1)S(1)}, bf16[256,128]{1,0:T(8,128)(2,1)S(1)}, u32[]{:S(2)}, u32[]{:S(2)}) collective-permute-start(bf16[256,128]{1,0:T(8,128)(2,1)S(1)} %get-tuple-element.42), channel_id=1, source_target_pairs={{0,20},{1,11},{2,22},{3,9},{4,16},{5,15},{6,18},{7,13},{8,28},{9,3... | collective-permute-start | bytes 196616 | tf_op jit(solution)/shard_map/ppermute | solution.py:409
  68.1 0.9 %turn.1 = bf16[128,1024]{1,0:T(8,128)(2,1)} custom-call(f32[128,1024]{1,0:T(8,128)S(1)} %get-tuple-element.30.turned), custom_call_target="tpu_custom_call" | custom-call | tf_op jit(solution)/shard_map/turn/pallas_call | solution.py:387
  69.0 2.3 %collective-permute-done.19 = bf16[256,128]{1,0:T(8,128)(2,1)S(1)} collective-permute-done((bf16[256,128]{1,0:T(8,128)(2,1)S(1)}, bf16[256,128]{1,0:T(8,128)(2,1)S(1)}, u32[]{:S(2)}, u32[]{:S(2)}) %collective-permute-start.19) | collective-permute-done | bytes 65568 | tf_op jit(solution)/shard_map/ppermute | solution.py:409
  (40 shorter events, 7.7 us)
Async XLA Ops:
  1.4 6.5 %collective-permute-start.2 = (bf16[256,128]{1,0:T(8,128)(2,1)S(1)}, bf16[256,128]{1,0:T(8,128)(2,1)S(1)}, u32[]{:S(2)}, u32[]{:S(2)}) collective-permute-start(bf16[256,128]{1,0:T(8,128)(2,1)S(1)} %pad_maximum_fusion.1), channel_id=1, source_target_pairs={{0,20},{1,11},{2,22},{3,9},{4,16},{5,15},{6,18},{7,13},{8,28},{9,3... | collective-permute-start | bytes 196616 | tf_op jit(solution)/shard_map/ppermute | solution.py:409
  5.4 4.3 %collective-permute-start.1 = (bf16[256,128]{1,0:T(8,128)(2,1)S(1)}, bf16[256,128]{1,0:T(8,128)(2,1)S(1)}, u32[]{:S(2)}, u32[]{:S(2)}) collective-permute-start(bf16[256,128]{1,0:T(8,128)(2,1)S(1)} %pad_maximum_fusion.1), channel_id=1, source_target_pairs={{0,16},{1,9},{2,18},{3,11},{4,20},{5,13},{6,22},{7,15},{8,24},{9,1... | collective-permute-start | bytes 196616 | tf_op jit(solution)/shard_map/ppermute | solution.py:409
  5.9 5.0 %collective-permute-start = (bf16[256,128]{1,0:T(8,128)(2,1)S(1)}, bf16[256,128]{1,0:T(8,128)(2,1)S(1)}, u32[]{:S(2)}, u32[]{:S(2)}) collective-permute-start(bf16[256,128]{1,0:T(8,128)(2,1)S(1)} %pad_maximum_fusion.1), channel_id=1, source_target_pairs={{0,4},{1,3},{2,6},{3,1},{4,0},{5,7},{6,2},{7,5},{8,12},{9,11},{10,... | collective-permute-start | bytes 196616 | tf_op jit(solution)/shard_map/ppermute | solution.py:409
  10.9 11.9 %collective-permute-start.5 = (bf16[1024,128]{1,0:T(8,128)(2,1)S(1)}, bf16[1024,128]{1,0:T(8,128)(2,1)S(1)}, u32[]{:S(2)}, u32[]{:S(2)}) collective-permute-start(bf16[1024,128]{1,0:T(8,128)(2,1)S(1)} %pad_maximum_fusion.refs_0_), channel_id=1, source_target_pairs={{0,14},{1,21},{2,12},{3,23},{4,10},{5,17},{6,8},{7,19},{8,6},{9,29... | collective-permute-start | bytes 786440 | tf_op jit(solution)/shard_map/ppermute | solution.py:409
  14.7 11.3 %collective-permute-start.4 = (bf16[1024,128]{1,0:T(8,128)(2,1)S(1)}, bf16[1024,128]{1,0:T(8,128)(2,1)S(1)}, u32[]{:S(2)}, u32[]{:S(2)}) collective-permute-start(bf16[1024,128]{1,0:T(8,128)(2,1)S(1)} %pad_maximum_fusion.refs_0_), channel_id=1, source_target_pairs={{0,12},{1,17},{2,14},{3,19},{4,8},{5,21},{6,10},{7,23},{8,4},{9,25... | collective-permute-start | bytes 786440 | tf_op jit(solution)/shard_map/ppermute | solution.py:409
  15.1 11.0 %collective-permute-start.3 = (bf16[1024,128]{1,0:T(8,128)(2,1)S(1)}, bf16[1024,128]{1,0:T(8,128)(2,1)S(1)}, u32[]{:S(2)}, u32[]{:S(2)}) collective-permute-start(bf16[1024,128]{1,0:T(8,128)(2,1)S(1)} %pad_maximum_fusion.refs_0_), channel_id=1, source_target_pairs={{0,2},{1,5},{2,0},{3,7},{4,6},{5,1},{6,4},{7,3},{8,10},{9,13},{10,... | collective-permute-start | bytes 786440 | tf_op jit(solution)/shard_map/ppermute | solution.py:409
  16.3 18.5 %collective-permute-start.6 = (bf16[1024,128]{1,0:T(8,128)(2,1)S(1)}, bf16[1024,128]{1,0:T(8,128)(2,1)S(1)}, u32[]{:S(2)}, u32[]{:S(2)}) collective-permute-start(bf16[1024,128]{1,0:T(8,128)(2,1)S(1)} %pad_maximum_fusion.refs_0_), channel_id=1, source_target_pairs={{0,1},{1,0},{2,3},{3,2},{4,5},{5,4},{6,7},{7,6},{8,9},{9,8},{10,11... | collective-permute-start | bytes 786440 | tf_op jit(solution)/shard_map/ppermute | solution.py:409
  22.9 11.9 %collective-permute-start.9 = (bf16[1024,128]{1,0:T(8,128)(2,1)S(1)}, bf16[1024,128]{1,0:T(8,128)(2,1)S(1)}, u32[]{:S(2)}, u32[]{:S(2)}) collective-permute-start(bf16[1024,128]{1,0:T(8,128)(2,1)S(1)} %collective-permute-done.5.refs_3_), channel_id=1, source_target_pairs={{0,1},{1,0},{2,3},{3,2},{4,5},{5,4},{6,7},{7,6},{8,9},{9,8},{10,11... | collective-permute-start | bytes 786440 | tf_op jit(solution)/shard_map/ppermute | solution.py:409
  26.0 8.7 %collective-permute-start.8 = (bf16[1024,128]{1,0:T(8,128)(2,1)S(1)}, bf16[1024,128]{1,0:T(8,128)(2,1)S(1)}, u32[]{:S(2)}, u32[]{:S(2)}) collective-permute-start(bf16[1024,128]{1,0:T(8,128)(2,1)S(1)} %collective-permute-done.4.refs_2_), channel_id=1, source_target_pairs={{0,1},{1,0},{2,3},{3,2},{4,5},{5,4},{6,7},{7,6},{8,9},{9,8},{10,11... | collective-permute-start | bytes 786440 | tf_op jit(solution)/shard_map/ppermute | solution.py:409
  26.0 8.8 %collective-permute-start.7 = (bf16[1024,128]{1,0:T(8,128)(2,1)S(1)}, bf16[1024,128]{1,0:T(8,128)(2,1)S(1)}, u32[]{:S(2)}, u32[]{:S(2)}) collective-permute-start(bf16[1024,128]{1,0:T(8,128)(2,1)S(1)} %collective-permute-done.3.refs_1_), channel_id=1, source_target_pairs={{0,1},{1,0},{2,3},{3,2},{4,5},{5,4},{6,7},{7,6},{8,9},{9,8},{10,11... | collective-permute-start | bytes 786440 | tf_op jit(solution)/shard_map/ppermute | solution.py:409
  27.3 1.0 %copy-start = (bf16[128,1024]{1,0:T(8,128)(2,1)S(1)}, bf16[128,1024]{1,0:T(8,128)(2,1)}, u32[]{:S(2)}) copy-start(bf16[128,1024]{1,0:T(8,128)(2,1)} %q_ref.1) | copy-start | bytes 786436
  28.2 0.9 %copy-start.1 = (bf16[128,1024]{1,0:T(8,128)(2,1)S(1)}, bf16[128,1024]{1,0:T(8,128)(2,1)}, u32[]{:S(2)}) copy-start(bf16[128,1024]{1,0:T(8,128)(2,1)} %g_ref.1) | copy-start | bytes 786436
  29.2 0.9 %copy-start.2 = (bf16[128,1024]{1,0:T(8,128)(2,1)S(1)}, bf16[128,1024]{1,0:T(8,128)(2,1)}, u32[]{:S(2)}) copy-start(bf16[128,1024]{1,0:T(8,128)(2,1)} %o_ref.1) | copy-start | bytes 786436
  30.1 0.7 copy-start.3
  46.6 1.6 %collective-permute-start.11 = (bf16[1024,128]{1,0:T(8,128)(2,1)S(1)}, bf16[1024,128]{1,0:T(8,128)(2,1)S(1)}, u32[]{:S(2)}, u32[]{:S(2)}) collective-permute-start(bf16[1024,128]{1,0:T(8,128)(2,1)S(1)} %get-tuple-element.34), channel_id=1, source_target_pairs={{0,1},{1,0},{2,3},{3,2},{4,5},{5,4},{6,7},{7,6},{8,9},{9,8},{10,11... | collective-permute-start | bytes 786440 | tf_op jit(solution)/shard_map/ppermute | solution.py:409
  46.7 2.5 %collective-permute-start.13 = (bf16[1024,128]{1,0:T(8,128)(2,1)S(1)}, bf16[1024,128]{1,0:T(8,128)(2,1)S(1)}, u32[]{:S(2)}, u32[]{:S(2)}) collective-permute-start(bf16[1024,128]{1,0:T(8,128)(2,1)S(1)} %get-tuple-element.36), channel_id=1, source_target_pairs={{0,1},{1,0},{2,3},{3,2},{4,5},{5,4},{6,7},{7,6},{8,9},{9,8},{10,11... | collective-permute-start | bytes 786440 | tf_op jit(solution)/shard_map/ppermute | solution.py:409
  47.2 6.7 %collective-permute-start.10 = (bf16[1024,128]{1,0:T(8,128)(2,1)S(1)}, bf16[1024,128]{1,0:T(8,128)(2,1)S(1)}, u32[]{:S(2)}, u32[]{:S(2)}) collective-permute-start(bf16[1024,128]{1,0:T(8,128)(2,1)S(1)} %get-tuple-element.32), channel_id=1, source_target_pairs={{0,1},{1,0},{2,3},{3,2},{4,5},{5,4},{6,7},{7,6},{8,9},{9,8},{10,11... | collective-permute-start | bytes 786440 | tf_op jit(solution)/shard_map/ppermute | solution.py:409
  47.3 3.7 %collective-permute-start.15 = (bf16[1024,128]{1,0:T(8,128)(2,1)S(1)}, bf16[1024,128]{1,0:T(8,128)(2,1)S(1)}, u32[]{:S(2)}, u32[]{:S(2)}) collective-permute-start(bf16[1024,128]{1,0:T(8,128)(2,1)S(1)} %get-tuple-element.38), channel_id=1, source_target_pairs={{0,1},{1,0},{2,3},{3,2},{4,5},{5,4},{6,7},{7,6},{8,9},{9,8},{10,11... | collective-permute-start | bytes 786440 | tf_op jit(solution)/shard_map/ppermute | solution.py:409
  48.3 6.4 %collective-permute-start.12 = (bf16[1024,128]{1,0:T(8,128)(2,1)S(1)}, bf16[1024,128]{1,0:T(8,128)(2,1)S(1)}, u32[]{:S(2)}, u32[]{:S(2)}) collective-permute-start(bf16[1024,128]{1,0:T(8,128)(2,1)S(1)} %add_convert_fusion.2), channel_id=1, source_target_pairs={{0,2},{1,5},{2,0},{3,7},{4,6},{5,1},{6,4},{7,3},{8,10},{9,13},{10,... | collective-permute-start | bytes 786440 | tf_op jit(solution)/shard_map/ppermute | solution.py:409
  49.2 11.0 %collective-permute-start.14 = (bf16[1024,128]{1,0:T(8,128)(2,1)S(1)}, bf16[1024,128]{1,0:T(8,128)(2,1)S(1)}, u32[]{:S(2)}, u32[]{:S(2)}) collective-permute-start(bf16[1024,128]{1,0:T(8,128)(2,1)S(1)} %add_convert_fusion.1), channel_id=1, source_target_pairs={{0,12},{1,17},{2,14},{3,19},{4,8},{5,21},{6,10},{7,23},{8,4},{9,25... | collective-permute-start | bytes 786440 | tf_op jit(solution)/shard_map/ppermute | solution.py:409
  51.1 13.3 %collective-permute-start.16 = (bf16[1024,128]{1,0:T(8,128)(2,1)S(1)}, bf16[1024,128]{1,0:T(8,128)(2,1)S(1)}, u32[]{:S(2)}, u32[]{:S(2)}) collective-permute-start(bf16[1024,128]{1,0:T(8,128)(2,1)S(1)} %add_convert_fusion), channel_id=1, source_target_pairs={{0,14},{1,21},{2,12},{3,23},{4,10},{5,17},{6,8},{7,19},{8,6},{9,29... | collective-permute-start | bytes 786440 | tf_op jit(solution)/shard_map/ppermute | solution.py:409
  64.6 4.5 %collective-permute-start.17 = (bf16[256,128]{1,0:T(8,128)(2,1)S(1)}, bf16[256,128]{1,0:T(8,128)(2,1)S(1)}, u32[]{:S(2)}, u32[]{:S(2)}) collective-permute-start(bf16[256,128]{1,0:T(8,128)(2,1)S(1)} %get-tuple-element.41), channel_id=1, source_target_pairs={{0,4},{1,3},{2,6},{3,1},{4,0},{5,7},{6,2},{7,5},{8,12},{9,11},{10,... | collective-permute-start | bytes 196616 | tf_op jit(solution)/shard_map/ppermute | solution.py:409
  66.2 5.2 %collective-permute-start.19 = (bf16[256,128]{1,0:T(8,128)(2,1)S(1)}, bf16[256,128]{1,0:T(8,128)(2,1)S(1)}, u32[]{:S(2)}, u32[]{:S(2)}) collective-permute-start(bf16[256,128]{1,0:T(8,128)(2,1)S(1)} %get-tuple-element.42), channel_id=1, source_target_pairs={{0,20},{1,11},{2,22},{3,9},{4,16},{5,15},{6,18},{7,13},{8,28},{9,3... | collective-permute-start | bytes 196616 | tf_op jit(solution)/shard_map/ppermute | solution.py:409
  67.5 4.6 %collective-permute-start.18 = (bf16[256,128]{1,0:T(8,128)(2,1)S(1)}, bf16[256,128]{1,0:T(8,128)(2,1)S(1)}, u32[]{:S(2)}, u32[]{:S(2)}) collective-permute-start(bf16[256,128]{1,0:T(8,128)(2,1)S(1)} %get-tuple-element.43), channel_id=1, source_target_pairs={{0,16},{1,9},{2,18},{3,11},{4,20},{5,13},{6,22},{7,15},{8,24},{9,1... | collective-permute-start | bytes 196616 | tf_op jit(solution)/shard_map/ppermute | solution.py:409
  (1 other events, 0.7 us)

commit v5 on v4

--- a/solution.py
+++ b/solution.py
@@ -139,7 +139,7 @@
 
 
 def groups_of(heads):
-    group = 2 if heads % 2 == 0 else 1
+    group = 4 if heads % 4 == 0 else 1
     wide = group * STRIPE
     return group, [pl.ds(i * wide, wide) for i in range(heads // group)]
 
@@ -378,7 +378,9 @@
         in_specs=[smem_spec] + [vmem_spec] * (3 + len(others)),
         out_specs=[vmem_spec] * len(outs),
         scratch_shapes=scratch,
-        compiler_params=vmem_limit(13 * half_rows * STRIPE + 12 * PAIR * wide * 2),
+        compiler_params=pltpu.CompilerParams(
+            vmem_limit_bytes=13 * half_rows * STRIPE + 12 * PAIR * wide * 2,
+        ),
         name="early" if early else "late",
     )(meta, q_flat, g_flat, delta, *others)
 

time: 73 us -> 73 us (level)
  no operation moved by 1% of the time
where the time goes in v5:
time: 73 us; the launch traced here: 72.7 us
  waiting for transfers between devices  28.6 us (39%)
  starting transfers between devices  20.6 us (28%)
  Pallas kernels  16 us (22%)
  local copies, waits for them, and re-layouts  4.8 us (7%)
  between operations  1.4 us (2%)
  other arithmetic  1.3 us (2%)
    ppermute x20, waiting for transfers between devices, send(): return lax.ppermute(value, AXES, layout.hop(**where))  28.6 us
    ppermute x20, starting transfers between devices, send(): return lax.ppermute(value, AXES, layout.hop(**where))  20.6 us
    pallas_call x2, Pallas kernels, run_attend(): pl.pallas_call(functools.partial(body, stripes, pieces, heads, keep, inv_...  11.8 us
    unnamed x10, local copies, waits for them, and re-layouts  4.16 us
    pallas_call x1, Pallas kernels, run_prepare(): pl.pallas_call(functools.partial(prepare, layout, heads), out_shape=[flat...  3.31 us
  transfers between devices with their start and end apart: 20, of which 11 were waited for; matrix products, arithmetic and copies ran while one was open for 0% of the time, Pallas kernels for 6%

profile of v5, /device:TPU:0, one launch (start us, length us, event | category | flops | bytes accessed | tf_op | source)
XLA Modules:
  0.0 72.7 jit_solution(687440048952569835)
XLA Ops:
  1.4 4.0 %collective-permute-start.2 = (bf16[256,128]{1,0:T(8,128)(2,1)S(1)}, bf16[256,128]{1,0:T(8,128)(2,1)S(1)}, u32[]{:S(2)}, u32[]{:S(2)}) collective-permute-start(bf16[256,128]{1,0:T(8,128)(2,1)S(1)} %pad_maximum_fusion.1), channel_id=1, source_target_pairs={{0,20},{1,11},{2,22},{3,9},{4,16},{5,15},{6,18},{7,13},{8,28},{9,3... | collective-permute-start | bytes 196616 | tf_op jit(solution)/shard_map/ppermute | solution.py:411
  6.0 1.9 %collective-permute-done.2 = bf16[256,128]{1,0:T(8,128)(2,1)S(1)} collective-permute-done((bf16[256,128]{1,0:T(8,128)(2,1)S(1)}, bf16[256,128]{1,0:T(8,128)(2,1)S(1)}, u32[]{:S(2)}, u32[]{:S(2)}) %collective-permute-start.2) | collective-permute-done | bytes 65568 | tf_op jit(solution)/shard_map/ppermute | solution.py:411
  7.9 1.8 %collective-permute-done.1 = bf16[256,128]{1,0:T(8,128)(2,1)S(1)} collective-permute-done((bf16[256,128]{1,0:T(8,128)(2,1)S(1)}, bf16[256,128]{1,0:T(8,128)(2,1)S(1)}, u32[]{:S(2)}, u32[]{:S(2)}) %collective-permute-start.1) | collective-permute-done | bytes 65568 | tf_op jit(solution)/shard_map/ppermute | solution.py:411
  9.7 1.2 %collective-permute-done = bf16[256,128]{1,0:T(8,128)(2,1)S(1)} collective-permute-done((bf16[256,128]{1,0:T(8,128)(2,1)S(1)}, bf16[256,128]{1,0:T(8,128)(2,1)S(1)}, u32[]{:S(2)}, u32[]{:S(2)}) %collective-permute-start) | collective-permute-done | bytes 65568 | tf_op jit(solution)/shard_map/ppermute | solution.py:411
  10.9 3.8 %collective-permute-start.5 = (bf16[1024,128]{1,0:T(8,128)(2,1)S(1)}, bf16[1024,128]{1,0:T(8,128)(2,1)S(1)}, u32[]{:S(2)}, u32[]{:S(2)}) collective-permute-start(bf16[1024,128]{1,0:T(8,128)(2,1)S(1)} %pad_maximum_fusion.refs_0_), channel_id=1, source_target_pairs={{0,14},{1,21},{2,12},{3,23},{4,10},{5,17},{6,8},{7,19},{8,6},{9,29... | collective-permute-start | bytes 786440 | tf_op jit(solution)/shard_map/ppermute | solution.py:411
  15.1 1.2 %collective-permute-start.3 = (bf16[1024,128]{1,0:T(8,128)(2,1)S(1)}, bf16[1024,128]{1,0:T(8,128)(2,1)S(1)}, u32[]{:S(2)}, u32[]{:S(2)}) collective-permute-start(bf16[1024,128]{1,0:T(8,128)(2,1)S(1)} %pad_maximum_fusion.refs_0_), channel_id=1, source_target_pairs={{0,2},{1,5},{2,0},{3,7},{4,6},{5,1},{6,4},{7,3},{8,10},{9,13},{10,... | collective-permute-start | bytes 786440 | tf_op jit(solution)/shard_map/ppermute | solution.py:411
  16.3 6.6 %collective-permute-done.5.refs_3_ = bf16[1024,128]{1,0:T(8,128)(2,1)S(1)} collective-permute-done((bf16[1024,128]{1,0:T(8,128)(2,1)S(1)}, bf16[1024,128]{1,0:T(8,128)(2,1)S(1)}, u32[]{:S(2)}, u32[]{:S(2)}) %collective-permute-start.5) | collective-permute-done | bytes 262176 | tf_op jit(solution)/shard_map/ppermute | solution.py:411
  22.9 3.2 %collective-permute-done.4.refs_2_ = bf16[1024,128]{1,0:T(8,128)(2,1)S(1)} collective-permute-done((bf16[1024,128]{1,0:T(8,128)(2,1)S(1)}, bf16[1024,128]{1,0:T(8,128)(2,1)S(1)}, u32[]{:S(2)}, u32[]{:S(2)}) %collective-permute-start.4) | collective-permute-done | bytes 262176 | tf_op jit(solution)/shard_map/ppermute | solution.py:411
  27.3 0.9 %copy-done = bf16[128,1024]{1,0:T(8,128)(2,1)S(1)} copy-done((bf16[128,1024]{1,0:T(8,128)(2,1)S(1)}, bf16[128,1024]{1,0:T(8,128)(2,1)}, u32[]{:S(2)}) %copy-start) | copy-done | bytes 262168
  28.2 0.9 %copy-done.1 = bf16[128,1024]{1,0:T(8,128)(2,1)S(1)} copy-done((bf16[128,1024]{1,0:T(8,128)(2,1)S(1)}, bf16[128,1024]{1,0:T(8,128)(2,1)}, u32[]{:S(2)}) %copy-start.1) | copy-done | bytes 262168
  29.2 0.9 %copy-done.2 = bf16[128,1024]{1,0:T(8,128)(2,1)S(1)} copy-done((bf16[128,1024]{1,0:T(8,128)(2,1)S(1)}, bf16[128,1024]{1,0:T(8,128)(2,1)}, u32[]{:S(2)}) %copy-start.2) | copy-done | bytes 262168
  31.4 3.3 %prep.1 = (bf16[1024,128]{1,0:T(8,128)(2,1)S(1)}, bf16[1024,128]{1,0:T(8,128)(2,1)S(1)}, f32[1,1024]{1,0:T(1,128)S(1)}, s32[71]{0:T(128)S(1)}) custom-call(s32[2]{0:T(128)S(1)} %pad_add_fusion.here, s32[32]{0:T(128)S(1)} %copy-done.3, s32[1]{0:T(128)S(6)} %copy.11.window, bf16[128,1024]{1,0:T(8,128)(2,1)S(1)} %copy-done, s32[1,128]{1,0:T(1,128)S(1)} %bitcast.3, ...), custom_call_target="tpu_custom_call" | custom-call | tf_op jit(solution)/shard_map/prep/pallas_call | solution.py:340
  34.8 8.0 %early.1 = (bf16[8448,128]{1,0:T(8,128)(2,1)S(1)}, f32[18,256,1024]{2,1,0:T(8,128)S(1)}, f32[1,1024]{1,0:T(1,128)S(1)}, f32[1,1024]{1,0:T(1,128)S(1)}, f32[128,1...) custom-call(s32[71]{0:T(128)S(1)} %get-tuple-element.21.meta, ...), custom_call_target="tpu_custom_call" | custom-call | tf_op jit(solution)/shard_map/early/pallas_call | solution.py:375
  42.8 3.8 %late.1 = (f32[128,1024]{1,0:T(8,128)S(1)}, bf16[1024,128]{1,0:T(8,128)(2,1)S(1)}, bf16[1024,128]{1,0:T(8,128)(2,1)S(1)}, bf16[1024,128]{1,0:T(8,128)(2,1)S(1)}, bf16[1024,128]{1,0:T(8,128)(2,1)S(1)}) custom-call(s32[71]{0:T(128)S(1)} %get-tuple-element.21.meta, bf16[1024,128]{1,0:T(8,128)(2,1)S(1)} %get-tuple-element.22.q_ref, ...), custom_call_target="tpu_custom_call" | custom-call | tf_op jit(solution)/shard_map/late/pallas_call | solution.py:375
  48.3 0.9 %collective-permute-start.12 = (bf16[1024,128]{1,0:T(8,128)(2,1)S(1)}, bf16[1024,128]{1,0:T(8,128)(2,1)S(1)}, u32[]{:S(2)}, u32[]{:S(2)}) collective-permute-start(bf16[1024,128]{1,0:T(8,128)(2,1)S(1)} %add_convert_fusion.2), channel_id=1, source_target_pairs={{0,2},{1,5},{2,0},{3,7},{4,6},{5,1},{6,4},{7,3},{8,10},{9,13},{10,... | collective-permute-start | bytes 786440 | tf_op jit(solution)/shard_map/ppermute | solution.py:411
  49.2 1.8 %collective-permute-start.14 = (bf16[1024,128]{1,0:T(8,128)(2,1)S(1)}, bf16[1024,128]{1,0:T(8,128)(2,1)S(1)}, u32[]{:S(2)}, u32[]{:S(2)}) collective-permute-start(bf16[1024,128]{1,0:T(8,128)(2,1)S(1)} %add_convert_fusion.1), channel_id=1, source_target_pairs={{0,12},{1,17},{2,14},{3,19},{4,8},{5,21},{6,10},{7,23},{8,4},{9,25... | collective-permute-start | bytes 786440 | tf_op jit(solution)/shard_map/ppermute | solution.py:411
  51.1 2.9 %collective-permute-start.16 = (bf16[1024,128]{1,0:T(8,128)(2,1)S(1)}, bf16[1024,128]{1,0:T(8,128)(2,1)S(1)}, u32[]{:S(2)}, u32[]{:S(2)}) collective-permute-start(bf16[1024,128]{1,0:T(8,128)(2,1)S(1)} %add_convert_fusion), channel_id=1, source_target_pairs={{0,14},{1,21},{2,12},{3,23},{4,10},{5,17},{6,8},{7,19},{8,6},{9,29... | collective-permute-start | bytes 786440 | tf_op jit(solution)/shard_map/ppermute | solution.py:411
  53.9 0.8 %collective-permute-done.12 = bf16[1024,128]{1,0:T(8,128)(2,1)S(1)} collective-permute-done((bf16[1024,128]{1,0:T(8,128)(2,1)S(1)}, bf16[1024,128]{1,0:T(8,128)(2,1)S(1)}, u32[]{:S(2)}, u32[]{:S(2)}) %collective-permute-start.12) | collective-permute-done | bytes 262176 | tf_op jit(solution)/shard_map/ppermute | solution.py:411
  54.7 5.5 %collective-permute-done.14 = bf16[1024,128]{1,0:T(8,128)(2,1)S(1)} collective-permute-done((bf16[1024,128]{1,0:T(8,128)(2,1)S(1)}, bf16[1024,128]{1,0:T(8,128)(2,1)S(1)}, u32[]{:S(2)}, u32[]{:S(2)}) %collective-permute-start.14) | collective-permute-done | bytes 262176 | tf_op jit(solution)/shard_map/ppermute | solution.py:411
  60.3 4.1 %collective-permute-done.16 = bf16[1024,128]{1,0:T(8,128)(2,1)S(1)} collective-permute-done((bf16[1024,128]{1,0:T(8,128)(2,1)S(1)}, bf16[1024,128]{1,0:T(8,128)(2,1)S(1)}, u32[]{:S(2)}, u32[]{:S(2)}) %collective-permute-start.16) | collective-permute-done | bytes 262176 | tf_op jit(solution)/shard_map/ppermute | solution.py:411
  64.6 1.6 %collective-permute-start.17 = (bf16[256,128]{1,0:T(8,128)(2,1)S(1)}, bf16[256,128]{1,0:T(8,128)(2,1)S(1)}, u32[]{:S(2)}, u32[]{:S(2)}) collective-permute-start(bf16[256,128]{1,0:T(8,128)(2,1)S(1)} %get-tuple-element.41), channel_id=1, source_target_pairs={{0,4},{1,3},{2,6},{3,1},{4,0},{5,7},{6,2},{7,5},{8,12},{9,11},{10,... | collective-permute-start | bytes 196616 | tf_op jit(solution)/shard_map/ppermute | solution.py:411
  66.2 1.3 %collective-permute-start.19 = (bf16[256,128]{1,0:T(8,128)(2,1)S(1)}, bf16[256,128]{1,0:T(8,128)(2,1)S(1)}, u32[]{:S(2)}, u32[]{:S(2)}) collective-permute-start(bf16[256,128]{1,0:T(8,128)(2,1)S(1)} %get-tuple-element.42), channel_id=1, source_target_pairs={{0,20},{1,11},{2,22},{3,9},{4,16},{5,15},{6,18},{7,13},{8,28},{9,3... | collective-permute-start | bytes 196616 | tf_op jit(solution)/shard_map/ppermute | solution.py:411
  68.1 0.9 %turn.1 = bf16[128,1024]{1,0:T(8,128)(2,1)} custom-call(f32[128,1024]{1,0:T(8,128)S(1)} %get-tuple-element.30.turned), custom_call_target="tpu_custom_call" | custom-call | tf_op jit(solution)/shard_map/turn/pallas_call | solution.py:389
  69.0 2.3 %collective-permute-done.19 = bf16[256,128]{1,0:T(8,128)(2,1)S(1)} collective-permute-done((bf16[256,128]{1,0:T(8,128)(2,1)S(1)}, bf16[256,128]{1,0:T(8,128)(2,1)S(1)}, u32[]{:S(2)}, u32[]{:S(2)}) %collective-permute-start.19) | collective-permute-done | bytes 65568 | tf_op jit(solution)/shard_map/ppermute | solution.py:411
  (40 shorter events, 7.7 us)
Async XLA Ops:
  1.4 6.5 %collective-permute-start.2 = (bf16[256,128]{1,0:T(8,128)(2,1)S(1)}, bf16[256,128]{1,0:T(8,128)(2,1)S(1)}, u32[]{:S(2)}, u32[]{:S(2)}) collective-permute-start(bf16[256,128]{1,0:T(8,128)(2,1)S(1)} %pad_maximum_fusion.1), channel_id=1, source_target_pairs={{0,20},{1,11},{2,22},{3,9},{4,16},{5,15},{6,18},{7,13},{8,28},{9,3... | collective-permute-start | bytes 196616 | tf_op jit(solution)/shard_map/ppermute | solution.py:411
  5.4 4.3 %collective-permute-start.1 = (bf16[256,128]{1,0:T(8,128)(2,1)S(1)}, bf16[256,128]{1,0:T(8,128)(2,1)S(1)}, u32[]{:S(2)}, u32[]{:S(2)}) collective-permute-start(bf16[256,128]{1,0:T(8,128)(2,1)S(1)} %pad_maximum_fusion.1), channel_id=1, source_target_pairs={{0,16},{1,9},{2,18},{3,11},{4,20},{5,13},{6,22},{7,15},{8,24},{9,1... | collective-permute-start | bytes 196616 | tf_op jit(solution)/shard_map/ppermute | solution.py:411
  5.9 5.0 %collective-permute-start = (bf16[256,128]{1,0:T(8,128)(2,1)S(1)}, bf16[256,128]{1,0:T(8,128)(2,1)S(1)}, u32[]{:S(2)}, u32[]{:S(2)}) collective-permute-start(bf16[256,128]{1,0:T(8,128)(2,1)S(1)} %pad_maximum_fusion.1), channel_id=1, source_target_pairs={{0,4},{1,3},{2,6},{3,1},{4,0},{5,7},{6,2},{7,5},{8,12},{9,11},{10,... | collective-permute-start | bytes 196616 | tf_op jit(solution)/shard_map/ppermute | solution.py:411
  10.9 11.9 %collective-permute-start.5 = (bf16[1024,128]{1,0:T(8,128)(2,1)S(1)}, bf16[1024,128]{1,0:T(8,128)(2,1)S(1)}, u32[]{:S(2)}, u32[]{:S(2)}) collective-permute-start(bf16[1024,128]{1,0:T(8,128)(2,1)S(1)} %pad_maximum_fusion.refs_0_), channel_id=1, source_target_pairs={{0,14},{1,21},{2,12},{3,23},{4,10},{5,17},{6,8},{7,19},{8,6},{9,29... | collective-permute-start | bytes 786440 | tf_op jit(solution)/shard_map/ppermute | solution.py:411
  14.7 11.3 %collective-permute-start.4 = (bf16[1024,128]{1,0:T(8,128)(2,1)S(1)}, bf16[1024,128]{1,0:T(8,128)(2,1)S(1)}, u32[]{:S(2)}, u32[]{:S(2)}) collective-permute-start(bf16[1024,128]{1,0:T(8,128)(2,1)S(1)} %pad_maximum_fusion.refs_0_), channel_id=1, source_target_pairs={{0,12},{1,17},{2,14},{3,19},{4,8},{5,21},{6,10},{7,23},{8,4},{9,25... | collective-permute-start | bytes 786440 | tf_op jit(solution)/shard_map/ppermute | solution.py:411
  15.1 11.0 %collective-permute-start.3 = (bf16[1024,128]{1,0:T(8,128)(2,1)S(1)}, bf16[1024,128]{1,0:T(8,128)(2,1)S(1)}, u32[]{:S(2)}, u32[]{:S(2)}) collective-permute-start(bf16[1024,128]{1,0:T(8,128)(2,1)S(1)} %pad_maximum_fusion.refs_0_), channel_id=1, source_target_pairs={{0,2},{1,5},{2,0},{3,7},{4,6},{5,1},{6,4},{7,3},{8,10},{9,13},{10,... | collective-permute-start | bytes 786440 | tf_op jit(solution)/shard_map/ppermute | solution.py:411
  16.3 18.5 %collective-permute-start.6 = (bf16[1024,128]{1,0:T(8,128)(2,1)S(1)}, bf16[1024,128]{1,0:T(8,128)(2,1)S(1)}, u32[]{:S(2)}, u32[]{:S(2)}) collective-permute-start(bf16[1024,128]{1,0:T(8,128)(2,1)S(1)} %pad_maximum_fusion.refs_0_), channel_id=1, source_target_pairs={{0,1},{1,0},{2,3},{3,2},{4,5},{5,4},{6,7},{7,6},{8,9},{9,8},{10,11... | collective-permute-start | bytes 786440 | tf_op jit(solution)/shard_map/ppermute | solution.py:411
  22.9 11.9 %collective-permute-start.9 = (bf16[1024,128]{1,0:T(8,128)(2,1)S(1)}, bf16[1024,128]{1,0:T(8,128)(2,1)S(1)}, u32[]{:S(2)}, u32[]{:S(2)}) collective-permute-start(bf16[1024,128]{1,0:T(8,128)(2,1)S(1)} %collective-permute-done.5.refs_3_), channel_id=1, source_target_pairs={{0,1},{1,0},{2,3},{3,2},{4,5},{5,4},{6,7},{7,6},{8,9},{9,8},{10,11... | collective-permute-start | bytes 786440 | tf_op jit(solution)/shard_map/ppermute | solution.py:411
  26.0 8.7 %collective-permute-start.8 = (bf16[1024,128]{1,0:T(8,128)(2,1)S(1)}, bf16[1024,128]{1,0:T(8,128)(2,1)S(1)}, u32[]{:S(2)}, u32[]{:S(2)}) collective-permute-start(bf16[1024,128]{1,0:T(8,128)(2,1)S(1)} %collective-permute-done.4.refs_2_), channel_id=1, source_target_pairs={{0,1},{1,0},{2,3},{3,2},{4,5},{5,4},{6,7},{7,6},{8,9},{9,8},{10,11... | collective-permute-start | bytes 786440 | tf_op jit(solution)/shard_map/ppermute | solution.py:411
  26.0 8.8 %collective-permute-start.7 = (bf16[1024,128]{1,0:T(8,128)(2,1)S(1)}, bf16[1024,128]{1,0:T(8,128)(2,1)S(1)}, u32[]{:S(2)}, u32[]{:S(2)}) collective-permute-start(bf16[1024,128]{1,0:T(8,128)(2,1)S(1)} %collective-permute-done.3.refs_1_), channel_id=1, source_target_pairs={{0,1},{1,0},{2,3},{3,2},{4,5},{5,4},{6,7},{7,6},{8,9},{9,8},{10,11... | collective-permute-start | bytes 786440 | tf_op jit(solution)/shard_map/ppermute | solution.py:411
  27.3 1.0 %copy-start = (bf16[128,1024]{1,0:T(8,128)(2,1)S(1)}, bf16[128,1024]{1,0:T(8,128)(2,1)}, u32[]{:S(2)}) copy-start(bf16[128,1024]{1,0:T(8,128)(2,1)} %q_ref.1) | copy-start | bytes 786436
  28.2 0.9 %copy-start.1 = (bf16[128,1024]{1,0:T(8,128)(2,1)S(1)}, bf16[128,1024]{1,0:T(8,128)(2,1)}, u32[]{:S(2)}) copy-start(bf16[128,1024]{1,0:T(8,128)(2,1)} %g_ref.1) | copy-start | bytes 786436
  29.2 0.9 %copy-start.2 = (bf16[128,1024]{1,0:T(8,128)(2,1)S(1)}, bf16[128,1024]{1,0:T(8,128)(2,1)}, u32[]{:S(2)}) copy-start(bf16[128,1024]{1,0:T(8,128)(2,1)} %o_ref.1) | copy-start | bytes 786436
  30.1 0.7 copy-start.3
  46.6 1.6 %collective-permute-start.11 = (bf16[1024,128]{1,0:T(8,128)(2,1)S(1)}, bf16[1024,128]{1,0:T(8,128)(2,1)S(1)}, u32[]{:S(2)}, u32[]{:S(2)}) collective-permute-start(bf16[1024,128]{1,0:T(8,128)(2,1)S(1)} %get-tuple-element.34), channel_id=1, source_target_pairs={{0,1},{1,0},{2,3},{3,2},{4,5},{5,4},{6,7},{7,6},{8,9},{9,8},{10,11... | collective-permute-start | bytes 786440 | tf_op jit(solution)/shard_map/ppermute | solution.py:411
  46.7 2.5 %collective-permute-start.13 = (bf16[1024,128]{1,0:T(8,128)(2,1)S(1)}, bf16[1024,128]{1,0:T(8,128)(2,1)S(1)}, u32[]{:S(2)}, u32[]{:S(2)}) collective-permute-start(bf16[1024,128]{1,0:T(8,128)(2,1)S(1)} %get-tuple-element.36), channel_id=1, source_target_pairs={{0,1},{1,0},{2,3},{3,2},{4,5},{5,4},{6,7},{7,6},{8,9},{9,8},{10,11... | collective-permute-start | bytes 786440 | tf_op jit(solution)/shard_map/ppermute | solution.py:411
  47.2 6.7 %collective-permute-start.10 = (bf16[1024,128]{1,0:T(8,128)(2,1)S(1)}, bf16[1024,128]{1,0:T(8,128)(2,1)S(1)}, u32[]{:S(2)}, u32[]{:S(2)}) collective-permute-start(bf16[1024,128]{1,0:T(8,128)(2,1)S(1)} %get-tuple-element.32), channel_id=1, source_target_pairs={{0,1},{1,0},{2,3},{3,2},{4,5},{5,4},{6,7},{7,6},{8,9},{9,8},{10,11... | collective-permute-start | bytes 786440 | tf_op jit(solution)/shard_map/ppermute | solution.py:411
  47.3 3.7 %collective-permute-start.15 = (bf16[1024,128]{1,0:T(8,128)(2,1)S(1)}, bf16[1024,128]{1,0:T(8,128)(2,1)S(1)}, u32[]{:S(2)}, u32[]{:S(2)}) collective-permute-start(bf16[1024,128]{1,0:T(8,128)(2,1)S(1)} %get-tuple-element.38), channel_id=1, source_target_pairs={{0,1},{1,0},{2,3},{3,2},{4,5},{5,4},{6,7},{7,6},{8,9},{9,8},{10,11... | collective-permute-start | bytes 786440 | tf_op jit(solution)/shard_map/ppermute | solution.py:411
  48.3 6.4 %collective-permute-start.12 = (bf16[1024,128]{1,0:T(8,128)(2,1)S(1)}, bf16[1024,128]{1,0:T(8,128)(2,1)S(1)}, u32[]{:S(2)}, u32[]{:S(2)}) collective-permute-start(bf16[1024,128]{1,0:T(8,128)(2,1)S(1)} %add_convert_fusion.2), channel_id=1, source_target_pairs={{0,2},{1,5},{2,0},{3,7},{4,6},{5,1},{6,4},{7,3},{8,10},{9,13},{10,... | collective-permute-start | bytes 786440 | tf_op jit(solution)/shard_map/ppermute | solution.py:411
  49.2 11.0 %collective-permute-start.14 = (bf16[1024,128]{1,0:T(8,128)(2,1)S(1)}, bf16[1024,128]{1,0:T(8,128)(2,1)S(1)}, u32[]{:S(2)}, u32[]{:S(2)}) collective-permute-start(bf16[1024,128]{1,0:T(8,128)(2,1)S(1)} %add_convert_fusion.1), channel_id=1, source_target_pairs={{0,12},{1,17},{2,14},{3,19},{4,8},{5,21},{6,10},{7,23},{8,4},{9,25... | collective-permute-start | bytes 786440 | tf_op jit(solution)/shard_map/ppermute | solution.py:411
  51.1 13.3 %collective-permute-start.16 = (bf16[1024,128]{1,0:T(8,128)(2,1)S(1)}, bf16[1024,128]{1,0:T(8,128)(2,1)S(1)}, u32[]{:S(2)}, u32[]{:S(2)}) collective-permute-start(bf16[1024,128]{1,0:T(8,128)(2,1)S(1)} %add_convert_fusion), channel_id=1, source_target_pairs={{0,14},{1,21},{2,12},{3,23},{4,10},{5,17},{6,8},{7,19},{8,6},{9,29... | collective-permute-start | bytes 786440 | tf_op jit(solution)/shard_map/ppermute | solution.py:411
  64.6 4.5 %collective-permute-start.17 = (bf16[256,128]{1,0:T(8,128)(2,1)S(1)}, bf16[256,128]{1,0:T(8,128)(2,1)S(1)}, u32[]{:S(2)}, u32[]{:S(2)}) collective-permute-start(bf16[256,128]{1,0:T(8,128)(2,1)S(1)} %get-tuple-element.41), channel_id=1, source_target_pairs={{0,4},{1,3},{2,6},{3,1},{4,0},{5,7},{6,2},{7,5},{8,12},{9,11},{10,... | collective-permute-start | bytes 196616 | tf_op jit(solution)/shard_map/ppermute | solution.py:411
  66.2 5.2 %collective-permute-start.19 = (bf16[256,128]{1,0:T(8,128)(2,1)S(1)}, bf16[256,128]{1,0:T(8,128)(2,1)S(1)}, u32[]{:S(2)}, u32[]{:S(2)}) collective-permute-start(bf16[256,128]{1,0:T(8,128)(2,1)S(1)} %get-tuple-element.42), channel_id=1, source_target_pairs={{0,20},{1,11},{2,22},{3,9},{4,16},{5,15},{6,18},{7,13},{8,28},{9,3... | collective-permute-start | bytes 196616 | tf_op jit(solution)/shard_map/ppermute | solution.py:411
  67.5 4.6 %collective-permute-start.18 = (bf16[256,128]{1,0:T(8,128)(2,1)S(1)}, bf16[256,128]{1,0:T(8,128)(2,1)S(1)}, u32[]{:S(2)}, u32[]{:S(2)}) collective-permute-start(bf16[256,128]{1,0:T(8,128)(2,1)S(1)} %get-tuple-element.43), channel_id=1, source_target_pairs={{0,16},{1,9},{2,18},{3,11},{4,20},{5,13},{6,22},{7,15},{8,24},{9,1... | collective-permute-start | bytes 196616 | tf_op jit(solution)/shard_map/ppermute | solution.py:411
  (1 other events, 0.7 us)
